TPU v7x, 32 devices: a whole 2x2x4 slice. The times are simulated.
32 devices in a mesh: fsdp: 8 (over z, x), tp: 4 (over y, core).
Axes of the slice: x: 2, y: 2, z: 4, core: 2. Of those that a mesh axis runs over, the one named last changes fastest.
Arguments:
- images: bfloat16 [256, 196, 512], P('fsdp'), may hold values from -6 to 6
- attn_norm_gain: bfloat16 [512], P('fsdp'), may hold values from 0.25 to 1.75
- attn_norm_bias: bfloat16 [512], P('fsdp'), may hold values from -1.75 to 1.75
- qkv_weight: bfloat16 [512, 3, 512], P('fsdp', None, 'tp'), may hold values from -0.25 to 0.25
- qkv_bias: bfloat16 [3, 512], P(None, 'tp'), may hold values from -1.75 to 1.75
- position_table: bfloat16 [169, 16], P(None, 'tp'), may hold values from -6 to 6
- proj_weight: bfloat16 [512, 512], P('tp', 'fsdp'), may hold values from -1 to 1
- proj_bias: bfloat16 [512], P('fsdp'), may hold values from -3 to 3
- mlp_norm_gain: bfloat16 [512], P('fsdp'), may hold values from 0.25 to 1.75
- mlp_norm_bias: bfloat16 [512], P('fsdp'), may hold values from -1.75 to 1.75
- fc1_weight: bfloat16 [512, 2048], P('fsdp', 'tp'), may hold values from -0.25 to 0.25
- fc1_bias: bfloat16 [2048], P('tp'), may hold values from -3 to 3
- fc2_weight: bfloat16 [2048, 512], P('tp', 'fsdp'), may hold values from -0.125 to 0.125
- fc2_bias: bfloat16 [512], P('fsdp'), may hold values from -3 to 3
- image_count: int32 [8], P('fsdp'), may hold values from 1 to 32, as said below
- out_grad: bfloat16 [256, 196, 512], P('fsdp'), may hold values from -6 to 6
Outputs:
- output: bfloat16 [256, 196, 512], P('fsdp')
- images_grad: bfloat16 [256, 196, 512], P('fsdp')
- attn_norm_gain_grad: float32 [512], P('fsdp')
- attn_norm_bias_grad: float32 [512], P('fsdp')
- qkv_weight_grad: float32 [512, 3, 512], P('fsdp', None, 'tp')
- qkv_bias_grad: float32 [3, 512], P(None, 'tp')
- position_table_grad: float32 [169, 16], P(None, 'tp')
- proj_weight_grad: float32 [512, 512], P('tp', 'fsdp')
- proj_bias_grad: float32 [512], P('fsdp')
- mlp_norm_gain_grad: float32 [512], P('fsdp')
- mlp_norm_bias_grad: float32 [512], P('fsdp')
- fc1_weight_grad: float32 [512, 2048], P('fsdp', 'tp')
- fc1_bias_grad: float32 [2048], P('tp')
- fc2_weight_grad: float32 [2048, 512], P('tp', 'fsdp')
- fc2_bias_grad: float32 [512], P('fsdp')
Inputs may be any that keep to these rules, and one draw needn't show every extreme that they name: Slots 0 to image_count[i] - 1 of image block i hold images; some block is full and some holds one image.
All inputs are finite; a program needn't handle non-finite values.
Results may differ from a plain program's by a relative error of at most 0.0095.
Values may be sent and summed in bfloat16 or wider, within the bound.
A program may use at most 256 MiB of HBM per device.

v0:
```python
from functools import partial

import jax
import jax.numpy as jnp
import numpy as np
from jax import lax
from jax.sharding import PartitionSpec as P

HD = 32
WIN = 7
SHIFT = 3
SIDE = 14
MB = 2


EPSILON = 1e-05
highest = lax.Precision.HIGHEST


def window_tables():
    offsets = np.arange(WIN)
    window_rows = np.repeat(offsets, WIN)
    window_cols = np.tile(offsets, WIN)
    relative = (window_rows[:, None] - window_rows[None, :] + WIN - 1) * (2 * WIN - 1) + (
        window_cols[:, None] - window_cols[None, :] + WIN - 1
    )
    region = np.zeros((SIDE, SIDE), np.int32)
    bounds = ((0, SIDE - WIN), (SIDE - WIN, SIDE - SHIFT), (SIDE - SHIFT, SIDE))
    region_id = 0
    for row_range in bounds:
        for col_range in bounds:
            region[row_range[0] : row_range[1], col_range[0] : col_range[1]] = region_id
            region_id = region_id + 1
    across = SIDE // WIN
    region_windows = (
        region.reshape(across, WIN, across, WIN)
        .transpose(0, 2, 1, 3)
        .reshape(across * across, WIN * WIN)
    )
    shift_mask = np.where(
        region_windows[:, :, None] == region_windows[:, None, :], 0.0, -100.0
    ).astype(np.float32)
    table_hot = (
        relative.reshape(-1)[None, :] == np.arange((2 * WIN - 1) * (2 * WIN - 1))[:, None]
    ).astype(np.float32)
    return (shift_mask, table_hot)


def to_windows(blocks):
    leading = blocks.shape[0]
    trailing = blocks.shape[2:]
    across = SIDE // WIN
    shaped = blocks.reshape((leading, SIDE, SIDE) + trailing)
    shaped = jnp.roll(shaped, (-SHIFT, -SHIFT), axis=(1, 2))
    shaped = shaped.reshape((leading, across, WIN, across, WIN) + trailing)
    permute = (0, 1, 3, 2, 4) + tuple(range(5, 5 + len(trailing)))
    return shaped.transpose(permute).reshape((leading, across * across, WIN * WIN) + trailing)


def from_windows(blocks):
    leading = blocks.shape[0]
    trailing = blocks.shape[3:]
    across = SIDE // WIN
    shaped = blocks.reshape((leading, across, across, WIN, WIN) + trailing)
    permute = (0, 1, 3, 2, 4) + tuple(range(5, 5 + len(trailing)))
    shaped = shaped.transpose(permute).reshape((leading, SIDE, SIDE) + trailing)
    shaped = jnp.roll(shaped, (SHIFT, SHIFT), axis=(1, 2))
    return shaped.reshape((leading, SIDE * SIDE) + trailing)


def moments(features):
    centered = features - jnp.mean(features, axis=-1, keepdims=True)
    variance = jnp.mean(centered * centered, axis=-1, keepdims=True)
    inverse = lax.rsqrt(variance + EPSILON)
    return (centered * inverse, inverse)


def norm_backward(grad_out, standardized, inverse, gain_vector):
    scaled = grad_out * gain_vector
    grad_in = inverse * (
        scaled
        - jnp.mean(scaled, axis=-1, keepdims=True)
        - standardized * jnp.mean(scaled * standardized, axis=-1, keepdims=True)
    )
    return (grad_in, jnp.sum(grad_out * standardized, axis=(0, 1)), jnp.sum(grad_out, axis=(0, 1)))


def token_product(left_rows, right_rows):
    return lax.dot_general(
        left_rows, right_rows, (((0, 1), (0, 1)), ((), ())), preferred_element_type=jnp.float32
    )


def right_transpose(left_rows, matrix):
    return lax.dot_general(
        left_rows, matrix, (((2,), (1,)), ((), ())), preferred_element_type=jnp.float32
    )


def per_device(
    images,
    attn_norm_gain,
    attn_norm_bias,
    qkv_weight,
    qkv_bias,
    position_table,
    proj_weight,
    proj_bias,
    mlp_norm_gain,
    mlp_norm_bias,
    fc1_weight,
    fc1_bias,
    fc2_weight,
    fc2_bias,
    image_count,
    out_grad,
):
    shift_mask, table_hot = window_tables()
    shift_mask = jnp.asarray(shift_mask)
    table_hot = jnp.asarray(table_hot)
    head_size = HD
    score_scale = head_size ** (-0.5)
    window_area = WIN * WIN
    alive_mask = (jnp.arange(images.shape[0], dtype=jnp.int32) < image_count[0]).astype(jnp.float32)

    def widen(gathered):
        return tuple(gathered) + (qkv_bias, position_table, fc1_bias)

    def full_bias(table):
        head_count = table.shape[1]
        position_bias = lax.dot_general(
            table,
            table_hot.astype(jnp.bfloat16),
            (((0,), (0,)), ((), ())),
            preferred_element_type=jnp.float32,
        )
        position_bias = position_bias.reshape(head_count, window_area, window_area)
        return position_bias[None] + shift_mask[:, None]

    def window_scores(queries, key_vectors, bias_full):
        return (
            jnp.einsum(
                "bwqhd,bwkhd->bwhqk", queries, key_vectors, preferred_element_type=jnp.float32
            )
            + bias_full[None]
        )

    per_batch = images.shape[0] // MB
    outputs_list = []
    input_grads_list = []
    totals = None
    for micro_index in range(MB):
        batch_rows = images[micro_index * per_batch : (micro_index + 1) * per_batch]
        cotangent = out_grad[micro_index * per_batch : (micro_index + 1) * per_batch]
        living = alive_mask[micro_index * per_batch : (micro_index + 1) * per_batch]
        forward_weights = widen(
            (
                lax.all_gather(attn_norm_gain, "fsdp", axis=0, tiled=True),
                lax.all_gather(attn_norm_bias, "fsdp", axis=0, tiled=True),
                lax.all_gather(proj_bias, "fsdp", axis=0, tiled=True),
                lax.all_gather(mlp_norm_gain, "fsdp", axis=0, tiled=True),
                lax.all_gather(mlp_norm_bias, "fsdp", axis=0, tiled=True),
                lax.all_gather(fc2_bias, "fsdp", axis=0, tiled=True),
                lax.all_gather(qkv_weight, "fsdp", axis=0, tiled=True),
                lax.all_gather(fc1_weight, "fsdp", axis=0, tiled=True),
                lax.all_gather(proj_weight, "fsdp", axis=1, tiled=True),
                lax.all_gather(fc2_weight, "fsdp", axis=1, tiled=True),
            )
        )
        forward_head_count = forward_weights[11].shape[1]
        forward_bias_full = full_bias(forward_weights[11])
        inputs = batch_rows.astype(jnp.float32)
        forward_standard_one, forward_inverse_one = moments(inputs)
        forward_normed = (
            forward_standard_one * forward_weights[0].astype(jnp.float32)
            + forward_weights[1].astype(jnp.float32)
        ).astype(jnp.bfloat16)
        projected = jnp.einsum(
            "btc,cjd->btjd", forward_normed, forward_weights[6], preferred_element_type=jnp.float32
        ) + forward_weights[10].astype(jnp.float32)
        windowed = to_windows(projected)
        shape_heads = windowed.shape[:3] + (forward_head_count, head_size)
        forward_queries = (
            (windowed[:, :, :, 0] * score_scale).astype(jnp.bfloat16).reshape(shape_heads)
        )
        forward_key_vectors = windowed[:, :, :, 1].astype(jnp.bfloat16).reshape(shape_heads)
        forward_value_vectors = windowed[:, :, :, 2].astype(jnp.bfloat16).reshape(shape_heads)
        forward_scores = window_scores(forward_queries, forward_key_vectors, forward_bias_full)
        row_max = jnp.max(forward_scores, axis=-1, keepdims=True)
        exponent = jnp.exp(forward_scores - row_max)
        sum_exp = jnp.sum(exponent, axis=-1, keepdims=True)
        forward_probabilities = (exponent / sum_exp).astype(jnp.bfloat16)
        forward_log_total = (row_max + jnp.log(sum_exp))[..., 0]
        mixed_heads = jnp.einsum(
            "bwhqk,bwkhd->bwqhd",
            forward_probabilities,
            forward_value_vectors,
            preferred_element_type=jnp.float32,
        )
        forward_mixed_low = from_windows(
            mixed_heads.reshape(mixed_heads.shape[:3] + (forward_head_count * head_size,))
        ).astype(jnp.bfloat16)
        attended_terms = jnp.dot(
            forward_mixed_low, forward_weights[8], preferred_element_type=jnp.float32
        )
        attended_terms = lax.psum(attended_terms, "tp")
        attended = attended_terms + forward_weights[2].astype(jnp.float32)
        residual = inputs + attended
        forward_standard_two, forward_inverse_two = moments(residual)
        forward_normed_two = (
            forward_standard_two * forward_weights[3].astype(jnp.float32)
            + forward_weights[4].astype(jnp.float32)
        ).astype(jnp.bfloat16)
        forward_hidden = jnp.dot(
            forward_normed_two, forward_weights[7], preferred_element_type=jnp.float32
        ) + forward_weights[12].astype(jnp.float32)
        forward_activated = jax.nn.gelu(forward_hidden, approximate=False).astype(jnp.bfloat16)
        branch_terms = jnp.dot(
            forward_activated, forward_weights[9], preferred_element_type=jnp.float32
        )
        branch_terms = lax.psum(branch_terms.astype(jnp.bfloat16), "tp").astype(jnp.float32)
        branch = branch_terms + forward_weights[5].astype(jnp.float32)
        output = residual + branch
        forward_saved_forward = (
            forward_standard_one,
            forward_inverse_one,
            forward_normed,
            forward_queries,
            forward_key_vectors,
            forward_value_vectors,
            forward_log_total,
            forward_mixed_low,
            forward_standard_two,
            forward_inverse_two,
            forward_normed_two,
            forward_hidden,
            forward_activated,
        )
        output, saved_forward = (output, forward_saved_forward)
        outputs_list.append((output * living[:, None, None]).astype(jnp.bfloat16))
        backward_weights = widen(
            (
                lax.all_gather(attn_norm_gain, "fsdp", axis=0, tiled=True),
                lax.all_gather(attn_norm_bias, "fsdp", axis=0, tiled=True),
                lax.all_gather(proj_bias, "fsdp", axis=0, tiled=True),
                lax.all_gather(mlp_norm_gain, "fsdp", axis=0, tiled=True),
                lax.all_gather(mlp_norm_bias, "fsdp", axis=0, tiled=True),
                lax.all_gather(fc2_bias, "fsdp", axis=0, tiled=True),
                lax.all_gather(qkv_weight, "fsdp", axis=0, tiled=True),
                lax.all_gather(fc1_weight, "fsdp", axis=0, tiled=True),
                lax.all_gather(proj_weight, "fsdp", axis=1, tiled=True),
                lax.all_gather(fc2_weight, "fsdp", axis=1, tiled=True),
            )
        )
        (
            standard_one,
            inverse_one,
            normed,
            backward_queries,
            backward_key_vectors,
            value_vectors,
            log_total,
            mixed_low,
            standard_two,
            inverse_two,
            normed_two,
            hidden,
            activated,
        ) = saved_forward
        backward_head_count = backward_weights[11].shape[1]
        backward_bias_full = full_bias(backward_weights[11])
        upstream = cotangent.astype(jnp.float32) * living[:, None, None]
        upstream_low = upstream.astype(jnp.bfloat16)
        grad_fc2_bias = jnp.sum(upstream_low.astype(jnp.float32), axis=(0, 1))
        grad_fc2 = token_product(activated, upstream_low)
        grad_activated = right_transpose(upstream_low, backward_weights[9])
        unused, gelu_pull = jax.vjp(partial(jax.nn.gelu, approximate=False), hidden)
        grad_hidden_low = gelu_pull(grad_activated)[0].astype(jnp.bfloat16)
        grad_fc1_bias = jnp.sum(grad_hidden_low.astype(jnp.float32), axis=(0, 1))
        grad_fc1 = token_product(normed_two, grad_hidden_low)
        grad_normed_two = right_transpose(grad_hidden_low, backward_weights[7])
        grad_normed_two = lax.psum(grad_normed_two, "tp")
        grad_from_norm, grad_gain_two, grad_bias_two = norm_backward(
            grad_normed_two, standard_two, inverse_two, backward_weights[3].astype(jnp.float32)
        )
        grad_residual = upstream + grad_from_norm
        grad_attended_low = grad_residual.astype(jnp.bfloat16)
        grad_proj_bias = jnp.sum(grad_attended_low.astype(jnp.float32), axis=(0, 1))
        grad_proj = token_product(mixed_low, grad_attended_low)
        grad_mixed = right_transpose(grad_attended_low, backward_weights[8]).astype(jnp.bfloat16)
        grad_mixed = to_windows(grad_mixed)
        grad_mixed = grad_mixed.reshape(grad_mixed.shape[:3] + (backward_head_count, head_size))
        scores = window_scores(backward_queries, backward_key_vectors, backward_bias_full)
        probabilities = jnp.exp(scores - log_total[..., None])
        probs_low = probabilities.astype(jnp.bfloat16)
        grad_values = jnp.einsum(
            "bwhqk,bwqhd->bwkhd", probs_low, grad_mixed, preferred_element_type=jnp.float32
        )
        grad_probs = jnp.einsum(
            "bwqhd,bwkhd->bwhqk", grad_mixed, value_vectors, preferred_element_type=jnp.float32
        )
        grad_scores = probabilities * (
            grad_probs - jnp.sum(probabilities * grad_probs, axis=-1, keepdims=True)
        )
        scores_low = grad_scores.astype(jnp.bfloat16)
        grad_queries = jnp.einsum(
            "bwhqk,bwkhd->bwqhd",
            scores_low,
            backward_key_vectors,
            preferred_element_type=jnp.float32,
        )
        grad_keys = jnp.einsum(
            "bwhqk,bwqhd->bwkhd", scores_low, backward_queries, preferred_element_type=jnp.float32
        )
        score_sum = jnp.sum(scores_low.astype(jnp.float32), axis=(0, 1)).reshape(
            backward_head_count, window_area * window_area
        )
        grad_table = lax.dot_general(
            table_hot, score_sum, (((1,), (1,)), ((), ())), precision=highest
        )
        stacked = jnp.stack((grad_queries * score_scale, grad_keys, grad_values), axis=3)
        stacked = stacked.reshape(stacked.shape[:4] + (backward_head_count * head_size,))
        grad_projected = from_windows(stacked).astype(jnp.bfloat16)
        grad_qkv_bias = jnp.sum(grad_projected.astype(jnp.float32), axis=(0, 1))
        grad_qkv = token_product(normed, grad_projected)
        grad_normed = lax.dot_general(
            grad_projected,
            backward_weights[6],
            (((2, 3), (1, 2)), ((), ())),
            preferred_element_type=jnp.float32,
        )
        grad_normed = lax.psum(grad_normed, "tp")
        grad_input_norm, grad_gain_one, grad_bias_one = norm_backward(
            grad_normed, standard_one, inverse_one, backward_weights[0].astype(jnp.float32)
        )
        grad_input = (grad_residual + grad_input_norm).astype(jnp.bfloat16)
        gradients = (
            grad_gain_one,
            grad_bias_one,
            grad_proj_bias,
            grad_gain_two,
            grad_bias_two,
            grad_fc2_bias,
            grad_qkv,
            grad_fc1,
            grad_proj,
            grad_fc2,
            grad_qkv_bias,
            grad_table,
            grad_fc1_bias,
        )
        grad_input, gradients = (grad_input, gradients)
        input_grads_list.append(grad_input)
        if totals is None:
            totals = gradients
        else:
            totals = tuple((total + gradient for total, gradient in zip(totals, gradients)))
    output_all = jnp.concatenate(outputs_list, axis=0)
    input_grad_all = jnp.concatenate(input_grads_list, axis=0)
    scattered = (
        lax.psum_scatter(totals[0], "fsdp", scatter_dimension=0, tiled=True),
        lax.psum_scatter(totals[1], "fsdp", scatter_dimension=0, tiled=True),
        lax.psum_scatter(totals[2], "fsdp", scatter_dimension=0, tiled=True),
        lax.psum_scatter(totals[3], "fsdp", scatter_dimension=0, tiled=True),
        lax.psum_scatter(totals[4], "fsdp", scatter_dimension=0, tiled=True),
        lax.psum_scatter(totals[5], "fsdp", scatter_dimension=0, tiled=True),
        lax.psum_scatter(totals[6], "fsdp", scatter_dimension=0, tiled=True),
        lax.psum_scatter(totals[7], "fsdp", scatter_dimension=0, tiled=True),
        lax.psum_scatter(totals[8], "fsdp", scatter_dimension=1, tiled=True),
        lax.psum_scatter(totals[9], "fsdp", scatter_dimension=1, tiled=True),
    )
    summed = lax.psum((totals[10], totals[11], totals[12]), "fsdp")
    return (
        output_all,
        input_grad_all,
        scattered[0],
        scattered[1],
        scattered[6],
        summed[0],
        summed[1],
        scattered[8],
        scattered[2],
        scattered[3],
        scattered[4],
        scattered[7],
        summed[2],
        scattered[9],
        scattered[5],
    )


def solution(mesh):
    return jax.shard_map(
        per_device,
        mesh=mesh,
        in_specs=(
            P("fsdp", None, None),
            P("fsdp"),
            P("fsdp"),
            P("fsdp", None, "tp"),
            P(None, "tp"),
            P(None, "tp"),
            P("tp", "fsdp"),
            P("fsdp"),
            P("fsdp"),
            P("fsdp"),
            P("fsdp", "tp"),
            P("tp"),
            P("tp", "fsdp"),
            P("fsdp"),
            P("fsdp"),
            P("fsdp", None, None),
        ),
        out_specs=(
            P("fsdp", None, None),
            P("fsdp", None, None),
            P("fsdp"),
            P("fsdp"),
            P("fsdp", None, "tp"),
            P(None, "tp"),
            P(None, "tp"),
            P("tp", "fsdp"),
            P("fsdp"),
            P("fsdp"),
            P("fsdp"),
            P("fsdp", "tp"),
            P("tp"),
            P("tp", "fsdp"),
            P("fsdp"),
        ),
        check_vma=False,
    )
```

profile of v0, /device:TPU:0, one launch (start us, length us, event | category | flops | bytes accessed | tf_op | source)
XLA Modules:
  0.0 1611.5 jit_solution(5736901572529291619)
XLA Ops:
  14.3 23.9 %all-reduce.14 = (bf16[512]{0:T(512)(128)(2,1)S(1)}, bf16[512]{0:T(512)(128)(2,1)S(1)}, bf16[512]{0:T(512)(128)(2,1)S(1)}, bf16[512]{0:T(512)(128)(2,1)S(1)}, bf...) all-reduce(bf16[512]{0:T(512)(128)(2,1)S(1)} %dynamic-update-slice.1, ...), channel_id=1, replica_groups=mesh['fsdp'=8,'tp'=4] {'fsdp'}, use_global_device_ids=true, to_apply=%add.1 | all-reduce | flops 3072 | bytes 12288
  38.9 31.2 %all_gather.22 = bf16[512,3,128]{2,0,1:T(8,128)(2,1)S(1)} all-gather(bf16[64,3,128]{2,0,1:T(8,128)(2,1)} %param.21), channel_id=1, replica_groups=mesh['fsdp'=8,'tp'=4] {'fsdp'}, dimensions={0}, use_global_device_ids=true | all-gather | bytes 442368 | tf_op jit(solution)/shard_map/all_gather | solution.py:164
  105.3 13.5 copy.110
  130.9 8.5 copy.115
  145.6 30.5 %all_gather.23 = bf16[128,512]{0,1:T(8,128)(2,1)S(1)} all-gather(bf16[128,64]{0,1:T(8,128)(2,1)S(1)} %copy-done.88), channel_id=1, replica_groups=mesh['fsdp'=8,'tp'=4] {'fsdp'}, dimensions={1}, use_global_device_ids=true | all-gather | bytes 147456 | tf_op jit(solution)/shard_map/all_gather | solution.py:166
  181.7 33.6 %all_gather.27 = bf16[512,512]{1,0:T(8,128)(2,1)} all-gather(bf16[64,512]{1,0:T(8,128)(2,1)S(1)} %copy-done.84), channel_id=1, replica_groups=mesh['fsdp'=8,'tp'=4] {'fsdp'}, dimensions={0}, use_global_device_ids=true | all-gather | bytes 589824 | tf_op jit(solution)/shard_map/all_gather | solution.py:165
  215.3 33.2 %all_gather.28 = bf16[512,512]{0,1:T(8,128)(2,1)} all-gather(bf16[512,64]{0,1:T(8,128)(2,1)S(1)} %copy-done.85), channel_id=1, replica_groups=mesh['fsdp'=8,'tp'=4] {'fsdp'}, dimensions={1}, use_global_device_ids=true | all-gather | bytes 589824 | tf_op jit(solution)/shard_map/all_gather | solution.py:167
  255.3 47.0 %all-reduce.23.cloned.1.call-done = f32[16,196,512]{2,1,0:T(8,128)} async-done(((f32[16,196,512]{2,1,0:T(8,128)}), f32[16,196,512]{2,1,0:T(8,128)}) %all-reduce.23.cloned.1.call-update) | async-done | bytes 6422544 | tf_op jit(solution)/shard_map/psum | solution.py:206
  315.8 15.7 multiply_convert_fusion.5
  380.5 89.1 %all-reduce.27.cloned.1.call-done = f32[16,196,512]{2,1,0:T(8,128)} async-done(((f32[16,196,512]{2,1,0:T(8,128)}), f32[16,196,512]{2,1,0:T(8,128)}) %all-reduce.27.cloned.1.call-update) | async-done | bytes 6422544 | tf_op jit(solution)/shard_map/psum | solution.py:282
  497.6 14.0 multiply_reduce_fusion.1
  534.3 124.2 %all-reduce.25.cloned.1.call-done = f32[16,196,512]{2,1,0:T(8,128)} async-done(((f32[16,196,512]{2,1,0:T(8,128)}), f32[16,196,512]{2,1,0:T(8,128)}) %all-reduce.25.cloned.1.call-update) | async-done | bytes 6422544 | tf_op jit(solution)/shard_map/psum | solution.py:206
  671.2 15.7 multiply_convert_fusion.3
  708.2 8.5 copy.138
  723.1 101.9 %all-reduce.29.cloned.1.call-done = f32[16,196,512]{2,1,0:T(8,128)} async-done(((f32[16,196,512]{2,1,0:T(8,128)}), f32[16,196,512]{2,1,0:T(8,128)}) %all-reduce.29.cloned.1.call-update) | async-done | bytes 6422544 | tf_op jit(solution)/shard_map/psum | solution.py:282
  856.8 16.3 %convert_reduce_fusion.3 = (f32[4,49,49]{1,2,0:T(8,128)}, bf16[16,4,4,49,49]{3,4,2,1,0:T(8,128)(2,1)}, f32[16,4,4,49]{3,2,1,0:T(4,128)}, f32[16,4,4,49,49]{3,4,2,1,0:T(8,128)}) fusion(f32[16,4,4,49,49]{3,4,2,1,0:T(8,128)} %get-tuple-element.147, f32[16,4,4,49]{3,2,1,0:T(4,128)} %get-tuple-element.80, f32[16,4,4,49]{3,2,1,0:T(4,128)S(1)} %bitcast.286, ...), kind=kOutput, calls=%fused_computation.21 | convolution fusion | flops 46077052 | bytes 13062224 | tf_op jit(solution)/shard_map/bwqhd,bwkhd->bwhqk/dot_general | solution.py:299
  894.9 8.5 copy.146
  908.2 8.5 copy.148
  921.4 8.5 copy.151
  939.4 8.5 copy.133
  952.6 8.5 copy.135
  1007.2 7.7 convolution_bitcast_fusion.5
  1034.8 9.5 fusion.106
  1058.2 154.2 %all-reduce.31.cloned.1.call-done = (f32[16,196,512]{2,1,0:T(8,128)}, f32[16,196,512]{2,1,0:T(8,128)}) async-done(((f32[16,196,512]{2,1,0:T(8,128)}, f32[16,196,512]{2,1,0:T(8,128)}), (f32[16,196,512]{2,1,0:T(8,128)}, f32[16,196,512]{2,1,0:T(8,128)})) %all-reduce.31.cloned.1.call-update) | async-done | bytes 12845072 | tf_op jit(solution)/shard_map/psum | solution.py:332
  1212.4 13.2 fusion.28
  1225.6 113.9 %all-reduce.33.cloned.1.call-done = (bf16[16,196,512]{2,1,0:T(8,128)(2,1)}, bf16[16,196,512]{2,1,0:T(8,128)(2,1)}) async-done(((bf16[16,196,512]{2,1,0:T(8,128)(2,1)}, bf16[16,196,512]{2,1,0:T(8,128)(2,1)}), (bf16[16,196,512]{2,1,0:T(8,128)(2,1)}, bf16[16,196,512]{2,1,0:T(8,128)(2,1)})) %all-reduce.33.cloned.1.call-update) | async-done | bytes 6422544 | tf_op jit(solution)/shard_map/psum | solution.py:221
  1339.5 18.0 %fusion.27 = (bf16[16,196,512]{2,1,0:T(8,128)(2,1)}, bf16[16,196,512]{2,1,0:T(8,128)(2,1)}, f32[512]{0:T(512)S(1)}) fusion(f32[16,196,512]{2,1,0:T(8,128)} %get-tuple-element.92, f32[16,196]{1,0:T(8,128)S(1)} %broadcast_multiply_fusion.4, f32[16,196]{1,0:T(8,128)S(1)} %broadcast_multiply_fusion.5, f32[512]{0:T(512)S(1)} %copy-done.87, ...), kind=kLoop, calls=%fused_computation.47 | loop fusion | flops 44957184 | bytes 35432512 | tf_op jit(solution)/shard_map/convert_element_type | solution.py:336
  1357.7 14.4 fusion.18
  1380.7 38.2 %all-reduce.12 = (f32[512]{0:T(512)S(1)}, f32[512]{0:T(512)S(1)}, f32[3,128]{1,0:T(4,128)}, f32[169,4]{0,1:T(4,128)}, f32[512]{0:T(512)S(1)}, /*index=5*/f32[512...) all-reduce(f32[512]{0:T(512)S(1)} %add.341, ...), channel_id=2, replica_groups=mesh['fsdp'=8,'tp'=4] {'fsdp'}, use_global_device_ids=true, to_apply=%region_32.33.clone | all-reduce | flops 4644 | bytes 37152
  1430.0 44.1 %reduce-scatter.11.cloned.1.call-done = f32[512,64]{0,1:T(8,128)} async-done(((f32[512,512]{0,1:T(8,128)}), f32[512,64]{0,1:T(8,128)}) %reduce-scatter.11.cloned.1.call-update) | async-done | bytes 131088 | tf_op jit(solution)/shard_map/reduce_scatter | solution.py:370
  1474.0 64.2 %reduce-scatter.7.cloned.1.call-done = f32[128,64]{0,1:T(8,128)} async-done(((f32[128,512]{0,1:T(8,128)}), f32[128,64]{0,1:T(8,128)}) %reduce-scatter.7.cloned.1.call-update) | async-done | bytes 32784 | tf_op jit(solution)/shard_map/reduce_scatter | solution.py:369
  1538.2 66.1 %reduce-scatter.5.cloned.1.call-done = f32[64,3,128]{2,0,1:T(8,128)} async-done(((f32[512,3,128]{2,0,1:T(8,128)}), f32[64,3,128]{2,0,1:T(8,128)}) %reduce-scatter.5.cloned.1.call-update) | async-done | bytes 98320 | tf_op jit(solution)/shard_map/reduce_scatter | solution.py:367
  (440 shorter events, 400.8 us)
Async XLA Ops:
  7.2 89.0 %copy-start = (bf16[169,4]{0,1:T(4,128)(2,1)S(1)}, bf16[169,4]{0,1:T(4,128)(2,1)}, u32[]{:S(2)}) copy-start(bf16[169,4]{0,1:T(4,128)(2,1)} %param.23) | copy-start | bytes 4060
  7.2 295.1 %all-reduce.23.cloned.1.call-start = ((), (), s32[]{:S(2)}) async-start(), calls=%async_computation.4 | async-start | bytes 13107200 | tf_op jit(solution)/shard_map/psum | solution.py:206
  38.2 312.6 %copy-start.100 = (f32[512]{0:T(512)}, f32[512]{0:T(512)S(1)}, u32[]{:S(2)}) copy-start(f32[512]{0:T(512)S(1)} %convert_element_type.231) | copy-start | bytes 6148
  38.2 312.6 %copy-start.86 = (f32[512]{0:T(512)}, f32[512]{0:T(512)S(1)}, u32[]{:S(2)}) copy-start(f32[512]{0:T(512)S(1)} %convert_element_type.230) | copy-start | bytes 6148
  38.9 47.0 %copy-start.102 = (f32[3,128]{1,0:T(4,128)}, f32[3,128]{1,0:T(4,128)S(1)}, u32[]{:S(2)}) copy-start(f32[3,128]{1,0:T(4,128)S(1)} %convert_element_type.233) | copy-start | bytes 4612
  73.9 277.0 %copy-start.5 = (bf16[16,196,512]{2,0,1:T(8,128)(2,1)}, bf16[16,196,512]{2,0,1:T(8,128)(2,1)S(1)}, u32[]{:S(2)}) copy-start(bf16[16,196,512]{2,0,1:T(8,128)(2,1)S(1)} %get-tuple-element.128) | copy-start | bytes 9633796
  177.1 38.2 %copy-start.85 = (bf16[512,64]{0,1:T(8,128)(2,1)S(1)}, bf16[512,64]{0,1:T(8,128)(2,1)}, u32[]{:S(2)}) copy-start(bf16[512,64]{0,1:T(8,128)(2,1)} %param.30) | copy-start | bytes 196612
  180.9 288.7 %all-reduce.27.cloned.1.call-start = ((), (), s32[]{:S(2)}) async-start(), calls=%async_computation.6 | async-start | bytes 13107200 | tf_op jit(solution)/shard_map/psum | solution.py:282
  181.7 295.0 %copy-start.95 = (f32[16]{0:T(128)}, f32[16]{0:T(128)S(1)}, u32[]{:S(2)}) copy-start(f32[16]{0:T(128)S(1)} %get-tuple-element.143) | copy-start | bytes 196
  181.7 825.4 %copy-start.93 = (f32[16]{0:T(128)}, f32[16]{0:T(128)S(1)}, u32[]{:S(2)}) copy-start(f32[16]{0:T(128)S(1)} %get-tuple-element.142) | copy-start | bytes 196
  309.9 166.8 %copy-start.63 = (f32[16,196]{1,0:T(8,128)}, f32[16,196]{1,0:T(8,128)S(1)}, u32[]{:S(2)}) copy-start(f32[16,196]{1,0:T(8,128)S(1)} %broadcast_multiply_fusion.10) | copy-start | bytes 37636
  311.6 165.1 %copy-start.67 = (f32[16,196]{1,0:T(8,128)}, f32[16,196]{1,0:T(8,128)S(1)}, u32[]{:S(2)}) copy-start(f32[16,196]{1,0:T(8,128)S(1)} %add_rsqrt_fusion.2) | copy-start | bytes 37636
  345.3 313.1 %all-reduce.25.cloned.1.call-start = ((), (), s32[]{:S(2)}) async-start(), calls=%async_computation.5 | async-start | bytes 13107200 | tf_op jit(solution)/shard_map/psum | solution.py:206
  380.5 96.2 %copy-start.19 = (bf16[16,196,512]{2,0,1:T(8,128)(2,1)S(1)}, bf16[16,196,512]{2,0,1:T(8,128)(2,1)}, u32[]{:S(2)}) copy-start(bf16[16,196,512]{2,0,1:T(8,128)(2,1)} %get-tuple-element.126) | copy-start | bytes 9633796
  490.0 21.6 %slice-start = ((s8[7340032]{0:T(1024)(128)(4,1)}), s8[3145728]{0:T(1024)(128)(4,1)S(1)}, s32[]{:S(2)}) async-start(s8[7340032]{0:T(1024)(128)(4,1)} %bitcast.230), calls=%async_computation.14 | async-start | bytes 6291456
  530.4 128.0 %copy-start.6 = (bf16[16,196,512]{2,0,1:T(8,128)(2,1)S(1)}, bf16[16,196,512]{2,0,1:T(8,128)(2,1)}, u32[]{:S(2)}) copy-start(bf16[16,196,512]{2,0,1:T(8,128)(2,1)} %copy-done.5) | copy-start | bytes 9633796
  534.3 290.7 %all-reduce.29.cloned.1.call-start = ((), (), s32[]{:S(2)}) async-start(), calls=%async_computation.7 | async-start | bytes 13107200 | tf_op jit(solution)/shard_map/psum | solution.py:282
  700.8 511.6 %all-reduce.31.cloned.1.call-start = ((), (), s32[]{:S(2)}) async-start(), calls=%async_computation.12 | async-start | bytes 26214400 | tf_op jit(solution)/shard_map/psum | solution.py:332
  982.5 357.0 %all-reduce.33.cloned.1.call-start = ((), (), s32[]{:S(2)}) async-start(), calls=%async_computation.13 | async-start | bytes 13107200 | tf_op jit(solution)/shard_map/psum | solution.py:221
  992.2 437.8 %reduce-scatter.9.cloned.1.call-start = ((), (), s32[]{:S(2)}) async-start(), calls=%async_computation.10 | async-start | bytes 1179648 | tf_op jit(solution)/shard_map/reduce_scatter | solution.py:368
  1006.0 468.0 %reduce-scatter.11.cloned.1.call-start = ((), (), s32[]{:S(2)}) async-start(), calls=%async_computation.11 | async-start | bytes 1179648 | tf_op jit(solution)/shard_map/reduce_scatter | solution.py:370
  1020.7 517.5 %reduce-scatter.7.cloned.1.call-start = ((), (), s32[]{:S(2)}) async-start(), calls=%async_computation.9 | async-start | bytes 294912 | tf_op jit(solution)/shard_map/reduce_scatter | solution.py:369
  1052.1 552.1 %reduce-scatter.5.cloned.1.call-start = ((), (), s32[]{:S(2)}) async-start(), calls=%async_computation.8 | async-start | bytes 884736 | tf_op jit(solution)/shard_map/reduce_scatter | solution.py:367
  1212.4 127.1 %copy-start.77 = (f32[16,196]{1,0:T(8,128)S(1)}, f32[16,196]{1,0:T(8,128)}, u32[]{:S(2)}) copy-start(f32[16,196]{1,0:T(8,128)} %copy-done.76) | copy-start | bytes 37636
  1212.4 127.1 %copy-start.79 = (f32[16,196]{1,0:T(8,128)S(1)}, f32[16,196]{1,0:T(8,128)}, u32[]{:S(2)}) copy-start(f32[16,196]{1,0:T(8,128)} %copy-done.78) | copy-start | bytes 37636
  1212.4 127.1 %copy-start.97 = (f32[16]{0:T(128)S(1)}, f32[16]{0:T(128)}, u32[]{:S(2)}) copy-start(f32[16]{0:T(128)} %copy-done.95) | copy-start | bytes 196
  1212.4 145.2 %slice-start.4 = ((s8[6553600]{0:T(1024)(128)(4,1)}), s8[2359296]{0:T(1024)(128)(4,1)S(1)}, s32[]{:S(2)}) async-start(s8[6553600]{0:T(1024)(128)(4,1)} %bitcast.234), calls=%async_computation.18 | async-start | bytes 4718592
  1339.5 18.1 %copy-start.7 = (bf16[16,196,512]{2,0,1:T(8,128)(2,1)S(1)}, bf16[16,196,512]{2,0,1:T(8,128)(2,1)}, u32[]{:S(2)}) copy-start(bf16[16,196,512]{2,0,1:T(8,128)(2,1)} %copy-done.5) | copy-start | bytes 9633796
  1339.5 18.1 %copy-start.17 = (bf16[16,196,512]{2,0,1:T(8,128)(2,1)S(1)}, bf16[16,196,512]{2,0,1:T(8,128)(2,1)}, u32[]{:S(2)}) copy-start(bf16[16,196,512]{2,0,1:T(8,128)(2,1)} %get-tuple-element.125) | copy-start | bytes 9633796
  1339.5 18.1 %copy-start.22 = (f32[16,196,512]{2,1,0:T(8,128)S(1)}, f32[16,196,512]{2,1,0:T(8,128)}, u32[]{:S(2)}) copy-start(f32[16,196,512]{2,1,0:T(8,128)} %get-tuple-element.91) | copy-start | bytes 19267588
  1375.6 46.8 %copy-start.33 = (bf16[16,196,512]{2,1,0:T(8,128)(2,1)S(1)}, bf16[16,196,512]{2,1,0:T(8,128)(2,1)}, u32[]{:S(2)}) copy-start(bf16[16,196,512]{2,1,0:T(8,128)(2,1)} %get-tuple-element.122) | copy-start | bytes 9633796
  1422.4 181.8 %copy-start.1 = (bf16[169,4]{0,1:T(4,128)(2,1)S(1)}, bf16[169,4]{0,1:T(4,128)(2,1)}, u32[]{:S(2)}) copy-start(bf16[169,4]{0,1:T(4,128)(2,1)} %param.23) | copy-start | bytes 4060
  (92 other events, 721.0 us)
Sparse Core Ops, SparseCore 0:
  181.0 121.2 all-reduce.22
  345.5 124.0 all-reduce.26
  534.4 124.0 all-reduce.24
  700.9 124.0 all-reduce.28
  982.6 229.7 all-reduce.30
  1215.2 124.2 all-reduce.32
  1343.4 63.6 reduce-scatter.8
  1411.5 62.4 reduce-scatter.10
  1477.9 60.2 reduce-scatter.6
  1541.9 62.2 reduce-scatter.4
where the time goes:
time: 1620 us; the launch traced here: 1610 us
  waiting for transfers between devices  805 us (50%)
  local copies, waits for them, and re-layouts  215 us (13%)
  matrix products  205 us (13%)
  blocking collectives  191 us (12%)
  other arithmetic  177 us (11%)
  between operations  18.3 us (1%)
    psum x2, waiting for transfers between devices, per_device(): grad_normed_two = lax.psum(grad_normed_two, 'tp')  191 us
    psum x2, waiting for transfers between devices, per_device(): attended_terms = lax.psum(attended_terms, 'tp')  171 us
    psum x1, waiting for transfers between devices, per_device(): grad_normed = lax.psum(grad_normed, 'tp')  154 us
    psum x1, waiting for transfers between devices, per_device(): lax.psum(branch_terms.astype(jnp.bfloat16), 'tp').astype(jnp.float32)  114 us
    reduce_scatter x1, waiting for transfers between devices, per_device(): lax.psum_scatter(totals[6], 'fsdp', scatter_dimension=0, tiled=True)  66.1 us
    reduce_scatter x1, waiting for transfers between devices, per_device(): lax.psum_scatter(totals[8], 'fsdp', scatter_dimension=1, tiled=True)  64.2 us
    unnamed x2, blocking collectives  62.1 us
    dot_general x8, matrix products, token_product(): lax.dot_general(left_rows, right_rows, (((0, 1), (0, 1)), ((), ())), pref...  53.5 us
  transfers between devices with their start and end apart: 10, of which 9 were waited for; matrix products, arithmetic and copies ran while one was open for 12% of the time, Pallas kernels for 0%

commit v1 on v0

v1 whole, which is shorter than its diff:
```python
import functools
import jax
import jax.numpy as jnp
import numpy as np
from jax import lax
from jax.experimental import pallas as pl
from jax.experimental.pallas import tpu as pltpu

HD = 32
WIN = 7
SHIFT = 3
SIDE = 14
AREA = WIN * WIN
ROWS = 64
GROUP = 4
EPSILON = 1e-05
F32 = jnp.float32
BF16 = jnp.bfloat16
PADDED = -1e30


def window_constants():
    offsets = np.arange(WIN)
    rows, cols = np.repeat(offsets, WIN), np.tile(offsets, WIN)
    relative = (rows[:, None] - rows[None, :] + WIN - 1) * (2 * WIN - 1) + (
        cols[:, None] - cols[None, :] + WIN - 1
    )
    span = (2 * WIN - 1) ** 2
    hot = np.zeros((span, ROWS, ROWS), np.float32)
    hot[:, :AREA, :AREA] = (relative.T[None] == np.arange(span)[:, None, None])
    region = np.zeros((SIDE, SIDE), np.int32)
    bounds = ((0, SIDE - WIN), (SIDE - WIN, SIDE - SHIFT), (SIDE - SHIFT, SIDE))
    for a, rr in enumerate(bounds):
        for b, cc in enumerate(bounds):
            region[rr[0] : rr[1], cc[0] : cc[1]] = 3 * a + b
    across = SIDE // WIN
    cut = region.reshape(across, WIN, across, WIN).transpose(0, 2, 1, 3).reshape(across * across, AREA)
    mask = np.zeros((across * across, ROWS, ROWS), np.float32)
    mask[:, :AREA, :AREA] = np.where(cut[:, :, None] == cut[:, None, :], 0.0, -100.0)
    mask[:, AREA:, :] = PADDED
    mask = np.tile(mask, (1, 1, GROUP))
    perm = np.zeros((across * across * ROWS, SIDE * SIDE), np.float32)
    for w in range(across * across):
        for s in range(AREA):
            r = ((w // across) * WIN + s // WIN + SHIFT) % SIDE
            c = ((w % across) * WIN + s % WIN + SHIFT) % SIDE
            perm[w * ROWS + s, r * SIDE + c] = 1.0
    return hot, mask, perm


def dot(a, b, dims=((1,), (0,))):
    return lax.dot_general(a, b, (dims, ((), ())), preferred_element_type=F32)


NT = ((1,), (1,))
TN = ((0,), (0,))


def standardize(x):
    c = x - jnp.mean(x, axis=-1, keepdims=True)
    inv = lax.rsqrt(jnp.mean(c * c, axis=-1, keepdims=True) + EPSILON)
    return c * inv, inv


def head_masks(dtype):
    lane = lax.broadcasted_iota(jnp.int32, (1, GROUP * HD), 1) // HD
    return [(lane == h).astype(F32).astype(dtype) for h in range(GROUP)]


def spread(x, masks):
    return jnp.concatenate([x * m for m in masks], axis=0)


def gather_heads(y, masks):
    out = y[:ROWS] * masks[0]
    for h in range(1, GROUP):
        out = out + y[h * ROWS : (h + 1) * ROWS] * masks[h]
    return out


def attn_fwd_kernel(img_ref, w_ref, b_ref, vec_ref, tab_ref, mask_ref, perm_ref, permt_ref, qkv_ref, p_ref, mix_ref, bias_scr, o_scr):
    n_win = mask_ref.shape[0]
    n_grp = w_ref.shape[1] // (3 * GROUP * HD)
    gw = GROUP * HD

    @pl.when(pl.program_id(0) == 0)
    def _():
        for g in range(n_grp):
            full = jnp.concatenate([tab_ref[g * GROUP + h] for h in range(GROUP)], axis=1)
            for w in range(n_win):
                bias_scr[g, w] = full + mask_ref[w]

    x = img_ref[0].astype(F32)
    xhat, _ = standardize(x)
    normed = (xhat * vec_ref[0:1] + vec_ref[1:2]).astype(BF16)
    xp = dot(perm_ref[...], normed).astype(BF16)
    mb, mf = head_masks(BF16), head_masks(F32)
    for g in range(n_grp):
        c0 = g * 3 * gw
        acc = dot(xp, w_ref[:, c0 : c0 + 3 * gw]) + b_ref[0:1, c0 : c0 + 3 * gw]
        q = (acc[:, :gw] * (HD ** -0.5)).astype(BF16)
        k = acc[:, gw : 2 * gw].astype(BF16)
        v = acc[:, 2 * gw :].astype(BF16)
        qkv_ref[0, :, c0 : c0 + gw] = q
        qkv_ref[0, :, c0 + gw : c0 + 2 * gw] = k
        qkv_ref[0, :, c0 + 2 * gw : c0 + 3 * gw] = v
        for w in range(n_win):
            r = slice(w * ROWS, (w + 1) * ROWS)
            s = dot(k[r], spread(q[r], mb), NT) + bias_scr[g, w]
            e = jnp.exp(s - jnp.max(s, axis=0, keepdims=True))
            p = (e * (1.0 / jnp.sum(e, axis=0, keepdims=True))).astype(BF16)
            p_ref[0, g, w] = p
            o = gather_heads(dot(p, v[r], TN), mf)
            o_scr[r, g * gw : (g + 1) * gw] = o.astype(BF16)
    mix_ref[0] = dot(permt_ref[...], o_scr[...]).astype(BF16)


def attn_fwd(images, wqkv, bqkv, vecs, table, consts):
    mask, perm, permt = consts
    n = images.shape[0]
    t, c = images.shape[1:]
    n_win, n_grp = mask.shape[0], wqkv.shape[1] // (3 * GROUP * HD)
    rows = n_win * ROWS
    whole = lambda a: pl.BlockSpec(a.shape, lambda i: (0,) * a.ndim)
    return pl.pallas_call(
        attn_fwd_kernel,
        grid=(n,),
        in_specs=[pl.BlockSpec((1, t, c), lambda i: (i, 0, 0))] + [whole(a) for a in (wqkv, bqkv, vecs, table, mask, perm, permt)],
        out_specs=[
            pl.BlockSpec((1, rows, wqkv.shape[1]), lambda i: (i, 0, 0)),
            pl.BlockSpec((1, n_grp, n_win, ROWS, GROUP * ROWS), lambda i: (i, 0, 0, 0, 0)),
            pl.BlockSpec((1, t, c), lambda i: (i, 0, 0)),
        ],
        out_shape=[
            jax.ShapeDtypeStruct((n, rows, wqkv.shape[1]), BF16),
            jax.ShapeDtypeStruct((n, n_grp, n_win, ROWS, GROUP * ROWS), BF16),
            jax.ShapeDtypeStruct((n, t, c), BF16),
        ],
        scratch_shapes=[
            pltpu.VMEM((n_grp, n_win, ROWS, GROUP * ROWS), F32),
            pltpu.VMEM((rows, c), BF16),
        ],
        compiler_params=pltpu.CompilerParams(vmem_limit_bytes=48 << 20),
        name="attn_fwd",
    )(images, wqkv, bqkv, vecs, table, mask, perm, permt)


SQRT_HALF = float(np.sqrt(0.5))
INV_SQRT_2PI = float(1.0 / np.sqrt(2.0 * np.pi))


def mlp_kernel(live_ref, img_ref, og_ref, mix_ref, wp_ref, w1_ref, w2_ref, vec_ref, b1_ref,
               out_ref, gres_ref, gmix_ref, dwp_ref, dw1_ref, dw2_ref, dvec_ref, db1_ref,
               *, ipb, chunk):
    step = pl.program_id(0)
    n_tok, c = img_ref.shape[1:]
    rows = ipb * n_tok

    @pl.when(step == 0)
    def _():
        dwp_ref[...] = jnp.zeros_like(dwp_ref)
        dw1_ref[...] = jnp.zeros_like(dw1_ref)
        dw2_ref[...] = jnp.zeros_like(dw2_ref)
        dvec_ref[...] = jnp.zeros_like(dvec_ref)
        db1_ref[...] = jnp.zeros_like(db1_ref)

    flat = lambda ref: jnp.concatenate([ref[i] for i in range(ipb)], axis=0) if ipb > 1 else ref[0]
    live = jnp.concatenate(
        [jnp.full((n_tok, 1), 1.0, F32) * live_ref[step * ipb + i] for i in range(ipb)], axis=0
    )
    mixed = flat(mix_ref)
    up = flat(og_ref).astype(F32) * live
    up16 = up.astype(BF16)
    res = flat(img_ref).astype(F32) + (dot(mixed, wp_ref[...], NT) + vec_ref[2:3])
    xhat, inv = standardize(res)
    normed = (xhat * vec_ref[3:4] + vec_ref[4:5]).astype(BF16)
    branch = jnp.zeros((rows, c), F32)
    dn = jnp.zeros((rows, c), F32)
    for c0 in range(0, w1_ref.shape[1], chunk):
        cs = slice(c0, c0 + chunk)
        hid = dot(normed, w1_ref[:, cs]) + b1_ref[0:1, cs]
        cdf = 0.5 * (1.0 + lax.erf(hid * SQRT_HALF))
        act = (hid * cdf).astype(BF16)
        slope = cdf + hid * (jnp.exp(-0.5 * hid * hid) * INV_SQRT_2PI)
        branch = branch + dot(act, w2_ref[:, cs], NT)
        dw2_ref[:, cs] += dot(up16, act, TN)
        dh = (dot(up16, w2_ref[:, cs]) * slope).astype(BF16)
        db1_ref[0:1, cs] += jnp.sum(dh.astype(F32), axis=0, keepdims=True)
        dw1_ref[:, cs] += dot(normed, dh, TN)
        dn = dn + dot(dh, w1_ref[:, cs], NT)
    out = (live * (res + (branch + vec_ref[5:6]))).astype(BF16)
    d = dn * vec_ref[3:4]
    gres = up + inv * (d - jnp.mean(d, axis=-1, keepdims=True) - xhat * jnp.mean(d * xhat, axis=-1, keepdims=True))
    gatt = gres.astype(BF16)
    dwp_ref[...] += dot(gatt, mixed, TN)
    gmix = dot(gatt, wp_ref[...]).astype(BF16)
    for i in range(ipb):
        r = slice(i * n_tok, (i + 1) * n_tok)
        out_ref[i] = out[r]
        gres_ref[i] = gres[r]
        gmix_ref[i] = gmix[r]
    dvec_ref[2:3] += jnp.sum(gatt.astype(F32), axis=0, keepdims=True)
    dvec_ref[3:4] += jnp.sum(dn * xhat, axis=0, keepdims=True)
    dvec_ref[4:5] += jnp.sum(dn, axis=0, keepdims=True)
    dvec_ref[5:6] += jnp.sum(up, axis=0, keepdims=True)


def mlp(live, images, out_grad, mixed, wp, w1, w2, vecs, b1, ipb=2, chunk=512):
    n, t, c = images.shape
    ff = w1.shape[1]
    whole = lambda s: pl.BlockSpec(s, lambda i: (0,) * len(s))
    once = lambda s: pl.BlockSpec(s, lambda i: (0,) * len(s), pipeline_mode=pl.Buffered(1))
    blk = pl.BlockSpec((ipb, t, c), lambda i: (i, 0, 0))
    return pl.pallas_call(
        functools.partial(mlp_kernel, ipb=ipb, chunk=chunk),
        grid=(n // ipb,),
        in_specs=[pl.BlockSpec(memory_space=pltpu.SMEM), blk, blk, blk] + [once(a.shape) for a in (wp, w1, w2, vecs, b1)],
        out_specs=[blk, blk, blk] + [whole(s) for s in ((c, c), (c, ff), (c, ff), (8, c), (1, ff))],
        out_shape=[
            jax.ShapeDtypeStruct((n, t, c), BF16),
            jax.ShapeDtypeStruct((n, t, c), F32),
            jax.ShapeDtypeStruct((n, t, c), BF16),
            jax.ShapeDtypeStruct((c, c), F32),
            jax.ShapeDtypeStruct((c, ff), F32),
            jax.ShapeDtypeStruct((c, ff), F32),
            jax.ShapeDtypeStruct((8, c), F32),
            jax.ShapeDtypeStruct((1, ff), F32),
        ],
        compiler_params=pltpu.CompilerParams(vmem_limit_bytes=56 << 20),
        name="mlp",
    )(live, images, out_grad, mixed, wp, w1, w2, vecs, b1)


def attn_bwd_kernel(img_ref, gres_ref, gmix_ref, qkv_ref, p_ref, w_ref, vec_ref, perm_ref, permt_ref,
                    gin_ref, dw_ref, dvec_ref, db_ref, dtab_ref, dqkv_scr):
    n_grp, n_win = p_ref.shape[1:3]
    gw = GROUP * HD

    @pl.when(pl.program_id(0) == 0)
    def _():
        dw_ref[...] = jnp.zeros_like(dw_ref)
        dvec_ref[...] = jnp.zeros_like(dvec_ref)
        db_ref[...] = jnp.zeros_like(db_ref)
        dtab_ref[...] = jnp.zeros_like(dtab_ref)

    mb, mf = head_masks(BF16), head_masks(F32)
    x = img_ref[0].astype(F32)
    xhat, inv = standardize(x)
    normed = (xhat * vec_ref[0:1] + vec_ref[1:2]).astype(BF16)
    xp = dot(perm_ref[...], normed).astype(BF16)
    gm = dot(perm_ref[...], gmix_ref[0]).astype(BF16)
    for g in range(n_grp):
        c0 = g * 3 * gw
        tab = jnp.zeros((ROWS, GROUP * ROWS), F32)
        for w in range(n_win):
            r = slice(w * ROWS, (w + 1) * ROWS)
            q = qkv_ref[0, r, c0 : c0 + gw]
            k = qkv_ref[0, r, c0 + gw : c0 + 2 * gw]
            v = qkv_ref[0, r, c0 + 2 * gw : c0 + 3 * gw]
            do = spread(gm[r, g * gw : (g + 1) * gw], mb)
            p = p_ref[0, g, w]
            dqkv_scr[r, c0 + 2 * gw : c0 + 3 * gw] = dot(p, do).astype(BF16)
            dp = dot(v, do, NT)
            pf = p.astype(F32)
            ds = pf * (dp - jnp.sum(pf * dp, axis=0, keepdims=True))
            tab = tab + ds
            ds16 = ds.astype(BF16)
            dqkv_scr[r, c0 + gw : c0 + 2 * gw] = dot(ds16, spread(q, mb)).astype(BF16)
            dq = gather_heads(dot(ds16, k, TN), mf) * (HD ** -0.5)
            dqkv_scr[r, c0 : c0 + gw] = dq.astype(BF16)
        dtab_ref[g] += tab
    dqkv = dqkv_scr[...]
    db_ref[0:1] += jnp.sum(dqkv.astype(F32), axis=0, keepdims=True)
    dw_ref[...] += dot(xp, dqkv, TN)
    dn = dot(dqkv, w_ref[...], NT)
    hi = dn.astype(BF16)
    lo = (dn - hi.astype(F32)).astype(BF16)
    dn = dot(permt_ref[...], hi) + dot(permt_ref[...], lo)
    d = dn * vec_ref[0:1]
    gin = inv * (d - jnp.mean(d, axis=-1, keepdims=True) - xhat * jnp.mean(d * xhat, axis=-1, keepdims=True))
    gin_ref[0] = (gres_ref[0] + gin).astype(BF16)
    dvec_ref[0:1] += jnp.sum(dn * xhat, axis=0, keepdims=True)
    dvec_ref[1:2] += jnp.sum(dn, axis=0, keepdims=True)


def attn_bwd(images, gres, gmix, qkv, p, wqkv, vecs, consts):
    _, perm, permt = consts
    n, t, c = images.shape
    rows, cols = qkv.shape[1:]
    n_grp, n_win = p.shape[1:3]
    whole = lambda s: pl.BlockSpec(s, lambda i: (0,) * len(s))
    blk = pl.BlockSpec((1, t, c), lambda i: (i, 0, 0))
    return pl.pallas_call(
        attn_bwd_kernel,
        grid=(n,),
        in_specs=[blk, blk, blk, pl.BlockSpec((1, rows, cols), lambda i: (i, 0, 0)),
                  pl.BlockSpec((1,) + p.shape[1:], lambda i: (i, 0, 0, 0, 0))] + [whole(a.shape) for a in (wqkv, vecs, perm, permt)],
        out_specs=[blk] + [whole(s) for s in ((c, cols), (8, c), (1, cols), (n_grp, ROWS, GROUP * ROWS))],
        out_shape=[
            jax.ShapeDtypeStruct((n, t, c), BF16),
            jax.ShapeDtypeStruct((c, cols), F32),
            jax.ShapeDtypeStruct((8, c), F32),
            jax.ShapeDtypeStruct((1, cols), F32),
            jax.ShapeDtypeStruct((n_grp, ROWS, GROUP * ROWS), F32),
        ],
        scratch_shapes=[pltpu.VMEM((rows, cols), BF16)],
        compiler_params=pltpu.CompilerParams(vmem_limit_bytes=48 << 20),
        name="attn_bwd",
    )(images, gres, gmix, qkv, p, wqkv, vecs, perm, permt)


def per_device(
    images,
    attn_norm_gain,
    attn_norm_bias,
    qkv_weight,
    qkv_bias,
    position_table,
    proj_weight,
    proj_bias,
    mlp_norm_gain,
    mlp_norm_bias,
    fc1_weight,
    fc1_bias,
    fc2_weight,
    fc2_bias,
    image_count,
    out_grad,
    *,
    fsdp,
    tp,
):
    both = ("fsdp", "tp")
    hot, mask, perm = window_constants()
    mask = jnp.asarray(mask)
    hot = jnp.asarray(hot)
    perm16 = jnp.asarray(perm, BF16)
    consts = (mask, perm16, jnp.asarray(perm.T, BF16))
    gw = GROUP * HD
    cut = qkv_weight.shape[0]
    width = attn_norm_gain.shape[0] * fsdp
    ff = fc1_bias.shape[0] * tp
    ff_cut = ff // tp
    n_slots = images.shape[0]
    mine = n_slots // tp
    first = lax.axis_index("tp") * mine
    img = lax.dynamic_slice_in_dim(images, first, mine, 0)
    cot = lax.dynamic_slice_in_dim(out_grad, first, mine, 0)
    live = (first + jnp.arange(mine, dtype=jnp.int32) < image_count[0]).astype(F32)

    pack = jnp.concatenate(
        [qkv_weight.reshape(cut, 3 * gw), proj_weight.T, fc1_weight, fc2_weight.T], axis=1
    )
    full = lax.all_gather(pack, both, axis=0, tiled=False).reshape(fsdp, tp, cut, pack.shape[1])
    full = full.transpose(0, 2, 1, 3)
    piece = lambda a, b: full[..., a:b].reshape(width, tp * (b - a))
    w_qkv = piece(0, 3 * gw)
    w_proj = piece(3 * gw, 4 * gw)
    w_one = piece(4 * gw, 4 * gw + ff_cut)
    w_two = piece(4 * gw + ff_cut, 4 * gw + 2 * ff_cut)
    zero = jnp.zeros_like(attn_norm_gain)
    vecs = jnp.stack(
        [attn_norm_gain, attn_norm_bias, proj_bias, mlp_norm_gain, mlp_norm_bias, fc2_bias, zero, zero]
    )
    vecs = lax.all_gather(vecs, "fsdp", axis=1, tiled=True).astype(F32)
    tail = jnp.concatenate([qkv_bias.reshape(-1), fc1_bias, position_table.reshape(-1)])
    tail = lax.all_gather(tail, "tp", axis=0, tiled=False)
    n_qkv = qkv_bias.size
    b_qkv = tail[:, :n_qkv].reshape(1, tp * n_qkv).astype(F32)
    b_one = tail[:, n_qkv : n_qkv + ff_cut].reshape(1, ff).astype(F32)
    table = tail[:, n_qkv + ff_cut :].reshape((tp,) + position_table.shape)
    table = table.transpose(0, 2, 1).reshape(-1, position_table.shape[0])
    table = jnp.dot(table, hot.astype(BF16).reshape(hot.shape[0], -1), preferred_element_type=F32)
    table = table.reshape(-1, ROWS, ROWS)

    qkv, probs, mixed = attn_fwd(img, w_qkv, b_qkv, vecs, table, consts)
    out, gres, gmix, d_proj, d_one, d_two, dv_two, db_one = mlp(
        live, img, cot, mixed, w_proj, w_one, w_two, vecs, b_one
    )
    gin, d_qkv, dv_one, db_qkv, d_tab = attn_bwd(img, gres, gmix, qkv, probs, w_qkv, vecs, consts)

    output = lax.all_gather(out, "tp", axis=0, tiled=True)
    images_grad = lax.all_gather(gin, "tp", axis=0, tiled=True)
    split = lambda a: a.reshape(fsdp, cut, tp, a.shape[1] // tp)
    grads = jnp.concatenate([split(a) for a in (d_qkv, d_proj, d_one, d_two)], axis=3)
    grads = grads.transpose(0, 2, 1, 3).reshape(fsdp * tp * cut, pack.shape[1])
    grads = lax.psum_scatter(grads, both, scatter_dimension=0, tiled=True)
    d_tab = jnp.einsum(
        "gjhi,rji->rgh",
        d_tab.reshape(-1, ROWS, GROUP, ROWS),
        hot,
        precision=lax.Precision.HIGHEST,
    ).reshape(hot.shape[0], -1)
    dvec = jnp.concatenate([dv_one[:2], dv_two[2:6]])
    small = lax.psum(
        jnp.concatenate([dvec.reshape(-1), db_qkv[0], db_one[0], d_tab.T.reshape(-1)]), both
    )
    dvec = small[: 6 * width].reshape(6, width)
    dvec = lax.dynamic_slice_in_dim(dvec, lax.axis_index("fsdp") * cut, cut, 1)
    at = 6 * width
    t = lax.axis_index("tp")
    dqkv_bias = lax.dynamic_slice_in_dim(small, at + t * n_qkv, n_qkv, 0).reshape(qkv_bias.shape)
    at = at + tp * n_qkv
    dfc1_bias = lax.dynamic_slice_in_dim(small, at + t * ff_cut, ff_cut, 0)
    at = at + ff
    size = position_table.size
    dtable = lax.dynamic_slice_in_dim(small, at + t * size, size, 0)
    dtable = dtable.reshape(position_table.shape[::-1]).T
    return (
        output,
        images_grad,
        dvec[0],
        dvec[1],
        grads[:, : 3 * gw].reshape(qkv_weight.shape),
        dqkv_bias,
        dtable,
        grads[:, 3 * gw : 4 * gw].T,
        dvec[2],
        dvec[3],
        dvec[4],
        grads[:, 4 * gw : 4 * gw + ff_cut],
        dfc1_bias,
        grads[:, 4 * gw + ff_cut :].T,
        dvec[5],
    )


def solution(mesh):
    P = jax.sharding.PartitionSpec
    return jax.shard_map(
        functools.partial(per_device, fsdp=mesh.shape["fsdp"], tp=mesh.shape["tp"]),
        mesh=mesh,
        in_specs=(
            P("fsdp", None, None),
            P("fsdp"),
            P("fsdp"),
            P("fsdp", None, "tp"),
            P(None, "tp"),
            P(None, "tp"),
            P("tp", "fsdp"),
            P("fsdp"),
            P("fsdp"),
            P("fsdp"),
            P("fsdp", "tp"),
            P("tp"),
            P("tp", "fsdp"),
            P("fsdp"),
            P("fsdp"),
            P("fsdp", None, None),
        ),
        out_specs=(
            P("fsdp", None, None),
            P("fsdp", None, None),
            P("fsdp"),
            P("fsdp"),
            P("fsdp", None, "tp"),
            P(None, "tp"),
            P(None, "tp"),
            P("tp", "fsdp"),
            P("fsdp"),
            P("fsdp"),
            P("fsdp"),
            P("fsdp", "tp"),
            P("tp"),
            P("tp", "fsdp"),
            P("fsdp"),
        ),
        check_vma=False,
    )
```

time: 1620 us -> 498 us (0.31)
  waiting for transfers between devices: 805 us -> 185 us
  matrix products: 205 us -> 6.69 us
  other arithmetic: 177 us -> 12.4 us
  local copies, waits for them, and re-layouts: 215 us -> 86.4 us
  blocking collectives: 191 us -> 79.6 us
  Pallas kernels: 0 us -> 108 us
    psum x6 -> x0, waiting for transfers between devices: 630 us -> none  [the longest x2 191 us: per_device(): grad_normed_two = lax.psum(grad_normed_two, 'tp')]
    dot_general x39 -> x2, matrix products: 205 us -> 6.69 us  [the longest x1 4.19 us: per_device(): jnp.einsum('gjhi,rji->rgh', d_tab.reshape(-1, ROWS, GROUP, ROWS), hot, pr...]
    pallas_call x0 -> x3, Pallas kernels: none -> 108 us  [the longest x1 47.5 us: attn_bwd(): pl.pallas_call(attn_bwd_kernel, grid=(n,), in_specs=[blk, blk, blk, pl.Bl...]
    all_gather x4 -> x1, blocking collectives: 128 us -> 26.6 us  [per_device(): vecs = lax.all_gather(vecs, 'fsdp', axis=1, tiled=True).astype(F32)]
    reduce_sum x17 -> x0, other arithmetic: 88.3 us -> none  [the longest x3 27.5 us: norm_backward(): jnp.sum(grad_out * standardized, axis=(0, 1))]
    convert_element_type x15 -> x1, other arithmetic: 68.9 us -> 0.51 us  [per_device(): (first + jnp.arange(mine, dtype=jnp.int32) < image_count[0]).astype(F32)]
    another operation x12 -> x2, local copies, waits for them, and re-layouts: 58.5 us -> 0.04 us  [per_device(): jnp.stack([attn_norm_gain, attn_norm_bias, proj_bias, mlp_norm_gain, mlp_...]
    unnamed x2 -> x1, blocking collectives: 62.1 us -> 13.1 us
  transfers between devices with their start and end apart: 10 -> 4, of which waited for: 9 -> 3; matrix products, arithmetic and copies ran while one was open for 12% -> 13% of each run, Pallas kernels for 0% -> 0%
where the time goes in v1:
time: 498 us; the launch traced here: 494 us
  waiting for transfers between devices  185 us (37%)
  Pallas kernels  108 us (22%)
  local copies, waits for them, and re-layouts  86.4 us (17%)
  blocking collectives  79.6 us (16%)
  between operations  16 us (3%)
  other arithmetic  12.4 us (2%)
  matrix products  6.69 us (1%)
    reduce_scatter x1, waiting for transfers between devices, per_device(): grads = lax.psum_scatter(grads, both, scatter_dimension=0, tiled=True)  161 us
    pallas_call x1, Pallas kernels, attn_bwd(): pl.pallas_call(attn_bwd_kernel, grid=(n,), in_specs=[blk, blk, blk, pl.Bl...  47.5 us
    psum x1, blocking collectives, per_device(): lax.psum(jnp.concatenate([dvec.reshape(-1), db_qkv[0], db_one[0], d_tab.T...  39.9 us
    pallas_call x1, Pallas kernels, mlp(): pl.pallas_call(functools.partial(mlp_kernel, ipb=ipb, chunk=chunk), grid=...  39.7 us
    all_gather x1, blocking collectives, per_device(): vecs = lax.all_gather(vecs, 'fsdp', axis=1, tiled=True).astype(F32)  26.6 us
    unnamed x65, local copies, waits for them, and re-layouts  24.7 us
    pallas_call x1, Pallas kernels, attn_fwd(): pl.pallas_call(attn_fwd_kernel, grid=(n,), in_specs=[pl.BlockSpec((1, t,...  20.4 us
    all_gather x1, waiting for transfers between devices, per_device(): lax.all_gather(pack, both, axis=0, tiled=False)  20 us
  transfers between devices with their start and end apart: 4, of which 3 were waited for; matrix products, arithmetic and copies ran while one was open for 13% of the time, Pallas kernels for 0%

profile of v1, /device:TPU:0, one launch (start us, length us, event | category | flops | bytes accessed | tf_op | source)
XLA Modules:
  0.0 494.1 jit_solution(16449594006914121462)
XLA Ops:
  8.0 1.6 pad_maximum_fusion
  9.7 3.3 constant_dynamic-slice_fusion.1
  15.6 13.1 %all-reduce = bf16[6288]{0:T(1024)(128)(2,1)S(1)} all-reduce(bf16[6288]{0:T(1024)(128)(2,1)S(1)} %dynamic-update-slice), channel_id=3, replica_groups=mesh['fsdp'=8,'tp'=4] {'tp'}, use_global_device_ids=true, to_apply=%add | all-reduce | flops 6288 | bytes 25152
  29.2 2.5 fusion.1
  32.0 26.6 %all-gather.2 = bf16[8,64,8]{1,2,0:T(8,128)(2,1)S(1)} all-gather(bf16[1,64,8]{1,2,0:T(8,128)(2,1)S(1)} %bitcast.115), channel_id=1, replica_groups=mesh['fsdp'=8,'tp'=4] {'fsdp'}, dimensions={0}, use_global_device_ids=true | all-gather | bytes 9216 | tf_op jit(solution)/shard_map/all_gather | solution.py:365
  58.7 3.4 copy.73.og_ref
  63.9 20.0 %all-gather.11.cloned.1.call-done = bf16[2048,1536]{1,0:T(8,128)(2,1)} async-done(((bf16[64,1536]{1,0:T(8,128)(2,1)}), bf16[2048,1536]{1,0:T(8,128)(2,1)}) %all-gather.11.cloned.1.call-update) | async-done | bytes 6291472 | tf_op jit(solution)/shard_map/all_gather | solution.py:354
  83.9 10.3 %copy.86 = bf16[8,4,64,1536]{3,1,2,0:T(4,128)(2,1)} copy(bf16[8,4,64,1536]{3,2,1,0:T(8,128)(2,1)} %bitcast.105) | data formatting | bytes 12582912 | tf_op jit(solution)/shard_map/reshape | solution.py:354
  94.3 1.9 slice.80
  96.2 3.0 fusion
  100.8 2.0 copy.79
  102.8 1.9 copy.80
  105.7 20.4 %attn_fwd.1 = (bf16[8,256,1536]{2,1,0:T(8,128)(2,1)}, bf16[8,4,4,64,256]{4,3,2,1,0:T(8,128)(2,1)}, bf16[8,196,512]{2,1,0:T(8,128)(2,1)S(1)}) custom-call(bf16[8,196,512]{2,1,0:T(8,128)(2,1)S(1)} %copy.72.img_ref, bf16[512,1536]{1,0:T(8,128)(2,1)S(1)} %bitcast.89, f32[1,1536]{1,0:T(1,128)S(1)} %bitcast.94, f32[8,512]{1,0:T(8,128)S(1)} %bitcast.91, ...), custom_call_target="tpu_custom_call" | custom-call | tf_op jit(solution)/shard_map/attn_fwd/pallas_call | solution.py:125
  127.3 39.7 %mlp.1 = (bf16[8,196,512]{2,1,0:T(8,128)(2,1)}, f32[8,196,512]{2,1,0:T(8,128)}, bf16[8,196,512]{2,1,0:T(8,128)(2,1)}, f32[512,512]{1,0:T(8,128)}, f32[512,2048]{...) custom-call(f32[8]{0:T(128)} %compare_convert_fusion.live_ref, ...), custom_call_target="tpu_custom_call" | custom-call | tf_op jit(solution)/shard_map/mlp/pallas_call | solution.py:214
  167.0 47.5 %attn_bwd.1 = (bf16[8,196,512]{2,1,0:T(8,128)(2,1)S(1)}, f32[512,1536]{1,0:T(8,128)}, f32[8,512]{1,0:T(8,128)S(1)}, f32[1,1536]{1,0:T(1,128)S(1)}, f32[4,64,256]{2,1,0:T(8,128)S(1)}) custom-call(bf16[8,196,512]{2,1,0:T(8,128)(2,1)S(1)} %copy-done.3, f32[8,196,512]{2,1,0:T(8,128)} %get-tuple-element.33.gres_ref, ...), custom_call_target="tpu_custom_call" | custom-call | tf_op jit(solution)/shard_map/attn_bwd/pallas_call | solution.py:293
  214.5 1.7 copy.67
  216.5 1.7 copy.66
  218.2 3.3 reshape.150
  221.5 6.5 %reshape.152 = f32[8,64,4,512]{3,2,1,0:T(4,128)} reshape(f32[512,2048]{1,0:T(8,128)} %get-tuple-element.45) | data formatting | bytes 8388608 | tf_op jit(solution)/shard_map/reshape | solution.py:384
  228.0 6.1 %reshape.153 = f32[8,64,4,512]{3,2,1,0:T(4,128)} reshape(f32[512,2048]{1,0:T(8,128)} %get-tuple-element.46) | data formatting | bytes 8388608 | tf_op jit(solution)/shard_map/reshape | solution.py:384
  234.1 2.5 reshape.151
  236.6 10.3 %maximum_bitcast_fusion = f32[8,4,64,1536]{3,1,2,0:T(4,128)} fusion(f32[8,64,4,512]{3,2,1,0:T(4,128)} %reshape.153, f32[8,64,4,512]{3,2,1,0:T(4,128)} %reshape.152, f32[8,64,4,128]{3,2,1,0:T(4,128)} %reshape.151, f32[8,64,4,384]{3,2,1,0:T(4,128)S(1)} %reshape.150), kind=kLoop, calls=%fused_computation | loop fusion | flops 9437184 | bytes 25165824 | tf_op jit(solution)/shard_map/transpose | solution.py:386
  246.9 12.9 %copy.69 = f32[8,4,64,1536]{3,2,1,0:T(8,128)} copy(f32[8,4,64,1536]{3,1,2,0:T(4,128)} %maximum_bitcast_fusion) | data formatting | bytes 25165824 | tf_op jit(solution)/shard_map/transpose | solution.py:386
  261.1 4.2 convolution_bitcast_fusion
  265.4 39.9 %psum.7 = f32[9360]{0:T(1024)S(1)} all-reduce(f32[9360]{0:T(1024)S(1)} %pad_maximum_fusion.1), channel_id=1, replica_groups=mesh['fsdp'=8,'tp'=4] {'fsdp','tp'}, use_global_device_ids=true, to_apply=%region_0.0 | all-reduce | flops 9360 | bytes 74880 | tf_op jit(solution)/shard_map/psum | solution.py:395
  308.1 3.5 all-gather.7.cloned.1.call-done
  311.6 161.3 %reduce-scatter.2.cloned.1.call-done = f32[64,1536]{1,0:T(8,128)} async-done(((f32[2048,1536]{1,0:T(8,128)}), f32[64,1536]{1,0:T(8,128)}) %reduce-scatter.2.cloned.1.call-update) | async-done | bytes 393232 | tf_op jit(solution)/shard_map/reduce_scatter | solution.py:387
  472.9 1.7 slice_bitcast_fusion
  474.5 1.5 copy_bitcast_fusion.2
  476.1 1.4 slice_bitcast_fusion.2
  477.5 6.9 %copy.92 = bf16[32,196,512]{2,0,1:T(8,128)(2,1)} copy(bf16[32,196,512]{2,0,1:T(8,128)(2,1)} %all-gather.7.cloned.1.call-done) | data formatting | bytes 12845056
  484.3 2.7 copy.93
  (104 shorter events, 12.7 us)
Async XLA Ops:
  7.2 0.8 copy-start
  7.2 76.7 %all-gather.11.cloned.1.call-start = ((), (), s32[]{:S(2)}) async-start(), calls=%async_computation.4 | async-start | bytes 6488064 | tf_op jit(solution)/shard_map/all_gather | solution.py:354
  9.6 298.5 %all-gather.9.cloned.1.call-start = ((), (), s32[]{:S(2)}) async-start(), calls=%async_computation.2 | async-start | bytes 8028160 | tf_op jit(solution)/shard_map/all_gather | solution.py:383
  9.7 3.9 copy-start.13
  9.7 4.2 copy-start.22
  9.7 5.6 %copy-start.14 = (bf16[512]{0:T(512)(128)(2,1)S(1)}, bf16[512]{0:T(512)(128)(2,1)}, u32[]{:S(2)}) copy-start(bf16[512]{0:T(512)(128)(2,1)} %param.31) | copy-start | bytes 3076
  9.7 5.6 %copy-start.15 = (bf16[3,128]{1,0:T(4,128)(2,1)S(1)}, bf16[3,128]{1,0:T(4,128)(2,1)}, u32[]{:S(2)}) copy-start(bf16[3,128]{1,0:T(4,128)(2,1)} %param.24) | copy-start | bytes 2308
  13.0 18.9 %copy-start.16 = (bf16[64]{0:T(256)(128)(2,1)S(1)}, bf16[64]{0:T(256)(128)(2,1)}, u32[]{:S(2)}) copy-start(bf16[64]{0:T(256)(128)(2,1)} %param.21) | copy-start | bytes 388
  13.0 19.0 %copy-start.17 = (bf16[64]{0:T(256)(128)(2,1)S(1)}, bf16[64]{0:T(256)(128)(2,1)}, u32[]{:S(2)}) copy-start(bf16[64]{0:T(256)(128)(2,1)} %param.22) | copy-start | bytes 388
  13.0 19.0 %copy-start.18 = (bf16[64]{0:T(256)(128)(2,1)S(1)}, bf16[64]{0:T(256)(128)(2,1)}, u32[]{:S(2)}) copy-start(bf16[64]{0:T(256)(128)(2,1)} %param.27) | copy-start | bytes 388
  13.0 19.0 %copy-start.19 = (bf16[64]{0:T(256)(128)(2,1)S(1)}, bf16[64]{0:T(256)(128)(2,1)}, u32[]{:S(2)}) copy-start(bf16[64]{0:T(256)(128)(2,1)} %param.28) | copy-start | bytes 388
  13.0 19.0 %copy-start.20 = (bf16[64]{0:T(256)(128)(2,1)S(1)}, bf16[64]{0:T(256)(128)(2,1)}, u32[]{:S(2)}) copy-start(bf16[64]{0:T(256)(128)(2,1)} %param.29) | copy-start | bytes 388
  13.0 19.0 %copy-start.21 = (bf16[64]{0:T(256)(128)(2,1)S(1)}, bf16[64]{0:T(256)(128)(2,1)}, u32[]{:S(2)}) copy-start(bf16[64]{0:T(256)(128)(2,1)} %param.33) | copy-start | bytes 388
  13.5 92.2 %copy-start.2 = (bf16[8,196,512]{2,1,0:T(8,128)(2,1)}, bf16[8,196,512]{2,1,0:T(8,128)(2,1)S(1)}, u32[]{:S(2)}) copy-start(bf16[8,196,512]{2,1,0:T(8,128)(2,1)S(1)} %copy.72.img_ref) | copy-start | bytes 4816900
  58.7 47.0 %copy-start.8 = (f32[512,8]{0,1:T(8,128)}, f32[512,8]{0,1:T(8,128)S(1)}, u32[]{:S(2)}) copy-start(f32[512,8]{0,1:T(8,128)S(1)} %reshape.170) | copy-start | bytes 49156
  100.7 5.0 %copy-start.5 = (bf16[256,196]{1,0:T(8,128)(2,1)S(1)}, bf16[256,196]{1,0:T(8,128)(2,1)}, u32[]{:S(2)}) copy-start(bf16[256,196]{1,0:T(8,128)(2,1)} %constant.48.clone.perm_ref) | copy-start | bytes 301060
  100.8 4.9 copy-start.6
  100.8 4.9 copy-start.7
  126.1 1.2 copy-start.4
  127.3 39.7 %copy-start.3 = (bf16[8,196,512]{2,1,0:T(8,128)(2,1)S(1)}, bf16[8,196,512]{2,1,0:T(8,128)(2,1)}, u32[]{:S(2)}) copy-start(bf16[8,196,512]{2,1,0:T(8,128)(2,1)} %copy-done.2) | copy-start | bytes 4816900
  127.3 39.7 %copy-start.9 = (f32[512,8]{0,1:T(8,128)S(1)}, f32[512,8]{0,1:T(8,128)}, u32[]{:S(2)}) copy-start(f32[512,8]{0,1:T(8,128)} %copy-done.8) | copy-start | bytes 49156
  214.5 2.0 copy-start.10
  216.2 95.4 %all-gather.7.cloned.1.call-start = ((), (), s32[]{:S(2)}) async-start(), calls=%async_computation.1 | async-start | bytes 8028160 | tf_op jit(solution)/shard_map/all_gather | solution.py:382
  218.2 254.7 %reduce-scatter.2.cloned.1.call-start = ((), (), s32[]{:S(2)}) async-start(), calls=%async_computation.3 | async-start | bytes 12976128 | tf_op jit(solution)/shard_map/reduce_scatter | solution.py:387
  259.8 0.7 copy-start.12
  259.9 5.6 %copy-start.11 = (f32[1,2048]{1,0:T(1,128)S(1)}, f32[1,2048]{1,0:T(1,128)}, u32[]{:S(2)}) copy-start(f32[1,2048]{1,0:T(1,128)} %get-tuple-element.41) | copy-start | bytes 24580
  477.5 6.9 %slice-start = ((s8[6422528]{0:T(1024)(128)(4,1)}), s8[4194304]{0:T(1024)(128)(4,1)S(1)}, s32[]{:S(2)}) async-start(s8[6422528]{0:T(1024)(128)(4,1)} %bitcast.103), calls=%async_computation.5 | async-start | bytes 8388608
  477.5 6.9 %slice-start.1 = ((s8[6422528]{0:T(1024)(128)(4,1)}), s8[2228224]{0:T(1024)(128)(4,1)S(1)}, s32[]{:S(2)}) async-start(s8[6422528]{0:T(1024)(128)(4,1)} %bitcast.103), calls=%async_computation.6 | async-start | bytes 4456448
  477.5 9.6 %copy-start.1 = (bf16[64,3,128]{2,0,1:T(8,128)(2,1)S(1)}, bf16[64,3,128]{2,0,1:T(8,128)(2,1)}, u32[]{:S(2)}) copy-start(bf16[64,3,128]{2,0,1:T(8,128)(2,1)} %param.23) | copy-start | bytes 147460
Sparse Core Ops, SparseCore 0:
  11.5 72.3 all-gather.10
  216.3 45.5 all-gather.8
  263.5 48.0 all-gather.6
  317.5 155.3 reduce-scatter.1

commit v2 on v1

v2 whole, which is shorter than its diff:
```python
import functools
import jax
import jax.numpy as jnp
import numpy as np
from jax import lax
from jax.experimental import pallas as pl
from jax.experimental.pallas import tpu as pltpu

HD = 32
WIN = 7
SHIFT = 3
SIDE = 14
AREA = WIN * WIN
ROWS = 64
GROUP = 4
EPSILON = 1e-05
F32 = jnp.float32
BF16 = jnp.bfloat16
PADDED = -1e30
MESH = pl.DeviceIdType.MESH


def window_constants():
    offsets = np.arange(WIN)
    rows, cols = np.repeat(offsets, WIN), np.tile(offsets, WIN)
    relative = (rows[:, None] - rows[None, :] + WIN - 1) * (2 * WIN - 1) + (
        cols[:, None] - cols[None, :] + WIN - 1
    )
    span = (2 * WIN - 1) ** 2
    index = np.full((ROWS, ROWS), span, np.int32)
    index[:AREA, :AREA] = relative.T
    region = np.zeros((SIDE, SIDE), np.int32)
    bounds = ((0, SIDE - WIN), (SIDE - WIN, SIDE - SHIFT), (SIDE - SHIFT, SIDE))
    for a, rr in enumerate(bounds):
        for b, cc in enumerate(bounds):
            region[rr[0] : rr[1], cc[0] : cc[1]] = 3 * a + b
    across = SIDE // WIN
    cut = region.reshape(across, WIN, across, WIN).transpose(0, 2, 1, 3).reshape(across * across, AREA)
    mask = np.zeros((across * across, ROWS, ROWS), np.float32)
    mask[:, :AREA, :AREA] = np.where(cut[:, :, None] == cut[:, None, :], 0.0, -100.0)
    mask[:, AREA:, :] = PADDED
    mask = np.tile(mask, (1, 1, GROUP))
    perm = np.zeros((across * across * ROWS, SIDE * SIDE), np.float32)
    for w in range(across * across):
        for s in range(AREA):
            r = ((w // across) * WIN + s // WIN + SHIFT) % SIDE
            c = ((w % across) * WIN + s % WIN + SHIFT) % SIDE
            perm[w * ROWS + s, r * SIDE + c] = 1.0
    return index, mask, perm


def dot(a, b, dims=((1,), (0,))):
    return lax.dot_general(a, b, (dims, ((), ())), preferred_element_type=F32)


NT = ((1,), (1,))
TN = ((0,), (0,))


def standardize(x):
    c = x - jnp.mean(x, axis=-1, keepdims=True)
    inv = lax.rsqrt(jnp.mean(c * c, axis=-1, keepdims=True) + EPSILON)
    return c * inv, inv


def head_masks(dtype):
    lane = lax.broadcasted_iota(jnp.int32, (1, GROUP * HD), 1) // HD
    return [(lane == h).astype(F32).astype(dtype) for h in range(GROUP)]


def spread(x, masks):
    return jnp.concatenate([x * m for m in masks], axis=0)


def gather_heads(y, masks):
    out = y[:ROWS] * masks[0]
    for h in range(1, GROUP):
        out = out + y[h * ROWS : (h + 1) * ROWS] * masks[h]
    return out


def bits_of(n):
    return [1 << b for b in reversed(range(n.bit_length() - 1))]

class Cube:
    def __init__(self, fsdp, tp):
        self.f, self.t = lax.axis_index("fsdp"), lax.axis_index("tp")
        self.digits = [("tp", b) for b in bits_of(tp)] + [("fsdp", b) for b in bits_of(fsdp)]
        self.own = [lax.rem((self.t if a == "tp" else self.f) // b, 2) for a, b in self.digits]
        self.count = len(self.digits)
        self.n_t = len(bits_of(tp))

    def partner(self, k):
        axis, b = self.digits[k]
        step = b * (1 - 2 * self.own[k])
        if axis == "tp":
            return (self.f, self.t + step)
        return (self.f + step, self.t)

    def at(self, free, flip=None):
        out = []
        for k in range(self.count):
            if k in free:
                out.append(slice(None))
            else:
                out.append(1 - self.own[k] if k == flip else self.own[k])
        return tuple(out)


def greet(cube, digits):
    bar = pltpu.get_barrier_semaphore()
    for k in digits:
        pl.semaphore_signal(bar, inc=1, device_id=cube.partner(k), device_id_type=MESH)
    pl.semaphore_wait(bar, len(digits))


def gather_orders(cube):
    t, f = list(range(cube.n_t)), list(range(cube.n_t, cube.count))
    return (f + t, f[:-1] + t[:-1] + f[-1:] + t[-1:])


class Gather:
    def __init__(self, cube, full, chunks, send, recv):
        self.cube, self.full, self.chunks, self.send, self.recv = cube, full, chunks, send, recv
        self.orders = gather_orders(cube)

    def copies(self, c, s):
        lo, hi = self.chunks[c]
        rows = self.full.shape[self.cube.count]
        half = rows // 2
        for h, order in enumerate(self.orders):
            ref = self.full.at[self.cube.at(order[:s]) + (pl.ds(h * half, half), pl.ds(lo, hi - lo))]
            i = (c * self.cube.count + s) * 2 + h
            yield pltpu.make_async_remote_copy(ref, ref, self.send.at[i], self.recv.at[i],
                device_id=self.cube.partner(order[s]), device_id_type=MESH)

    def start(self, c, s):
        for copy in self.copies(c, s):
            copy.start()

    def wait(self, c, s):
        for copy in self.copies(c, s):
            copy.wait()

    def plan(self):
        n = self.cube.count
        return sorted(((c, s) for c in range(len(self.chunks)) for s in range(n + 1)), key=lambda e: (e[0] + e[1], e[0]))

    def advance(self, c, s):
        if s > 0:
            self.wait(c, s - 1)
        if s < self.cube.count:
            self.start(c, s)


def ag_kernel(pack_ref, full_ref, local, send, recv, *, fsdp, tp, chunks):
    cube = Cube(fsdp, tp)
    own = pltpu.make_async_copy(pack_ref, full_ref.at[cube.at(())], local)
    own.start()
    greet(cube, range(cube.count))
    own.wait()
    g = Gather(cube, full_ref, chunks, send, recv)
    for c, s in g.plan():
        g.advance(c, s)


def all_gather(pack, fsdp, tp, chunks):
    digits = len(bits_of(fsdp)) + len(bits_of(tp))
    n = len(chunks) * digits * 2
    return pl.pallas_call(
        functools.partial(ag_kernel, fsdp=fsdp, tp=tp, chunks=chunks),
        in_specs=[pl.BlockSpec(memory_space=pl.ANY)],
        out_specs=pl.BlockSpec(memory_space=pl.ANY),
        out_shape=jax.ShapeDtypeStruct((2,) * digits + pack.shape, pack.dtype),
        scratch_shapes=[pltpu.SemaphoreType.DMA, pltpu.SemaphoreType.DMA((n,)), pltpu.SemaphoreType.DMA((n,))],
        compiler_params=pltpu.CompilerParams(collective_id=1, has_side_effects=True),
        name="weights",
    )(pack)
def attn_fwd_kernel(img_ref, w_ref, b_ref, vec_ref, tab_ref, mask_ref, perm_ref, permt_ref, qkv_ref, p_ref, mix_ref, bias_scr, o_scr):
    n_win = mask_ref.shape[0]
    n_grp = w_ref.shape[0]
    gw = GROUP * HD

    @pl.when(pl.program_id(0) == 0)
    def _():
        for g in range(n_grp):
            full = jnp.concatenate([tab_ref[g * GROUP + h] for h in range(GROUP)], axis=1)
            for w in range(n_win):
                bias_scr[g, w] = full + mask_ref[w]

    x = img_ref[0].astype(F32)
    xhat, _ = standardize(x)
    normed = (xhat * vec_ref[0:1] + vec_ref[1:2]).astype(BF16)
    xp = dot(perm_ref[...], normed).astype(BF16)
    mb, mf = head_masks(BF16), head_masks(F32)
    for g in range(n_grp):
        c0 = g * 3 * gw
        acc = dot(xp, w_ref[g]) + b_ref[0:1, c0 : c0 + 3 * gw]
        q = (acc[:, :gw] * (HD ** -0.5)).astype(BF16)
        k = acc[:, gw : 2 * gw].astype(BF16)
        v = acc[:, 2 * gw :].astype(BF16)
        qkv_ref[0, :, c0 : c0 + gw] = q
        qkv_ref[0, :, c0 + gw : c0 + 2 * gw] = k
        qkv_ref[0, :, c0 + 2 * gw : c0 + 3 * gw] = v
        for w in range(n_win):
            r = slice(w * ROWS, (w + 1) * ROWS)
            s = dot(k[r], spread(q[r], mb), NT) + bias_scr[g, w]
            e = jnp.exp(s - jnp.max(s, axis=0, keepdims=True))
            p = (e * (1.0 / jnp.sum(e, axis=0, keepdims=True))).astype(BF16)
            p_ref[0, g, w] = p
            o = gather_heads(dot(p, v[r], TN), mf)
            o_scr[r, g * gw : (g + 1) * gw] = o.astype(BF16)
    mix_ref[0] = dot(permt_ref[...], o_scr[...]).astype(BF16)


def attn_fwd(images, w_all, bqkv, vecs, table, consts):
    mask, perm, permt = consts
    n = images.shape[0]
    t, c = images.shape[1:]
    n_win, n_grp = mask.shape[0], w_all.shape[0]
    cols = n_grp * 3 * GROUP * HD
    rows = n_win * ROWS
    whole = lambda a: pl.BlockSpec(a.shape, lambda i: (0,) * a.ndim)
    return pl.pallas_call(
        attn_fwd_kernel,
        grid=(n,),
        in_specs=[pl.BlockSpec((1, t, c), lambda i: (i, 0, 0)), pl.BlockSpec((n_grp, c, 3 * GROUP * HD), lambda i: (0, 0, 0))]
        + [whole(a) for a in (bqkv, vecs, table, mask, perm, permt)],
        out_specs=[
            pl.BlockSpec((1, rows, cols), lambda i: (i, 0, 0)),
            pl.BlockSpec((1, n_grp, n_win, ROWS, GROUP * ROWS), lambda i: (i, 0, 0, 0, 0)),
            pl.BlockSpec((1, t, c), lambda i: (i, 0, 0)),
        ],
        out_shape=[
            jax.ShapeDtypeStruct((n, rows, cols), BF16),
            jax.ShapeDtypeStruct((n, n_grp, n_win, ROWS, GROUP * ROWS), BF16),
            jax.ShapeDtypeStruct((n, t, c), BF16),
        ],
        scratch_shapes=[
            pltpu.VMEM((n_grp, n_win, ROWS, GROUP * ROWS), F32),
            pltpu.VMEM((rows, c), BF16),
        ],
        compiler_params=pltpu.CompilerParams(vmem_limit_bytes=48 << 20),
        name="attn_fwd",
    )(images, w_all, bqkv, vecs, table, mask, perm, permt)


SQRT_HALF = float(np.sqrt(0.5))
INV_SQRT_2PI = float(1.0 / np.sqrt(2.0 * np.pi))


class Spread:
    def __init__(self, cube, full, send, recv):
        self.cube, self.full, self.send, self.recv = cube, full, send, recv
        self.stages = cube.n_t

    def ref(self, s, i):
        own = self.cube.own
        return self.full.at[tuple(slice(None) if k < s else own[k] for k in range(self.stages)) + (i,)]

    def copy(self, s, i):
        ref = self.ref(s, i)
        return pltpu.make_async_remote_copy(
            ref, ref, self.send.at[s, i], self.recv.at[s, i], device_id=self.cube.partner(s), device_id_type=MESH
        )


def mlp_kernel(live_ref, img_ref, og_ref, mix_ref, w1_ref, w2_ref, wp_ref, vec_ref, b1_ref,
               full_ref, gres_ref, gmix_ref, grad_ref, dvec_ref, db1_ref,
               dw1, dw2, dwp, wp, out_scr, local, send, recv, *, ipb, fsdp, tp):
    step, steps = pl.program_id(0), pl.num_programs(0)
    n_tok, c = img_ref.shape[1:]
    rows = ipb * n_tok
    n_grp, _, chunk = w1_ref.shape
    cube = Cube(fsdp, tp)
    spread_out = Spread(cube, full_ref, send, recv)

    def keep(i):
        return pltpu.make_async_copy(out_scr.at[i], spread_out.ref(0, i), local.at[i])

    @pl.when(step == 0)
    def _():
        greet(cube, range(cube.n_t))
        dw1[...] = jnp.zeros_like(dw1)
        dw2[...] = jnp.zeros_like(dw2)
        dwp[...] = jnp.zeros_like(dwp)
        dvec_ref[...] = jnp.zeros_like(dvec_ref)
        db1_ref[...] = jnp.zeros_like(db1_ref)
        for g in range(n_grp):
            wp[:, g * GROUP * HD : (g + 1) * GROUP * HD] = wp_ref[g]

    @pl.when(step >= 1)
    def _():
        keep(step - 1).wait()
        spread_out.copy(0, step - 1).start()

    for s in range(1, cube.n_t):

        @pl.when(step >= 1 + s)
        def _():
            spread_out.copy(s - 1, step - 1 - s).wait()
            spread_out.copy(s, step - 1 - s).start()

    flat = lambda ref: jnp.concatenate([ref[i] for i in range(ipb)], axis=0) if ipb > 1 else ref[0]
    live = jnp.concatenate(
        [jnp.full((n_tok, 1), 1.0, F32) * live_ref[step * ipb + i] for i in range(ipb)], axis=0
    )
    mixed = flat(mix_ref)
    up = flat(og_ref).astype(F32) * live
    up16 = up.astype(BF16)
    res = flat(img_ref).astype(F32) + (dot(mixed, wp[...], NT) + vec_ref[2:3])
    xhat, inv = standardize(res)
    normed = (xhat * vec_ref[3:4] + vec_ref[4:5]).astype(BF16)
    branch = jnp.zeros((rows, c), F32)
    dn = jnp.zeros((rows, c), F32)
    for g in range(n_grp):
        cs = slice(g * chunk, (g + 1) * chunk)
        hid = dot(normed, w1_ref[g]) + b1_ref[0:1, cs]
        cdf = 0.5 * (1.0 + lax.erf(hid * SQRT_HALF))
        act = (hid * cdf).astype(BF16)
        slope = cdf + hid * (jnp.exp(-0.5 * hid * hid) * INV_SQRT_2PI)
        branch = branch + dot(act, w2_ref[g], NT)
        dw2[g] += dot(up16, act, TN)
        dh = (dot(up16, w2_ref[g]) * slope).astype(BF16)
        db1_ref[0:1, cs] += jnp.sum(dh.astype(F32), axis=0, keepdims=True)
        dw1[g] += dot(normed, dh, TN)
        dn = dn + dot(dh, w1_ref[g], NT)
    out = (live * (res + (branch + vec_ref[5:6]))).astype(BF16)
    for i in range(ipb):
        out_scr[step, i] = out[i * n_tok : (i + 1) * n_tok]
    keep(step).start()
    d = dn * vec_ref[3:4]
    gres = up + inv * (d - jnp.mean(d, axis=-1, keepdims=True) - xhat * jnp.mean(d * xhat, axis=-1, keepdims=True))
    gatt = gres.astype(BF16)
    dwp[...] += dot(gatt, mixed, TN)
    gmix = dot(gatt, wp[...]).astype(BF16)
    for i in range(ipb):
        r = slice(i * n_tok, (i + 1) * n_tok)
        gres_ref[i] = gres[r]
        gmix_ref[i] = gmix[r]
    dvec_ref[2:3] += jnp.sum(gatt.astype(F32), axis=0, keepdims=True)
    dvec_ref[3:4] += jnp.sum(dn * xhat, axis=0, keepdims=True)
    dvec_ref[4:5] += jnp.sum(dn, axis=0, keepdims=True)
    dvec_ref[5:6] += jnp.sum(up, axis=0, keepdims=True)

    @pl.when(step == steps - 1)
    def _():
        last = full_ref.shape[cube.n_t] - 1
        keep(last).wait()
        spread_out.copy(0, last).start()
        for g in range(n_grp):
            grad_ref[g, :, :chunk] = dw1[g].astype(BF16)
            grad_ref[g, :, chunk : 2 * chunk] = dw2[g].astype(BF16)
            grad_ref[g, :, 2 * chunk :] = dwp[:, g * GROUP * HD : (g + 1) * GROUP * HD].astype(BF16)
        for s in range(1, cube.n_t):
            for i in range(max(last - s, 0), last + 1):
                if i + s >= last:
                    spread_out.copy(s - 1, i).wait()
                    spread_out.copy(s, i).start()
        for i in range(last + 1):
            spread_out.copy(cube.n_t - 1, i).wait()


def mlp(live, images, out_grad, mixed, w_all, vecs, b1, fsdp, tp, ipb=2):
    n, t, c = images.shape
    n_grp = w_all.shape[0]
    ff = b1.shape[1]
    chunk, gw = ff // n_grp, GROUP * HD
    steps, n_t = n // ipb, len(bits_of(tp))
    whole = lambda s: pl.BlockSpec(s, lambda i: (0,) * len(s))
    once = lambda s, at=None: pl.BlockSpec(s, lambda i: at or (0,) * len(s), pipeline_mode=pl.Buffered(1))
    blk = pl.BlockSpec((ipb, t, c), lambda i: (i, 0, 0))
    first = 4 * gw
    return pl.pallas_call(
        functools.partial(mlp_kernel, ipb=ipb, fsdp=fsdp, tp=tp),
        grid=(steps,),
        in_specs=[pl.BlockSpec(memory_space=pltpu.SMEM), blk, blk, blk]
        + [
            once((n_grp, c, chunk), (0, 0, first // chunk)),
            once((n_grp, c, chunk), (0, 0, first // chunk + 1)),
            once((n_grp, c, gw), (0, 0, (first + 2 * chunk) // gw)),
        ]
        + [once(a.shape) for a in (vecs, b1)],
        out_specs=[pl.BlockSpec(memory_space=pl.ANY), blk, blk]
        + [whole(s) for s in ((n_grp, c, 2 * chunk + gw), (8, c), (1, ff))],
        out_shape=[
            jax.ShapeDtypeStruct((2,) * n_t + (steps, ipb, t, c), BF16),
            jax.ShapeDtypeStruct((n, t, c), F32),
            jax.ShapeDtypeStruct((n, t, c), BF16),
            jax.ShapeDtypeStruct((n_grp, c, 2 * chunk + gw), BF16),
            jax.ShapeDtypeStruct((8, c), F32),
            jax.ShapeDtypeStruct((1, ff), F32),
        ],
        scratch_shapes=[
            pltpu.VMEM((n_grp, c, chunk), F32),
            pltpu.VMEM((n_grp, c, chunk), F32),
            pltpu.VMEM((c, c), F32),
            pltpu.VMEM((c, c), BF16),
            pltpu.VMEM((steps, ipb, t, c), BF16),
            pltpu.SemaphoreType.DMA((steps,)),
            pltpu.SemaphoreType.DMA((n_t, steps)),
            pltpu.SemaphoreType.DMA((n_t, steps)),
        ],
        compiler_params=pltpu.CompilerParams(
            vmem_limit_bytes=58 << 20, collective_id=2, has_side_effects=True
        ),
        name="mlp",
    )(live, images, out_grad, mixed, w_all, w_all, w_all, vecs, b1)


def blocks_of(ref, n, body):
    if n == 0:
        body(())
        return

    def one(i, carry):
        body(tuple(lax.rem(lax.div(i, 2 ** (n - 1 - k)), 2) for k in range(n)))
        return carry

    lax.fori_loop(0, 2**n, one, 0)


class Reduce:
    def __init__(self, cube, acc, order, bufs, send, recv, n_digits):
        self.cube, self.acc, self.order, self.bufs = cube, acc, order, bufs
        self.send, self.recv, self.n_digits = send, recv, n_digits
        self.stages = len(order)

    def at(self, free, flip=None):
        own = self.cube.own
        return tuple(
            slice(None) if k in free else (1 - own[k] if k == flip else own[k]) for k in range(self.n_digits)
        )

    def left(self, s):
        return [k for k in self.order[s + 1 :] if k < self.n_digits]

    def copy(self, s):
        return pltpu.make_async_remote_copy(
            self.acc.at[self.at(self.left(s), self.order[s])],
            self.bufs[s],
            self.send.at[s],
            self.recv.at[s],
            device_id=self.cube.partner(self.order[s]),
            device_id_type=MESH,
        )

    def start(self, s):
        self.copy(s).start()

    def finish(self, s, out=None):
        self.copy(s).wait()
        free = sorted(self.left(s))
        own = self.cube.own

        def add(index):
            at = dict(zip(free, index))
            dst = tuple(at.get(k, own[k]) for k in range(self.n_digits))
            total = self.acc[dst].astype(F32) + self.bufs[s][index].astype(F32)
            if out is None:
                self.acc[dst] = total.astype(self.acc.dtype)
            else:
                out(total)

        blocks_of(self.acc, len(free), add)


def reduce_orders(n_t, n):
    t, f = list(range(n_t)), list(range(n_t, n))
    t_in, f_in = t[1:][::-1], f[::-1]
    early = (t_in + f_in + t[:1], t_in + f[:-1][::-1] + f[-1:] + t[:1])
    late = (t_in + f[-1:] + t[:1] + f[:-1][::-1], t_in + t[:1] + f_in)
    return early, late, t[::-1] + f_in


def attn_bwd_kernel(img_ref, gres_ref, gmix_ref, qkv_ref, p_ref, w_ref, vec_ref, perm_ref, permt_ref, grad_ref, dvec_in, db1_ref,
                    full_ref, dqkv_ref, dw1_ref, dw2_ref, dwp_ref, small_ref,
                    dqkv_scr, dw_ref, dvec_ref, db_ref, dtab_ref, gin_scr,
                    acc_a, acc_b, late_a, late_b, small, *rest, fsdp, tp):
    step, steps = pl.program_id(0), pl.num_programs(0)
    n_img = full_ref.shape[len(bits_of(tp))]
    n_grp, n_win = p_ref.shape[1:3]
    gw = GROUP * HD
    ff_cut = dw1_ref.shape[1]
    cube = Cube(fsdp, tp)
    n, n_t = cube.count, cube.n_t
    early, late, both = reduce_orders(n_t, n)
    bufs, (load, local, send, recv, rs_send, rs_recv) = rest[: 5 * n], rest[5 * n :]
    cut_bufs = [bufs[k * n : (k + 1) * n] for k in range(5)]
    reduces = [
        Reduce(cube, acc, order, buf, rs_send.at[k], rs_recv.at[k], digits)
        for k, (acc, order, buf, digits) in enumerate(
            zip((acc_a, acc_b, late_a, late_b, small), early + late + (both,), cut_bufs, (n, n, n, n, n_t))
        )
    ]
    first, second, third, fourth, fifth = reduces
    loads = [
        pltpu.make_async_copy(grad_ref.at[(slice(None),) * n + (slice(None), pl.ds(0, ff_cut))], acc_a, load.at[0]),
        pltpu.make_async_copy(
            grad_ref.at[(slice(None),) * n + (slice(None), pl.ds(ff_cut, ff_cut + gw))], acc_b, load.at[1]
        ),
    ]
    spread_in = Spread(cube, full_ref, send, recv)

    def keep(i):
        return pltpu.make_async_copy(gin_scr.at[i], spread_in.ref(0, i), local.at[i])

    def result_a(total):
        dw1_ref[...] = total

    def result_b(total):
        dw2_ref[...] = total[:, :ff_cut].T
        dwp_ref[...] = total[:, ff_cut:].T

    events = {}

    def plan(at, *work):
        events.setdefault(at, []).extend(work)

    points = n_grp + 1

    def advance(red, s, out=None):
        def go():
            red.finish(s, out if s == n - 1 else None)
            if s < n - 1:
                red.start(s + 1)

        return go

    begin = 2
    plan(begin, lambda: [(ld.wait(), red.start(0)) for ld, red in zip(loads, (first, second))])
    span = (n_img * points - begin - 2) // (n + 1)
    for s in range(n):
        plan(begin + (s + 1) * span, advance(first, s, result_a), advance(second, s, result_b))

    def point(k):
        for at in sorted(events):
            if at % points == k:

                @pl.when(step == at // points)
                def _(at=at):
                    for work in events[at]:
                        work()

    @pl.when(step == 0)
    def _():
        for ld in loads:
            ld.start()
        greet(cube, range(n))
        dw_ref[...] = jnp.zeros_like(dw_ref)
        dvec_ref[...] = dvec_in[...]
        db_ref[...] = jnp.zeros_like(db_ref)
        dtab_ref[...] = jnp.zeros_like(dtab_ref)

    @pl.when(step >= 1)
    def _():
        keep(step - 1).wait()
        spread_in.copy(0, step - 1).start()

    for s in range(1, n_t):

        @pl.when(step >= 1 + s)
        def _():
            spread_in.copy(s - 1, step - 1 - s).wait()
            spread_in.copy(s, step - 1 - s).start()

    mb, mf = head_masks(BF16), head_masks(F32)
    x = img_ref[0].astype(F32)
    xhat, inv = standardize(x)
    normed = (xhat * vec_ref[0:1] + vec_ref[1:2]).astype(BF16)
    xp = dot(perm_ref[...], normed).astype(BF16)
    gm = dot(perm_ref[...], gmix_ref[0]).astype(BF16)
    dn = jnp.zeros((n_win * ROWS, x.shape[1]), F32)
    for g in range(n_grp):
        point(g)
        c0 = g * 3 * gw
        tab = jnp.zeros((ROWS, GROUP * ROWS), F32)
        for w in range(n_win):
            r = slice(w * ROWS, (w + 1) * ROWS)
            q = qkv_ref[0, r, c0 : c0 + gw]
            k = qkv_ref[0, r, c0 + gw : c0 + 2 * gw]
            v = qkv_ref[0, r, c0 + 2 * gw : c0 + 3 * gw]
            do = spread(gm[r, g * gw : (g + 1) * gw], mb)
            p = p_ref[0, g, w]
            dqkv_scr[r, 2 * gw : 3 * gw] = dot(p, do).astype(BF16)
            dp = dot(v, do, NT)
            pf = p.astype(F32)
            ds = pf * (dp - jnp.sum(pf * dp, axis=0, keepdims=True))
            tab = tab + ds
            ds16 = ds.astype(BF16)
            dqkv_scr[r, gw : 2 * gw] = dot(ds16, spread(q, mb)).astype(BF16)
            dq = gather_heads(dot(ds16, k, TN), mf) * (HD ** -0.5)
            dqkv_scr[r, :gw] = dq.astype(BF16)
        dtab_ref[g] += tab
        dqkv = dqkv_scr[...]
        db_ref[0:1, c0 : c0 + 3 * gw] += jnp.sum(dqkv.astype(F32), axis=0, keepdims=True)
        dw_ref[g] += dot(xp, dqkv, TN)
        dn = dn + dot(dqkv, w_ref[g], NT)
    point(n_grp)
    hi = dn.astype(BF16)
    lo = (dn - hi.astype(F32)).astype(BF16)
    dn = dot(permt_ref[...], hi) + dot(permt_ref[...], lo)
    d = dn * vec_ref[0:1]
    gin = inv * (d - jnp.mean(d, axis=-1, keepdims=True) - xhat * jnp.mean(d * xhat, axis=-1, keepdims=True))
    gin_scr[step] = (gres_ref[0] + gin).astype(BF16)
    keep(step).start()
    dvec_ref[0:1] += jnp.sum(dn * xhat, axis=0, keepdims=True)
    dvec_ref[1:2] += jnp.sum(dn, axis=0, keepdims=True)

    @pl.when(step == steps - 1)
    def _():
        last = n_img - 1
        c, half = x.shape[1], 2 * gw
        cut = c // fsdp

        def fill(index):
            t, f = index[:n_t], index[n_t:]
            at = lambda part: functools.reduce(lambda a, b: 2 * a + b, part)
            rows = pl.ds(pl.multiple_of(at(f) * cut, cut), cut)
            late_a[index] = dw_ref[at(t), rows, :half].astype(BF16)
            late_b[index] = dw_ref[at(t), rows, half:].astype(BF16)

        blocks_of(late_a, n, fill)
        third.start(0)
        fourth.start(0)

        for g in range(n_grp):
            index = tuple((g >> (n_t - 1 - k)) & 1 for k in range(n_t))
            panel = small.at[index]
            panel[:ROWS] = dtab_ref[g]
            c0, f0, wide = g * 3 * gw, g * ff_cut, GROUP * ROWS
            panel[ROWS : ROWS + 1] = db_ref[0:1, c0 : c0 + wide]
            panel[ROWS + 1 : ROWS + 2] = jnp.concatenate(
                [db_ref[0:1, c0 + wide : c0 + 3 * gw], jnp.zeros((1, 2 * wide - 3 * gw), F32)], axis=1
            )
            for k in range(ff_cut // wide):
                panel[ROWS + 2 + k : ROWS + 3 + k] = db1_ref[0:1, f0 + k * wide : f0 + (k + 1) * wide]
            for i in range(6):
                for k in range(c // wide):
                    r = ROWS + 2 + ff_cut // wide + i * (c // wide) + k
                    panel[r : r + 1] = dvec_ref[i : i + 1, k * wide : (k + 1) * wide]
        fifth.start(0)

        keep(last).wait()
        spread_in.copy(0, last).start()
        for s in range(1, n_t):
            for i in range(max(last - s, 0), last + 1):
                if i + s >= last:
                    spread_in.copy(s - 1, i).wait()
                    spread_in.copy(s, i).start()

        def result_c(total):
            dqkv_ref[:, :half] = total

        def result_d(total):
            dqkv_ref[:, half:] = total

        def result_e(total):
            small_ref[...] = total

        for s in range(n):
            advance(third, s, result_c)()
            advance(fourth, s, result_d)()
            advance(fifth, s, result_e)()
        for i in range(n_img):
            spread_in.copy(n_t - 1, i).wait()


def attn_bwd(images, gres, gmix, qkv, p, w_all, vecs, consts, grads, dvec, db1, fsdp, tp):
    _, perm, permt = consts
    n_img, t, c = images.shape
    rows, cols = qkv.shape[1:]
    n_grp, n_win = p.shape[1:3]
    gw, wide = GROUP * HD, GROUP * ROWS
    ff_cut = db1.shape[1] // n_grp
    cut = c // fsdp
    n_t = len(bits_of(tp))
    n = n_t + len(bits_of(fsdp))
    digits = (2,) * n
    n_small = ROWS + 2 + ff_cut // wide + 6 * (c // wide)
    early, late, both = reduce_orders(n_t, n)
    half = 2 * gw
    bufs = []
    for order, width in zip(early + late, (ff_cut, ff_cut + gw, half, gw)):
        for s in range(n):
            bufs.append(pltpu.VMEM((2,) * (n - 1 - s) + (cut, width), BF16))
    for s in range(n):
        bufs.append(pltpu.VMEM((2,) * max(n_t - 1 - s, 0) + (n_small, wide), F32))
    whole = lambda s: pl.BlockSpec(s, lambda i: (0,) * len(s))
    once = lambda s: pl.BlockSpec(s, lambda i: (0,) * len(s), pipeline_mode=pl.Buffered(1))
    blk = pl.BlockSpec((1, t, c), lambda i: (i, 0, 0))
    any_spec = pl.BlockSpec(memory_space=pl.ANY)
    return pl.pallas_call(
        functools.partial(attn_bwd_kernel, fsdp=fsdp, tp=tp),
        grid=(n_img,),
        in_specs=[blk, blk, blk, pl.BlockSpec((1, rows, cols), lambda i: (i, 0, 0)),
                  pl.BlockSpec((1,) + p.shape[1:], lambda i: (i, 0, 0, 0, 0)), once((n_grp, c, 3 * gw))]
        + [once(a.shape) for a in (vecs, perm, permt)] + [any_spec] + [once(a.shape) for a in (dvec, db1)],
        out_specs=[any_spec] + [whole(s) for s in ((cut, 3 * gw), (cut, ff_cut), (ff_cut, cut), (gw, cut), (n_small, wide))],
        out_shape=[
            jax.ShapeDtypeStruct((2,) * n_t + (n_img, t, c), BF16),
            jax.ShapeDtypeStruct((cut, 3 * gw), F32),
            jax.ShapeDtypeStruct((cut, ff_cut), F32),
            jax.ShapeDtypeStruct((ff_cut, cut), F32),
            jax.ShapeDtypeStruct((gw, cut), F32),
            jax.ShapeDtypeStruct((n_small, wide), F32),
        ],
        scratch_shapes=[
            pltpu.VMEM((rows, 3 * gw), BF16),
            pltpu.VMEM((n_grp, c, 3 * gw), F32),
            pltpu.VMEM((8, c), F32),
            pltpu.VMEM((1, cols), F32),
            pltpu.VMEM((n_grp, ROWS, wide), F32),
            pltpu.VMEM((n_img, t, c), BF16),
            pltpu.VMEM(digits + (cut, ff_cut), BF16),
            pltpu.VMEM(digits + (cut, ff_cut + gw), BF16),
            pltpu.VMEM(digits + (cut, half), BF16),
            pltpu.VMEM(digits + (cut, gw), BF16),
            pltpu.VMEM((2,) * n_t + (n_small, wide), F32),
            *bufs,
            pltpu.SemaphoreType.DMA((2,)),
            pltpu.SemaphoreType.DMA((n_img,)),
            pltpu.SemaphoreType.DMA((n_t, n_img)),
            pltpu.SemaphoreType.DMA((n_t, n_img)),
            pltpu.SemaphoreType.DMA((5, n)),
            pltpu.SemaphoreType.DMA((5, n)),
        ],
        compiler_params=pltpu.CompilerParams(
            vmem_limit_bytes=58 << 20, collective_id=3, has_side_effects=True
        ),
        name="attn_bwd",
    )(images, gres, gmix, qkv, p, w_all, vecs, perm, permt, grads.reshape(digits + (cut, 2 * ff_cut + gw)), dvec, db1)


def per_device(
    images,
    attn_norm_gain,
    attn_norm_bias,
    qkv_weight,
    qkv_bias,
    position_table,
    proj_weight,
    proj_bias,
    mlp_norm_gain,
    mlp_norm_bias,
    fc1_weight,
    fc1_bias,
    fc2_weight,
    fc2_bias,
    image_count,
    out_grad,
    *,
    fsdp,
    tp,
):
    index, mask, perm = window_constants()
    span = position_table.shape[0]
    hot = jnp.asarray(index)[None] == jnp.arange(span, dtype=jnp.int32)[:, None, None]
    perm16 = jnp.asarray(perm).astype(BF16)
    consts = (jnp.asarray(mask), perm16, perm16.T)
    gw = GROUP * HD
    cut = qkv_weight.shape[0]
    width = cut * fsdp
    ff_cut = fc1_bias.shape[0]
    n_slots, n_tok, _ = images.shape
    mine = n_slots // tp
    first = lax.axis_index("tp") * mine
    img = lax.dynamic_slice_in_dim(images, first, mine, 0)
    cot = lax.dynamic_slice_in_dim(out_grad, first, mine, 0)
    live = (first + jnp.arange(mine, dtype=jnp.int32) < image_count[0]).astype(F32)

    vectors = (attn_norm_gain, attn_norm_bias, proj_bias, mlp_norm_gain, mlp_norm_bias, fc2_bias)
    flat = jnp.concatenate(vectors + (qkv_bias.reshape(-1), fc1_bias, position_table.reshape(-1)))
    lines = -(-flat.size // gw)
    flat = jnp.pad(flat, (0, lines * gw - flat.size)).reshape(lines, gw)
    pack = jnp.concatenate(
        [
            qkv_weight.reshape(cut, 3 * gw),
            jnp.pad(flat, ((0, cut - lines), (0, 0))),
            fc1_weight,
            fc2_weight.T,
            proj_weight.T,
        ],
        axis=1,
    )
    first_cols, cols = 4 * gw, pack.shape[1]
    chunks = ((0, first_cols), (first_cols, first_cols + ff_cut), (first_cols + ff_cut, cols))
    w_all = all_gather(pack, fsdp, tp, chunks)
    w_all = w_all.reshape(tp, width, cols)
    small = w_all[:, :, 3 * gw : 4 * gw].reshape(tp, fsdp, cut, gw)[:, :, :lines].reshape(tp, fsdp, lines * gw)
    vecs = small[0, :, : 6 * cut].reshape(fsdp, 6, cut).transpose(1, 0, 2).reshape(6, width).astype(F32)
    vecs = jnp.pad(vecs, ((0, 2), (0, 0)))
    rest = small[:, 0, 6 * cut :]
    n_qkv = qkv_bias.size
    b_qkv = rest[:, :n_qkv].reshape(1, tp * n_qkv).astype(F32)
    b_one = rest[:, n_qkv : n_qkv + ff_cut].reshape(1, tp * ff_cut).astype(F32)
    table = rest[:, n_qkv + ff_cut : n_qkv + ff_cut + position_table.size].reshape((tp,) + position_table.shape)
    table = table.transpose(0, 2, 1).reshape(-1, span)
    table = jnp.dot(table, hot.astype(BF16).reshape(span, -1), preferred_element_type=F32)
    table = table.reshape(-1, ROWS, ROWS)

    qkv, probs, mixed = attn_fwd(img, w_all, b_qkv, vecs, table, consts)
    output, gres, gmix, grads, dvec, db_one = mlp(live, img, cot, mixed, w_all, vecs, b_one, fsdp, tp)
    images_grad, d_qkv, d_one, d_two, d_proj, small = attn_bwd(
        img, gres, gmix, qkv, probs, w_all, vecs, consts, grads, dvec, db_one, fsdp, tp
    )
    wide = GROUP * ROWS
    d_tab = jnp.einsum(
        "jhi,rji->rh",
        small[:ROWS].reshape(ROWS, GROUP, ROWS),
        hot.astype(F32),
        precision=lax.Precision.HIGHEST,
    )
    at = ROWS + 2
    dqkv_bias = small[ROWS:at].reshape(-1)[:n_qkv].reshape(qkv_bias.shape)
    dfc1_bias = small[at : at + ff_cut // wide].reshape(-1)
    dvec = small[at + ff_cut // wide :].reshape(6, width)
    dvec = lax.dynamic_slice_in_dim(dvec, lax.axis_index("fsdp") * cut, cut, 1)
    return (
        output.reshape(images.shape),
        images_grad.reshape(images.shape),
        dvec[0],
        dvec[1],
        d_qkv.reshape(qkv_weight.shape),
        dqkv_bias,
        d_tab,
        d_proj,
        dvec[2],
        dvec[3],
        dvec[4],
        d_one,
        dfc1_bias,
        d_two,
        dvec[5],
    )


def solution(mesh):
    P = jax.sharding.PartitionSpec
    return jax.shard_map(
        functools.partial(per_device, fsdp=mesh.shape["fsdp"], tp=mesh.shape["tp"]),
        mesh=mesh,
        in_specs=(
            P("fsdp", None, None),
            P("fsdp"),
            P("fsdp"),
            P("fsdp", None, "tp"),
            P(None, "tp"),
            P(None, "tp"),
            P("tp", "fsdp"),
            P("fsdp"),
            P("fsdp"),
            P("fsdp"),
            P("fsdp", "tp"),
            P("tp"),
            P("tp", "fsdp"),
            P("fsdp"),
            P("fsdp"),
            P("fsdp", None, None),
        ),
        out_specs=(
            P("fsdp", None, None),
            P("fsdp", None, None),
            P("fsdp"),
            P("fsdp"),
            P("fsdp", None, "tp"),
            P(None, "tp"),
            P(None, "tp"),
            P("tp", "fsdp"),
            P("fsdp"),
            P("fsdp"),
            P("fsdp"),
            P("fsdp", "tp"),
            P("tp"),
            P("tp", "fsdp"),
            P("fsdp"),
        ),
        check_vma=False,
    )
```

time: 498 us -> 281 us (0.56)
  waiting for transfers between devices: 185 us -> 0 us
  Pallas kernels: 108 us -> 245 us
  blocking collectives: 79.6 us -> 0 us
  local copies, waits for them, and re-layouts: 86.4 us -> 29.8 us
  between operations: 16 us -> 1.82 us
  other arithmetic: 12.4 us -> 0.53 us
    reduce_scatter x1 -> x0, waiting for transfers between devices: 161 us -> none  [per_device(): grads = lax.psum_scatter(grads, both, scatter_dimension=0, tiled=True)]
    pallas_call x2 -> x3, Pallas kernels: 87.2 us -> 223 us  [the longest x1 112 us: attn_bwd(): pl.pallas_call(functools.partial(attn_bwd_kernel, fsdp=fsdp, tp=tp), grid...]
    psum x1 -> x0, blocking collectives: 39.9 us -> none  [per_device(): lax.psum(jnp.concatenate([dvec.reshape(-1), db_qkv[0], db_one[0], d_tab.T...]
    reshape x16 -> x7, local copies, waits for them, and re-layouts: 30.9 us -> 0.53 us  [the longest x2 0.23 us: per_device(): small[:ROWS].reshape(ROWS, GROUP, ROWS)]
    all_gather x1 -> x0, blocking collectives: 26.6 us -> none  [per_device(): vecs = lax.all_gather(vecs, 'fsdp', axis=1, tiled=True).astype(F32)]
    all_gather x3 -> x0, waiting for transfers between devices: 23.6 us -> none  [the longest x1 20 us: per_device(): lax.all_gather(pack, both, axis=0, tiled=False)]
    transpose x4 -> x1, local copies, waits for them, and re-layouts: 16.1 us -> 0.14 us  [per_device(): table = table.transpose(0, 2, 1).reshape(-1, span)]
    unnamed x1 -> x0, blocking collectives: 13.1 us -> none
  transfers between devices with their start and end apart: 4 -> 0, of which waited for: 3 -> 0; matrix products, arithmetic and copies ran while one was open for 13% -> 0% of each run, Pallas kernels for 0% -> 0%
where the time goes in v2:
time: 281 us
  Pallas kernels  245 us (87%)
  local copies, waits for them, and re-layouts  29.8 us (11%)
  matrix products  3.8 us (1%)
    pallas_call x1, Pallas kernels, attn_bwd(): pl.pallas_call(functools.partial(attn_bwd_kernel, fsdp=fsdp, tp=tp), grid...  112 us
    pallas_call x1, Pallas kernels, mlp(): pl.pallas_call(functools.partial(mlp_kernel, ipb=ipb, fsdp=fsdp, tp=tp),...  57.4 us
    pallas_call x1, Pallas kernels, all_gather(): pl.pallas_call(functools.partial(ag_kernel, fsdp=fsdp, tp=tp, chunks=chun...  53.8 us
    unnamed x74, local copies, waits for them, and re-layouts  24.1 us
    pallas_call x1, Pallas kernels, attn_fwd(): pl.pallas_call(attn_fwd_kernel, grid=(n,), in_specs=[pl.BlockSpec((1, t,...  21.9 us

profile of v2, /device:TPU:0, one launch (start us, length us, event | category | flops | bytes accessed | tf_op | source)
XLA Modules:
  0.0 281.1 jit_solution(16123361752252917398)
XLA Ops:
  1.3 0.5 compare_convert_fusion.live_ref
  1.8 2.1 constant_dynamic-slice_fusion.1
  4.1 0.5 copy.63.img_ref
  4.6 1.7 copy.64.og_ref
  6.3 0.1 copy.50
  6.5 0.1 reshape.140
  6.7 0.1 concatenate.6
  6.9 0.7 copy-done.8
  7.6 53.8 %weights.1 = bf16[2,2,2,2,2,64,1664]{6,5,4,3,2,1,0:T(8,128)(2,1)} custom-call(bf16[64,1664]{1,0:T(8,128)(2,1)} %copy-done.8), custom_call_target="tpu_custom_call" | custom-call | tf_op jit(solution)/shard_map/weights/pallas_call | solution.py:170
  61.4 1.1 slice.76
  62.7 0.1 convert_element_type.39
  62.9 0.2 reshape.145
  63.1 0.1 copy.53
  63.3 1.8 fusion.1
  65.0 0.2 copy.55.tab_ref
  65.3 21.9 %attn_fwd.1 = (bf16[8,256,1536]{2,1,0:T(8,128)(2,1)}, bf16[8,4,4,64,256]{4,3,2,1,0:T(8,128)(2,1)}, bf16[8,196,512]{2,1,0:T(8,128)(2,1)S(1)}) custom-call(bf16[8,196,512]{2,1,0:T(8,128)(2,1)S(1)} %copy.63.img_ref, bf16[4,512,1664]{2,1,0:T(8,128)(2,1)} %bitcast.64, f32[1,1536]{1,0:T(1,128)S(1)} %bitcast.62, f32[8,512]{1,0:T(8,128)S(1)} %pad_convert_fusion.vec_ref, ...), custom_call_target="tpu_custom_call" | custom-call | tf_op jit(solution)/shard_map/attn_fwd/pallas_call | solution.py:224
  87.2 1.2 copy-done.3
  88.4 0.6 copy.71
  89.0 57.4 %mlp.1 = (bf16[2,2,4,2,196,512]{5,4,3,2,1,0:T(8,128)(2,1)}, f32[8,196,512]{2,1,0:T(8,128)}, bf16[8,196,512]{2,1,0:T(8,128)(2,1)}, bf16[4,512,1152]{2,1,0:T(8,128...) custom-call(f32[8]{0:T(128)} %compare_convert_fusion.live_ref, bf16[8,196,512]{2,1,0:T(8,128)(2,1)} %copy-done.2, ...), custom_call_target="tpu_custom_call" | custom-call | tf_op jit(solution)/shard_map/mlp/pallas_call | solution.py:374
  146.4 7.8 %copy.57 = bf16[32,196,512]{2,0,1:T(8,128)(2,1)} copy(bf16[32,196,512]{2,1,0:T(8,128)(2,1)} %bitcast.70) | data formatting | bytes 12845056
  154.2 112.1 %attn_bwd.1 = (bf16[2,2,8,196,512]{4,3,2,1,0:T(8,128)(2,1)}, f32[64,384]{1,0:T(8,128)}, f32[64,512]{1,0:T(8,128)}, f32[512,64]{1,0:T(8,128)}, f32[128,64]{1,0:T(8,128)}, /*index=5*/f32[80,256]{1,0:T(8,128)}) custom-call(bf16[8,196,512]{2,1,0:T(8,128)(2,1)} %copy-done.2, f32[8,196,512]{2,1,0:T(8,128)} %get-tuple-element.32.gres_ref, ...), custom_call_target="tpu_custom_call" | custom-call | tf_op jit(solution)/shard_map/attn_bwd/pallas_call | solution.py:693
  266.3 7.9 %copy.58 = bf16[32,196,512]{2,0,1:T(8,128)(2,1)} copy(bf16[32,196,512]{2,1,0:T(8,128)(2,1)} %bitcast.69) | data formatting | bytes 12845056
  274.3 0.5 slice_bitcast_fusion.1
  274.9 0.6 copy_bitcast_fusion
  275.5 0.6 slice.68
  276.1 0.1 reshape.152
  276.2 0.1 copy.56
  276.4 2.0 fusion.6
  278.4 0.7 copy.60
  279.1 0.6 copy.72
  279.7 0.8 copy.61
  280.4 0.7 copy.83
  (78 shorter events, 0.6 us)
Async XLA Ops:
  0.6 5.7 %copy-start = (bf16[64,3,128]{2,0,1:T(8,128)(2,1)S(1)}, bf16[64,3,128]{2,0,1:T(8,128)(2,1)}, u32[]{:S(2)}) copy-start(bf16[64,3,128]{2,0,1:T(8,128)(2,1)} %param.22) | copy-start | bytes 147460
  4.0 2.4 copy-start.17
  4.0 2.6 copy-start.18
  4.0 2.6 copy-start.19
  4.0 2.6 copy-start.20
  4.0 2.6 copy-start.21
  4.0 2.6 copy-start.22
  4.0 2.6 copy-start.23
  4.0 2.6 copy-start.24
  4.1 2.6 copy-start.25
  4.1 2.7 copy-start.14
  4.1 2.8 copy-start.15
  4.1 2.8 copy-start.16
  4.6 60.6 %copy-start.2 = (bf16[8,196,512]{2,1,0:T(8,128)(2,1)}, bf16[8,196,512]{2,1,0:T(8,128)(2,1)S(1)}, u32[]{:S(2)}) copy-start(bf16[8,196,512]{2,1,0:T(8,128)(2,1)S(1)} %copy.63.img_ref) | copy-start | bytes 4816900
  6.9 0.7 copy-start.8
  7.6 55.7 %copy-start.27 = (s32[64,64]{1,0:T(8,128)S(1)}, s32[64,64]{1,0:T(8,128)}, u32[]{:S(2)}) copy-start(s32[64,64]{1,0:T(8,128)} %constant.41) | copy-start | bytes 49156
  7.6 57.7 %copy-start.4 = (bf16[256,196]{1,0:T(8,128)(2,1)S(1)}, bf16[256,196]{1,0:T(8,128)(2,1)}, u32[]{:S(2)}) copy-start(bf16[256,196]{1,0:T(8,128)(2,1)} %constant.39.perm_ref) | copy-start | bytes 301060
  7.6 57.7 %copy-start.5 = (bf16[196,256]{1,0:T(8,128)(2,1)S(1)}, bf16[196,256]{1,0:T(8,128)(2,1)}, u32[]{:S(2)}) copy-start(bf16[196,256]{1,0:T(8,128)(2,1)} %constant.40.permt_ref) | copy-start | bytes 301060
  7.6 57.7 %copy-start.6 = (f32[4,64,256]{2,1,0:T(8,128)S(1)}, f32[4,64,256]{2,1,0:T(8,128)}, u32[]{:S(2)}) copy-start(f32[4,64,256]{2,1,0:T(8,128)} %constant.31.clone.mask_ref) | copy-start | bytes 786436
  62.8 24.3 %copy-start.7 = (f32[8,512]{1,0:T(8,128)}, f32[8,512]{1,0:T(8,128)S(1)}, u32[]{:S(2)}) copy-start(f32[8,512]{1,0:T(8,128)S(1)} %pad_convert_fusion.vec_ref) | copy-start | bytes 49156
  87.2 1.2 copy-start.3
  266.3 8.0 %copy-start.12 = (f32[80,256]{1,0:T(8,128)S(1)}, f32[80,256]{1,0:T(8,128)}, u32[]{:S(2)}) copy-start(f32[80,256]{1,0:T(8,128)} %get-tuple-element.40) | copy-start | bytes 245764
  266.3 8.6 %copy-start.11 = (f32[64,384]{1,0:T(8,128)S(1)}, f32[64,384]{1,0:T(8,128)}, u32[]{:S(2)}) copy-start(f32[64,384]{1,0:T(8,128)} %get-tuple-element.41) | copy-start | bytes 294916
  266.3 10.1 %copy-start.26 = (s32[64,64]{0,1:T(8,128)S(1)}, s32[64,64]{0,1:T(8,128)}, u32[]{:S(2)}) copy-start(s32[64,64]{0,1:T(8,128)} %constant.29.clone) | copy-start | bytes 49156
  266.3 12.1 %copy-start.13 = (f32[128,64]{1,0:T(8,128)S(1)}, f32[128,64]{1,0:T(8,128)}, u32[]{:S(2)}) copy-start(f32[128,64]{1,0:T(8,128)} %get-tuple-element.67) | copy-start | bytes 98308
  266.3 13.4 %copy-start.9 = (f32[512,64]{1,0:T(8,128)S(1)}, f32[512,64]{1,0:T(8,128)}, u32[]{:S(2)}) copy-start(f32[512,64]{1,0:T(8,128)} %get-tuple-element.73) | copy-start | bytes 393220
  266.3 14.1 %copy-start.10 = (f32[64,512]{1,0:T(8,128)S(1)}, f32[64,512]{1,0:T(8,128)}, u32[]{:S(2)}) copy-start(f32[64,512]{1,0:T(8,128)} %get-tuple-element.111) | copy-start | bytes 393220
  266.3 14.8 %copy-start.1 = (bf16[64,3,128]{2,0,1:T(8,128)(2,1)S(1)}, bf16[64,3,128]{2,0,1:T(8,128)(2,1)}, u32[]{:S(2)}) copy-start(bf16[64,3,128]{2,0,1:T(8,128)(2,1)} %param.22) | copy-start | bytes 147460

commit v3 on v2

v3 whole, which is shorter than its diff:
```python
import functools
import jax
import jax.numpy as jnp
import numpy as np
from jax import lax
from jax.experimental import pallas as pl
from jax.experimental.pallas import tpu as pltpu

HD = 32
WIN = 7
SHIFT = 3
SIDE = 14
AREA = WIN * WIN
ROWS = 64
GROUP = 4
EPSILON = 1e-05
F32 = jnp.float32
BF16 = jnp.bfloat16
PADDED = -1e30
MESH = pl.DeviceIdType.MESH


def window_constants():
    offsets = np.arange(WIN)
    rows, cols = np.repeat(offsets, WIN), np.tile(offsets, WIN)
    relative = (rows[:, None] - rows[None, :] + WIN - 1) * (2 * WIN - 1) + (
        cols[:, None] - cols[None, :] + WIN - 1
    )
    span = (2 * WIN - 1) ** 2
    index = np.full((ROWS, ROWS), span, np.int32)
    index[:AREA, :AREA] = relative.T
    region = np.zeros((SIDE, SIDE), np.int32)
    bounds = ((0, SIDE - WIN), (SIDE - WIN, SIDE - SHIFT), (SIDE - SHIFT, SIDE))
    for a, rr in enumerate(bounds):
        for b, cc in enumerate(bounds):
            region[rr[0] : rr[1], cc[0] : cc[1]] = 3 * a + b
    across = SIDE // WIN
    cut = region.reshape(across, WIN, across, WIN).transpose(0, 2, 1, 3).reshape(across * across, AREA)
    mask = np.zeros((across * across, ROWS, ROWS), np.float32)
    mask[:, :AREA, :AREA] = np.where(cut[:, :, None] == cut[:, None, :], 0.0, -100.0)
    mask[:, AREA:, :] = PADDED
    mask = np.tile(mask, (1, 1, GROUP))
    perm = np.zeros((across * across * ROWS, SIDE * SIDE), np.float32)
    for w in range(across * across):
        for s in range(AREA):
            r = ((w // across) * WIN + s // WIN + SHIFT) % SIDE
            c = ((w % across) * WIN + s % WIN + SHIFT) % SIDE
            perm[w * ROWS + s, r * SIDE + c] = 1.0
    return index, mask, perm


def dot(a, b, dims=((1,), (0,))):
    return lax.dot_general(a, b, (dims, ((), ())), preferred_element_type=F32)


NT = ((1,), (1,))
TN = ((0,), (0,))


def standardize(x):
    c = x - jnp.mean(x, axis=-1, keepdims=True)
    inv = lax.rsqrt(jnp.mean(c * c, axis=-1, keepdims=True) + EPSILON)
    return c * inv, inv


def head_masks(dtype):
    lane = lax.broadcasted_iota(jnp.int32, (1, GROUP * HD), 1) // HD
    return [(lane == h).astype(F32).astype(dtype) for h in range(GROUP)]


def spread(x, masks):
    return jnp.concatenate([x * m for m in masks], axis=0)


def gather_heads(y, masks):
    out = y[:ROWS] * masks[0]
    for h in range(1, GROUP):
        out = out + y[h * ROWS : (h + 1) * ROWS] * masks[h]
    return out


def bits_of(n):
    return [1 << b for b in reversed(range(n.bit_length() - 1))]

class Cube:
    def __init__(self, fsdp, tp):
        self.f, self.t = lax.axis_index("fsdp"), lax.axis_index("tp")
        self.digits = [("tp", b) for b in bits_of(tp)] + [("fsdp", b) for b in bits_of(fsdp)]
        self.own = [lax.rem((self.t if a == "tp" else self.f) // b, 2) for a, b in self.digits]
        self.count = len(self.digits)
        self.n_t = len(bits_of(tp))

    def partner(self, k):
        axis, b = self.digits[k]
        step = b * (1 - 2 * self.own[k])
        if axis == "tp":
            return (self.f, self.t + step)
        return (self.f + step, self.t)

    def at(self, free, flip=None):
        out = []
        for k in range(self.count):
            if k in free:
                out.append(slice(None))
            else:
                out.append(1 - self.own[k] if k == flip else self.own[k])
        return tuple(out)


def greet(cube, digits):
    bar = pltpu.get_barrier_semaphore()
    for k in digits:
        pl.semaphore_signal(bar, inc=1, device_id=cube.partner(k), device_id_type=MESH)
    pl.semaphore_wait(bar, len(digits))


def gather_orders(cube):
    t, f = list(range(cube.n_t)), list(range(cube.n_t, cube.count))
    return (f + t, f[:-1] + t[:-1] + f[-1:] + t[-1:])


class Gather:
    def __init__(self, cube, full, chunks, send, recv):
        self.cube, self.full, self.chunks, self.send, self.recv = cube, full, chunks, send, recv
        self.orders = gather_orders(cube)

    def copies(self, c, s):
        lo, hi = self.chunks[c]
        rows = self.full.shape[self.cube.count]
        half = rows // 2
        for h, order in enumerate(self.orders):
            ref = self.full.at[self.cube.at(order[:s]) + (pl.ds(h * half, half), pl.ds(lo, hi - lo))]
            i = (c * self.cube.count + s) * 2 + h
            yield pltpu.make_async_remote_copy(ref, ref, self.send.at[i], self.recv.at[i],
                device_id=self.cube.partner(order[s]), device_id_type=MESH)

    def start(self, c, s):
        for copy in self.copies(c, s):
            copy.start()

    def wait(self, c, s):
        for copy in self.copies(c, s):
            copy.wait()

    def plan(self):
        n = self.cube.count
        return sorted(((c, s) for c in range(len(self.chunks)) for s in range(n + 1)), key=lambda e: (e[0] + e[1], e[0]))

    def advance(self, c, s):
        if s > 0:
            self.wait(c, s - 1)
        if s < self.cube.count:
            self.start(c, s)


def ag_kernel(pack_ref, full_ref, local, send, recv, *, fsdp, tp, chunks):
    cube = Cube(fsdp, tp)
    own = pltpu.make_async_copy(pack_ref, full_ref.at[cube.at(())], local)
    own.start()
    greet(cube, range(cube.count))
    own.wait()
    g = Gather(cube, full_ref, chunks, send, recv)
    for c, s in g.plan():
        g.advance(c, s)


def all_gather(pack, fsdp, tp, chunks):
    digits = len(bits_of(fsdp)) + len(bits_of(tp))
    n = len(chunks) * digits * 2
    return pl.pallas_call(
        functools.partial(ag_kernel, fsdp=fsdp, tp=tp, chunks=chunks),
        in_specs=[pl.BlockSpec(memory_space=pl.ANY)],
        out_specs=pl.BlockSpec(memory_space=pl.ANY),
        out_shape=jax.ShapeDtypeStruct((2,) * digits + pack.shape, pack.dtype),
        scratch_shapes=[pltpu.SemaphoreType.DMA, pltpu.SemaphoreType.DMA((n,)), pltpu.SemaphoreType.DMA((n,))],
        compiler_params=pltpu.CompilerParams(collective_id=1, has_side_effects=True),
        name="weights",
    )(pack)
def attn_fwd_kernel(img_ref, w_ref, b_ref, vec_ref, tab_ref, mask_ref, perm_ref, permt_ref, qkv_ref, p_ref, mix_ref, bias_scr, o_scr):
    n_win = mask_ref.shape[0]
    n_grp = w_ref.shape[0]
    gw = GROUP * HD

    @pl.when(pl.program_id(0) == 0)
    def _():
        for g in range(n_grp):
            full = jnp.concatenate([tab_ref[g * GROUP + h] for h in range(GROUP)], axis=1)
            for w in range(n_win):
                bias_scr[g, w] = full + mask_ref[w]

    x = img_ref[0].astype(F32)
    xhat, _ = standardize(x)
    normed = (xhat * vec_ref[0:1] + vec_ref[1:2]).astype(BF16)
    xp = dot(perm_ref[...], normed).astype(BF16)
    mb, mf = head_masks(BF16), head_masks(F32)
    for g in range(n_grp):
        c0 = g * 3 * gw
        acc = dot(xp, w_ref[g]) + b_ref[0:1, c0 : c0 + 3 * gw]
        qkv_ref[0, :, c0 : c0 + gw] = (acc[:, :gw] * (HD ** -0.5)).astype(BF16)
        qkv_ref[0, :, c0 + gw : c0 + 3 * gw] = acc[:, gw:].astype(BF16)

    def part(g, w, j):
        return qkv_ref[0, w * ROWS : (w + 1) * ROWS, (3 * g + j) * gw : (3 * g + j + 1) * gw]

    def score(g, w):
        return dot(part(g, w, 1), spread(part(g, w, 0), mb), NT) + bias_scr[g, w]

    def store(g, w, o):
        o_scr[w * ROWS : (w + 1) * ROWS, g * gw : (g + 1) * gw] = gather_heads(o, mf).astype(BF16)

    units = [(g, w) for g in range(n_grp) for w in range(n_win)]
    ahead, behind = score(*units[0]), None
    for at, (g, w) in enumerate(units):
        s = ahead
        if at + 1 < len(units):
            ahead = score(*units[at + 1])
        e = jnp.exp(s - jnp.max(s, axis=0, keepdims=True))
        p = (e * (1.0 / jnp.sum(e, axis=0, keepdims=True))).astype(BF16)
        p_ref[0, g, w] = p
        o = dot(p, part(g, w, 2), TN)
        if behind is not None:
            store(*behind)
        behind = (g, w, o)
    store(*behind)
    mix_ref[0] = dot(permt_ref[...], o_scr[...]).astype(BF16)


def attn_fwd(images, w_all, bqkv, vecs, table, consts):
    mask, perm, permt = consts
    n = images.shape[0]
    t, c = images.shape[1:]
    n_win, n_grp = mask.shape[0], w_all.shape[0]
    cols = n_grp * 3 * GROUP * HD
    rows = n_win * ROWS
    whole = lambda a: pl.BlockSpec(a.shape, lambda i: (0,) * a.ndim)
    return pl.pallas_call(
        attn_fwd_kernel,
        grid=(n,),
        in_specs=[pl.BlockSpec((1, t, c), lambda i: (i, 0, 0)), pl.BlockSpec((n_grp, c, 3 * GROUP * HD), lambda i: (0, 0, 0))]
        + [whole(a) for a in (bqkv, vecs, table, mask, perm, permt)],
        out_specs=[
            pl.BlockSpec((1, rows, cols), lambda i: (i, 0, 0)),
            pl.BlockSpec((1, n_grp, n_win, ROWS, GROUP * ROWS), lambda i: (i, 0, 0, 0, 0)),
            pl.BlockSpec((1, t, c), lambda i: (i, 0, 0)),
        ],
        out_shape=[
            jax.ShapeDtypeStruct((n, rows, cols), BF16),
            jax.ShapeDtypeStruct((n, n_grp, n_win, ROWS, GROUP * ROWS), BF16),
            jax.ShapeDtypeStruct((n, t, c), BF16),
        ],
        scratch_shapes=[
            pltpu.VMEM((n_grp, n_win, ROWS, GROUP * ROWS), F32),
            pltpu.VMEM((rows, c), BF16),
        ],
        compiler_params=pltpu.CompilerParams(vmem_limit_bytes=48 << 20),
        name="attn_fwd",
    )(images, w_all, bqkv, vecs, table, mask, perm, permt)


SQRT_HALF = float(np.sqrt(0.5))
INV_SQRT_2PI = float(1.0 / np.sqrt(2.0 * np.pi))
LANES = GROUP * HD
W_PROJ = 4 * LANES


class Spread:
    def __init__(self, cube, full, send, recv):
        self.cube, self.full, self.send, self.recv = cube, full, send, recv
        self.stages = cube.n_t

    def ref(self, s, i):
        own = self.cube.own
        return self.full.at[tuple(slice(None) if k < s else own[k] for k in range(self.stages)) + (i,)]

    def copy(self, s, i):
        ref = self.ref(s, i)
        return pltpu.make_async_remote_copy(
            ref, ref, self.send.at[s, i], self.recv.at[s, i], device_id=self.cube.partner(s), device_id_type=MESH
        )


def blocks_of(n, body):
    if n == 0:
        body(())
        return

    def one(i, carry):
        body(tuple(lax.rem(lax.div(i, 2 ** (n - 1 - k)), 2) for k in range(n)))
        return carry

    lax.fori_loop(0, 2**n, one, 0)


class Reduce:
    def __init__(self, cube, acc, order, bufs, send, recv, n_digits, out):
        self.cube, self.acc, self.order, self.bufs = cube, acc, order, bufs
        self.send, self.recv, self.n_digits, self.out = send, recv, n_digits, out
        self.stages = len(order)

    def at(self, free, flip=None):
        own = self.cube.own
        return tuple(
            slice(None) if k in free else (1 - own[k] if k == flip else own[k]) for k in range(self.n_digits)
        )

    def left(self, s):
        return sorted(k for k in self.order[s + 1 :] if k < self.n_digits)

    def copy(self, s):
        return pltpu.make_async_remote_copy(
            self.acc.at[self.at(self.left(s), self.order[s])],
            self.bufs[s],
            self.send.at[s],
            self.recv.at[s],
            device_id=self.cube.partner(self.order[s]),
            device_id_type=MESH,
        )

    def start(self):
        self.copy(0).start()

    def advance(self, s):
        self.copy(s).wait()
        free = self.left(s)
        own = self.cube.own

        def add(index):
            at = dict(zip(free, index))
            dst = tuple(at.get(k, own[k]) for k in range(self.n_digits))
            if s + 1 == self.stages:
                self.out(self.acc[dst].astype(F32) + self.bufs[s][index].astype(F32))
            else:
                self.acc[dst] = self.acc[dst] + self.bufs[s][index]

        blocks_of(len(free), add)
        if s + 1 < self.stages:
            self.copy(s + 1).start()


def reduce_orders(n_t, n):
    t, f = list(range(n_t)), list(range(n_t, n))
    t_in, f_in = t[1:][::-1], f[::-1]
    early = (t_in + f_in + t[:1], t_in + f[:-1][::-1] + f[-1:] + t[:1])
    late = (t_in + f[-1:] + t[:1] + f[:-1][::-1], t_in + t[:1] + f_in)
    return early, late, t[::-1] + f_in


def digits_of(value, n):
    return tuple((value >> (n - 1 - k)) & 1 for k in range(n))


def layer_kernel(live_ref, img_hbm, cot_hbm, mix_ref, w_hbm, vec_ref, b1_ref, qkv_ref, p_ref, perm_ref, permt_ref,
                 out_ref, gin_ref, dqkv_ref, dw1_ref, dw2_ref, dwp_ref, small_ref,
                 img_ref, cot_ref, w1_ref, w2_ref, wq_ref, wp, act, slope, normed_two, up_scr, gres_scr,
                 db1, dvec, dqkv_scr, dw, db, dtab, res_scr, acc, acc_p, late_a, late_b, small, *rest,
                 fsdp, tp, per, n_q):
    step = pl.program_id(0)
    cube = Cube(fsdp, tp)
    n, n_t, n_f = cube.count, cube.n_t, cube.count - cube.n_t
    n_img, n_tok, c = img_ref.shape
    n_grp, n_win = p_ref.shape[1:3]
    gw = LANES
    cut = c // fsdp
    fwd_steps = n_img // per
    bwd_at = fwd_steps
    att_at = bwd_at + n_q
    last_step = att_at + n_img - 1

    early, late, both = reduce_orders(n_t, n)
    bufs, rest = rest[: 5 * n], rest[5 * n :]
    load, local, send, recv, local_in, send_in, recv_in, rs_send, rs_recv = rest

    columns_at = lambda lo, width: w_hbm.at[:, :, pl.ds(lo, width)]
    wide_q = n_q * gw
    loads = [
        pltpu.make_async_copy(columns_at(lo, ref.shape[2]), ref, load.at[k])
        for k, (lo, ref) in enumerate(
            ((W_PROJ + gw, w1_ref), (W_PROJ + gw + wide_q, w2_ref), (0, wq_ref))
        )
    ]
    loads += [pltpu.make_async_copy(img_hbm, img_ref, load.at[3]), pltpu.make_async_copy(cot_hbm, cot_ref, load.at[4])]
    loads += [
        pltpu.make_async_copy(
            w_hbm.at[g, :, pl.ds(W_PROJ, gw)], wp.at[:, pl.ds(g * gw, gw)], load.at[5 + g]
        )
        for g in range(n_grp)
    ]
    gmix_scr = cot_ref

    def result_of(q):
        def out(total):
            dw1_ref[:, q * gw : (q + 1) * gw] = total[:, :gw]
            dw2_ref[q * gw : (q + 1) * gw] = total[:, gw:].T

        return out

    def result_p(total):
        dwp_ref[...] = total.T

    def result_a(total):
        dqkv_ref[:, : 2 * gw] = total

    def result_b(total):
        dqkv_ref[:, 2 * gw :] = total

    def result_s(total):
        small_ref[...] = total

    plans = [
        (acc.at[q], [ref.at[q] for ref in bufs[:n]], early[q % 2], n, result_of(q)) for q in range(n_q)
    ]
    plans += [
        (acc_p, bufs[n : 2 * n], early[0], n, result_p),
        (late_a, bufs[2 * n : 3 * n], late[0], n, result_a),
        (late_b, bufs[3 * n : 4 * n], late[1], n, result_b),
        (small, bufs[4 * n :], both, n_t, result_s),
    ]
    reduces = [
        Reduce(cube, ref, order, buf, rs_send.at[k], rs_recv.at[k], d, out)
        for k, (ref, buf, order, d, out) in enumerate(plans)
    ]
    n_early = n_q + 1
    spread_out = Spread(cube, out_ref, send, recv)
    spread_in = Spread(cube, gin_ref, send_in, recv_in)

    def keep_out(i):
        return pltpu.make_async_copy(res_scr.at[pl.ds(i * per, per)], spread_out.ref(0, i), local.at[i])

    def keep_in(i):
        return pltpu.make_async_copy(res_scr.at[i], spread_in.ref(0, i), local_in.at[i])

    events = {}

    def plan(at, work):
        events.setdefault(at, []).append(work)

    def point(k):
        for at in sorted(events):
            if at[1] == k:

                @pl.when(step == at[0])
                def _(at=at):
                    for work in events[at]:
                        work()

    def send_out(i):
        keep_out(i).wait()
        spread_out.copy(0, i).start()

    def pass_out(i, s):
        spread_out.copy(s - 1, i).wait()
        spread_out.copy(s, i).start()

    def send_in_(i):
        keep_in(i).wait()
        spread_in.copy(0, i).start()

    def pass_in(i, s):
        spread_in.copy(s - 1, i).wait()
        spread_in.copy(s, i).start()

    for i in range(fwd_steps):
        plan((i + 1, 0), functools.partial(send_out, i))
    later = [att_at - 1 + 3 * i for i in range(fwd_steps)]
    for s in range(1, n_t):
        for i in range(fwd_steps):
            plan((min(later[i] + s - 1, last_step), 0), functools.partial(pass_out, i, s))
    for i in range(n_img - 1):
        plan((att_at + i + 1, 0), functools.partial(send_in_, i))
    tail = []
    for i in range(n_img):
        for s in range(1, n_t):
            at = att_at + i + 3 + s
            if at <= last_step:
                plan((at, 0), functools.partial(pass_in, i, s))
            else:
                tail.append(functools.partial(pass_in, i, s))
    ends = []
    for k in range(n_early):
        begin = (bwd_at + k + 1, 1) if k + 1 < n_q else (att_at, 0)
        plan(begin, reduces[k].start)
        slots = SLOTS[k] if k < len(SLOTS) else ()
        for s in range(n):
            work = functools.partial(reduces[k].advance, s)
            if s < len(slots):
                plan((bwd_at + slots[s][0], slots[s][1]), work)
            else:
                ends.append(work)

    @pl.when(step == 0)
    def _():
        for ld in loads:
            ld.start()
        greet(cube, range(n))
        dw[...] = jnp.zeros_like(dw)
        dvec[...] = jnp.zeros_like(dvec)
        db[...] = jnp.zeros_like(db)
        db1[...] = jnp.zeros_like(db1)
        dtab[...] = jnp.zeros_like(dtab)
        for ld in loads:
            ld.wait()

    def columns(ref, q):
        at = pl.ds(pl.multiple_of(q * gw, gw), gw)
        return jnp.concatenate([ref[g, :, at] for g in range(n_grp)], axis=1)

    def rows_of(ref, b):
        return jnp.concatenate([ref[b * per + i] for i in range(per)], axis=0)

    def middle(b):
        mixed = rows_of(mix_ref, b)
        res = rows_of(img_ref, b).astype(F32) + (dot(mixed, wp[...], NT) + vec_ref[2:3])
        return (mixed, res) + standardize(res)

    @pl.when(step < bwd_at)
    def _():
        point(0)
        live = jnp.concatenate(
            [jnp.full((n_tok, 1), 1.0, F32) * live_ref[step * per + i] for i in range(per)], axis=0
        )
        up = rows_of(cot_ref, step).astype(F32) * live
        up_scr[step] = up.astype(BF16)
        dvec[5:6] += jnp.sum(up, axis=0, keepdims=True)
        mixed, res, xhat, _ = middle(step)
        normed_two[step] = (xhat * vec_ref[3:4] + vec_ref[4:5]).astype(BF16)

        def hidden_part(q, branch):
            hid = dot(normed_two[step], columns(w1_ref, q)) + b1_ref[pl.ds(q, 1)]
            cdf = 0.5 * (1.0 + lax.erf(hid * SQRT_HALF))
            a = (hid * cdf).astype(BF16)
            act[step, q] = a
            slope[step, q] = (cdf + hid * (jnp.exp(-0.5 * hid * hid) * INV_SQRT_2PI)).astype(BF16)
            return branch + dot(a, columns(w2_ref, q), NT)

        total = lax.fori_loop(0, n_q, hidden_part, res + vec_ref[5:6])
        out = (live * total).astype(BF16)
        for i in range(per):
            res_scr[step * per + i] = out[i * n_tok : (i + 1) * n_tok]
        keep_out(step).start()

    @pl.when(jnp.logical_and(step >= bwd_at, step < att_at))
    def _():
        q = step - bwd_at
        point(0)
        w2 = columns(w2_ref, q)
        d_one = d_two = None
        for b in range(fwd_steps):
            if b == 1:
                point(1)
            up = up_scr[b]
            dh = (dot(up, w2) * slope[b, q].astype(F32)).astype(BF16)
            slope[b, q] = dh
            db1[pl.ds(q, 1)] += jnp.sum(dh.astype(F32), axis=0, keepdims=True)
            one, two = dot(normed_two[b], dh, TN), dot(up, act[b, q], TN)
            d_one, d_two = (one, two) if b == 0 else (d_one + one, d_two + two)
        for t in range(n_grp):
            for f in range(fsdp):
                at = (q,) + digits_of(t, n_t) + digits_of(f, n_f)
                r, l = slice(f * cut, (f + 1) * cut), slice(t * gw, (t + 1) * gw)
                acc[at + (slice(None), slice(0, gw))] = d_one[r, l].astype(BF16)
                acc[at + (slice(None), slice(gw, 2 * gw))] = d_two[r, l].astype(BF16)

    @pl.when(step == att_at - 1)
    def _():
        def back(b, d_proj):
            dn = dot(slope[b, 0], columns(w1_ref, 0), NT)
            for k in range(1, n_q):
                dn = dn + dot(slope[b, k], columns(w1_ref, k), NT)
            mixed, _, xhat, inv = middle(b)
            d = dn * vec_ref[3:4]
            gres = up_scr[b].astype(F32) + inv * (
                d - jnp.mean(d, axis=-1, keepdims=True) - xhat * jnp.mean(d * xhat, axis=-1, keepdims=True)
            )
            gatt = gres.astype(BF16)
            gmix = dot(gatt, wp[...]).astype(BF16)
            for i in range(per):
                r = slice(i * n_tok, (i + 1) * n_tok)
                gres_scr[b * per + i] = gres[r]
                gmix_scr[b * per + i] = gmix[r]
            dvec[2:3] += jnp.sum(gatt.astype(F32), axis=0, keepdims=True)
            dvec[3:4] += jnp.sum(dn * xhat, axis=0, keepdims=True)
            dvec[4:5] += jnp.sum(dn, axis=0, keepdims=True)
            return d_proj + dot(gatt, mixed, TN)

        d_proj = lax.fori_loop(0, fwd_steps, back, jnp.zeros((c, c), F32))
        for t in range(n_grp):
            for f in range(fsdp):
                at = digits_of(t, n_t) + digits_of(f, n_f)
                acc_p[at] = d_proj[f * cut : (f + 1) * cut, t * gw : (t + 1) * gw].astype(BF16)

    @pl.when(step >= att_at)
    def _():
        j = step - att_at
        mb, mf = head_masks(BF16), head_masks(F32)
        point(0)
        x = img_ref[j].astype(F32)
        xhat, inv = standardize(x)
        normed = (xhat * vec_ref[0:1] + vec_ref[1:2]).astype(BF16)
        xp = dot(perm_ref[...], normed).astype(BF16)
        gm = dot(perm_ref[...], gmix_scr[j]).astype(BF16)
        dn = jnp.zeros((n_win * ROWS, c), F32)
        for g in range(n_grp):
            if g > 0:
                point(g)
            c0 = g * 3 * gw
            tab = jnp.zeros((ROWS, GROUP * ROWS), F32)
            cuts = [slice(w * ROWS, (w + 1) * ROWS) for w in range(n_win)]
            dos = [spread(gm[r, g * gw : (g + 1) * gw], mb) for r in cuts]
            dps = [dot(qkv_ref[0, r, c0 + 2 * gw : c0 + 3 * gw], do, NT) for r, do in zip(cuts, dos)]
            ps = [p_ref[0, g, w] for w in range(n_win)]
            dvs = [dot(p, do) for p, do in zip(ps, dos)]
            dss = []
            for p, dp in zip(ps, dps):
                pf = p.astype(F32)
                ds = pf * (dp - jnp.sum(pf * dp, axis=0, keepdims=True))
                tab = tab + ds
                dss.append(ds.astype(BF16))
            dks = [dot(ds, spread(qkv_ref[0, r, c0 : c0 + gw], mb)) for r, ds in zip(cuts, dss)]
            dqs = [dot(ds, qkv_ref[0, r, c0 + gw : c0 + 2 * gw], TN) for r, ds in zip(cuts, dss)]
            for r, dq, dk, dv in zip(cuts, dqs, dks, dvs):
                dqkv_scr[r, :gw] = (gather_heads(dq, mf) * (HD ** -0.5)).astype(BF16)
                dqkv_scr[r, gw : 2 * gw] = dk.astype(BF16)
                dqkv_scr[r, 2 * gw :] = dv.astype(BF16)
            dtab[g] += tab
            dqkv = dqkv_scr[...]
            db[0:1, c0 : c0 + 3 * gw] += jnp.sum(dqkv.astype(F32), axis=0, keepdims=True)
            dw[g] += dot(xp, dqkv, TN)
            dn = dn + dot(dqkv, wq_ref[g], NT)
        hi = dn.astype(BF16)
        lo = (dn - hi.astype(F32)).astype(BF16)
        dn = dot(permt_ref[...], hi) + dot(permt_ref[...], lo)
        d = dn * vec_ref[0:1]
        gin = inv * (
            d - jnp.mean(d, axis=-1, keepdims=True) - xhat * jnp.mean(d * xhat, axis=-1, keepdims=True)
        )
        res_scr[j] = (gres_scr[j] + gin).astype(BF16)
        keep_in(j).start()
        dvec[0:1] += jnp.sum(dn * xhat, axis=0, keepdims=True)
        dvec[1:2] += jnp.sum(dn, axis=0, keepdims=True)

    @pl.when(step == last_step)
    def _():
        def fill(index):
            t, f = index[:n_t], index[n_t:]
            at = lambda part: functools.reduce(lambda a, b: 2 * a + b, part)
            rows = pl.ds(pl.multiple_of(at(f) * cut, cut), cut)
            late_a[index] = dw[at(t), rows, : 2 * gw].astype(BF16)
            late_b[index] = dw[at(t), rows, 2 * gw :].astype(BF16)

        blocks_of(n, fill)
        for red in reduces[n_early : n_early + 2]:
            red.start()
        wide = GROUP * ROWS
        for g in range(n_grp):
            panel = small.at[digits_of(g, n_t)]
            panel[:ROWS] = dtab[g]
            c0 = g * 3 * gw
            panel[ROWS : ROWS + 1] = db[0:1, c0 : c0 + wide]
            panel[ROWS + 1 : ROWS + 2] = jnp.concatenate(
                [db[0:1, c0 + wide : c0 + 3 * gw], jnp.zeros((1, 2 * wide - 3 * gw), F32)], axis=1
            )
            r = ROWS + 2
            for q in range(0, n_q, 2):
                pair = [db1[q + k : q + k + 1, g * gw : (g + 1) * gw] for k in range(2)]
                panel[r : r + 1] = jnp.concatenate(pair, axis=1)
                r = r + 1
            for i in range(6):
                for k in range(c // wide):
                    panel[r : r + 1] = dvec[i : i + 1, k * wide : (k + 1) * wide]
                    r = r + 1
        reduces[n_early + 2].start()
        send_in_(n_img - 1)
        for work in ends:
            work()
        for s in range(n):
            for red in reduces[n_early:]:
                red.advance(s)
            if s == 0:
                for work in tail[: len(tail) // 2]:
                    work()
        for work in tail[len(tail) // 2 :]:
            work()
        for i in range(fwd_steps):
            spread_out.copy(n_t - 1, i).wait()
        for i in range(n_img):
            spread_in.copy(n_t - 1, i).wait()


SLOTS = (
    ((2, 0), (3, 1), (4, 0), (5, 2), (8, 0)),
    ((3, 0), (4, 0), (6, 0), (8, 0), (10, 0)),
    ((4, 0), (6, 2), (8, 2), (10, 2)),
    ((5, 2), (8, 0), (9, 3), (11, 2)),
    ((5, 2), (8, 0), (9, 3), (11, 2)),
)


def layer(live, images, out_grad, mixed, w_all, vecs, b1, qkv, p, perm, permt, fsdp, tp, per=4):
    n_img, t, c = mixed.shape
    rows, cols = qkv.shape[1:]
    n_grp, n_win = p.shape[1:3]
    gw, wide = LANES, GROUP * ROWS
    n_q = b1.shape[0]
    ff_cut = n_q * gw
    cut = c // fsdp
    n_t, n_f = len(bits_of(tp)), len(bits_of(fsdp))
    n = n_t + n_f
    digits = (2,) * n
    n_small = ROWS + 2 + ff_cut // wide + 6 * (c // wide)
    fwd_steps = n_img // per
    att_at = fwd_steps + n_q
    bufs = []
    for lead, width in (((n_q,), 2 * gw), ((), gw), ((), 2 * gw), ((), gw)):
        bufs += [pltpu.VMEM(lead + (2,) * (n - 1 - s) + (cut, width), BF16) for s in range(n)]
    bufs += [pltpu.VMEM((2,) * max(n_t - 1 - s, 0) + (n_small, wide), F32) for s in range(n)]
    whole = lambda s: pl.BlockSpec(s, lambda i: (0,) * len(s))
    once = lambda s: pl.BlockSpec(s, lambda i: (0,) * len(s), pipeline_mode=pl.Buffered(1))
    image = lambda i: jnp.clip(i - att_at, 0, n_img - 1)
    any_spec = pl.BlockSpec(memory_space=pl.ANY)
    hidden = (fwd_steps, n_q, per * t, n_grp * gw)
    return pl.pallas_call(
        functools.partial(layer_kernel, fsdp=fsdp, tp=tp, per=per, n_q=n_q),
        grid=(att_at + n_img,),
        in_specs=[
            pl.BlockSpec(memory_space=pltpu.SMEM),
            any_spec,
            any_spec,
            once(mixed.shape),
            any_spec,
            once(vecs.shape),
            once(b1.shape),
            pl.BlockSpec((1, rows, cols), lambda i: (image(i), 0, 0)),
            pl.BlockSpec((1,) + p.shape[1:], lambda i: (image(i), 0, 0, 0, 0)),
            once(perm.shape),
            once(permt.shape),
        ],
        out_specs=[any_spec, any_spec]
        + [whole(s) for s in ((cut, 3 * gw), (cut, ff_cut), (ff_cut, cut), (gw, cut), (n_small, wide))],
        out_shape=[
            jax.ShapeDtypeStruct((2,) * n_t + (fwd_steps, per, t, c), BF16),
            jax.ShapeDtypeStruct((2,) * n_t + (n_img, t, c), BF16),
            jax.ShapeDtypeStruct((cut, 3 * gw), F32),
            jax.ShapeDtypeStruct((cut, ff_cut), F32),
            jax.ShapeDtypeStruct((ff_cut, cut), F32),
            jax.ShapeDtypeStruct((gw, cut), F32),
            jax.ShapeDtypeStruct((n_small, wide), F32),
        ],
        scratch_shapes=[
            pltpu.VMEM((n_img, t, c), BF16),
            pltpu.VMEM((n_img, t, c), BF16),
            pltpu.VMEM((n_grp, c, ff_cut), BF16),
            pltpu.VMEM((n_grp, c, ff_cut), BF16),
            pltpu.VMEM((n_grp, c, 3 * gw), BF16),
            pltpu.VMEM((c, c), BF16),
            pltpu.VMEM(hidden, BF16),
            pltpu.VMEM(hidden, BF16),
            pltpu.VMEM((fwd_steps, per * t, c), BF16),
            pltpu.VMEM((fwd_steps, per * t, c), BF16),
            pltpu.VMEM((n_img, t, c), F32),
            pltpu.VMEM((8, n_grp * gw), F32),
            pltpu.VMEM((8, c), F32),
            pltpu.VMEM((rows, 3 * gw), BF16),
            pltpu.VMEM((n_grp, c, 3 * gw), F32),
            pltpu.VMEM((1, cols), F32),
            pltpu.VMEM((n_grp, ROWS, wide), F32),
            pltpu.VMEM((n_img, t, c), BF16),
            pltpu.VMEM((n_q,) + digits + (cut, 2 * gw), BF16),
            pltpu.VMEM(digits + (cut, gw), BF16),
            pltpu.VMEM(digits + (cut, 2 * gw), BF16),
            pltpu.VMEM(digits + (cut, gw), BF16),
            pltpu.VMEM((2,) * n_t + (n_small, wide), F32),
            *bufs,
            pltpu.SemaphoreType.DMA((5 + n_grp,)),
            pltpu.SemaphoreType.DMA((fwd_steps,)),
            pltpu.SemaphoreType.DMA((n_t, fwd_steps)),
            pltpu.SemaphoreType.DMA((n_t, fwd_steps)),
            pltpu.SemaphoreType.DMA((n_img,)),
            pltpu.SemaphoreType.DMA((n_t, n_img)),
            pltpu.SemaphoreType.DMA((n_t, n_img)),
            pltpu.SemaphoreType.DMA((n_q + 4, n)),
            pltpu.SemaphoreType.DMA((n_q + 4, n)),
        ],
        compiler_params=pltpu.CompilerParams(
            vmem_limit_bytes=60 << 20, collective_id=2, has_side_effects=True
        ),
        name="layer",
    )(live, images, out_grad, mixed, w_all, vecs, b1, qkv, p, perm, permt)


def per_device(
    images,
    attn_norm_gain,
    attn_norm_bias,
    qkv_weight,
    qkv_bias,
    position_table,
    proj_weight,
    proj_bias,
    mlp_norm_gain,
    mlp_norm_bias,
    fc1_weight,
    fc1_bias,
    fc2_weight,
    fc2_bias,
    image_count,
    out_grad,
    *,
    fsdp,
    tp,
):
    index, mask, perm = window_constants()
    span = position_table.shape[0]
    hot = jnp.asarray(index)[None] == jnp.arange(span, dtype=jnp.int32)[:, None, None]
    perm16 = jnp.asarray(perm).astype(BF16)
    consts = (jnp.asarray(mask), perm16, perm16.T)
    gw = GROUP * HD
    cut = qkv_weight.shape[0]
    width = cut * fsdp
    ff_cut = fc1_bias.shape[0]
    n_slots, n_tok, _ = images.shape
    mine = n_slots // tp
    first = lax.axis_index("tp") * mine
    img = lax.dynamic_slice_in_dim(images, first, mine, 0)
    cot = lax.dynamic_slice_in_dim(out_grad, first, mine, 0)
    live = (first + jnp.arange(mine, dtype=jnp.int32) < image_count[0]).astype(F32)

    vectors = (attn_norm_gain, attn_norm_bias, proj_bias, mlp_norm_gain, mlp_norm_bias, fc2_bias)
    flat = jnp.concatenate(vectors + (qkv_bias.reshape(-1), fc1_bias, position_table.reshape(-1)))
    lines = -(-flat.size // gw)
    flat = jnp.pad(flat, (0, lines * gw - flat.size)).reshape(lines, gw)
    pack = jnp.concatenate(
        [
            qkv_weight.reshape(cut, 3 * gw),
            jnp.pad(flat, ((0, cut - lines), (0, 0))),
            proj_weight.T,
            fc1_weight,
            fc2_weight.T,
        ],
        axis=1,
    )
    first_cols, cols = 4 * gw, pack.shape[1]
    chunks = ((0, first_cols), (first_cols, first_cols + gw + ff_cut), (first_cols + gw + ff_cut, cols))
    w_all = all_gather(pack, fsdp, tp, chunks)
    w_all = w_all.reshape(tp, width, cols)
    small = w_all[:, :, 3 * gw : 4 * gw].reshape(tp, fsdp, cut, gw)[:, :, :lines].reshape(tp, fsdp, lines * gw)
    vecs = small[0, :, : 6 * cut].reshape(fsdp, 6, cut).transpose(1, 0, 2).reshape(6, width).astype(F32)
    vecs = jnp.pad(vecs, ((0, 2), (0, 0)))
    rest = small[:, 0, 6 * cut :]
    n_qkv = qkv_bias.size
    b_qkv = rest[:, :n_qkv].reshape(1, tp * n_qkv).astype(F32)
    b_one = rest[:, n_qkv : n_qkv + ff_cut].reshape(1, tp * ff_cut).astype(F32)
    table = rest[:, n_qkv + ff_cut : n_qkv + ff_cut + position_table.size].reshape((tp,) + position_table.shape)
    table = table.transpose(0, 2, 1).reshape(-1, span)
    table = jnp.dot(table, hot.astype(BF16).reshape(span, -1), preferred_element_type=F32)
    table = table.reshape(-1, ROWS, ROWS)

    qkv, probs, mixed = attn_fwd(img, w_all, b_qkv, vecs, table, consts)
    b_one = b_one.reshape(tp, -1, gw).transpose(1, 0, 2).reshape(-1, tp * gw)
    output, images_grad, d_qkv, d_one, d_two, d_proj, small = layer(
        live, img, cot, mixed, w_all, vecs, b_one, qkv, probs, consts[1], consts[2], fsdp, tp
    )
    wide = GROUP * ROWS
    d_tab = jnp.einsum(
        "jhi,rji->rh",
        small[:ROWS].reshape(ROWS, GROUP, ROWS),
        hot.astype(F32),
        precision=lax.Precision.HIGHEST,
    )
    at = ROWS + 2
    dqkv_bias = small[ROWS:at].reshape(-1)[:n_qkv].reshape(qkv_bias.shape)
    dfc1_bias = small[at : at + ff_cut // wide].reshape(-1)
    dvec = small[at + ff_cut // wide :].reshape(6, width)
    dvec = lax.dynamic_slice_in_dim(dvec, lax.axis_index("fsdp") * cut, cut, 1)
    return (
        output.reshape(images.shape),
        images_grad.reshape(images.shape),
        dvec[0],
        dvec[1],
        d_qkv.reshape(qkv_weight.shape),
        dqkv_bias,
        d_tab,
        d_proj,
        dvec[2],
        dvec[3],
        dvec[4],
        d_one,
        dfc1_bias,
        d_two,
        dvec[5],
    )


def solution(mesh):
    P = jax.sharding.PartitionSpec
    return jax.shard_map(
        functools.partial(per_device, fsdp=mesh.shape["fsdp"], tp=mesh.shape["tp"]),
        mesh=mesh,
        in_specs=(
            P("fsdp", None, None),
            P("fsdp"),
            P("fsdp"),
            P("fsdp", None, "tp"),
            P(None, "tp"),
            P(None, "tp"),
            P("tp", "fsdp"),
            P("fsdp"),
            P("fsdp"),
            P("fsdp"),
            P("fsdp", "tp"),
            P("tp"),
            P("tp", "fsdp"),
            P("fsdp"),
            P("fsdp"),
            P("fsdp", None, None),
        ),
        out_specs=(
            P("fsdp", None, None),
            P("fsdp", None, None),
            P("fsdp"),
            P("fsdp"),
            P("fsdp", None, "tp"),
            P(None, "tp"),
            P(None, "tp"),
            P("tp", "fsdp"),
            P("fsdp"),
            P("fsdp"),
            P("fsdp"),
            P("fsdp", "tp"),
            P("tp"),
            P("tp", "fsdp"),
            P("fsdp"),
        ),
        check_vma=False,
    )
```

time: 281 us -> 236 us (0.84)
  Pallas kernels: 245 us -> 194 us
  local copies, waits for them, and re-layouts: 29.8 us -> 35 us
    pallas_call x2 -> x1, Pallas kernels: 169 us -> 122 us  [layer(): pl.pallas_call(functools.partial(layer_kernel, fsdp=fsdp, tp=tp, per=per,...]
    concatenate x1, local copies, waits for them, and re-layouts: 0.09 us -> 5.46 us  [per_device(): jnp.concatenate(vectors + (qkv_bias.reshape(-1), fc1_bias, position_table...]
    pallas_call x1, Pallas kernels: 21.9 us -> 18.7 us  [attn_fwd(): pl.pallas_call(attn_fwd_kernel, grid=(n,), in_specs=[pl.BlockSpec((1, t,...]
    unnamed x74 -> x54, local copies, waits for them, and re-layouts: 24.1 us -> 23 us
where the time goes in v3:
time: 236 us; the launch traced here: 235 us
  Pallas kernels  194 us (82%)
  local copies, waits for them, and re-layouts  35 us (15%)
  matrix products  3.61 us (2%)
    pallas_call x1, Pallas kernels, layer(): pl.pallas_call(functools.partial(layer_kernel, fsdp=fsdp, tp=tp, per=per,...  122 us
    pallas_call x1, Pallas kernels, all_gather(): pl.pallas_call(functools.partial(ag_kernel, fsdp=fsdp, tp=tp, chunks=chun...  54.2 us
    unnamed x54, local copies, waits for them, and re-layouts  23 us
    pallas_call x1, Pallas kernels, attn_fwd(): pl.pallas_call(attn_fwd_kernel, grid=(n,), in_specs=[pl.BlockSpec((1, t,...  18.7 us
    concatenate x1, local copies, waits for them, and re-layouts, per_device(): jnp.concatenate(vectors + (qkv_bias.reshape(-1), fc1_bias, position_table...  5.46 us

profile of v3, /device:TPU:0, one launch (start us, length us, event | category | flops | bytes accessed | tf_op | source)
XLA Modules:
  0.0 235.2 jit_solution(7862869733447267853)
XLA Ops:
  1.3 0.5 compare_convert_fusion.live_ref
  1.8 0.8 copy.50
  2.7 0.1 reshape.135
  2.8 5.5 %concatenate.6 = bf16[1956]{0:T(1024)(128)(2,1)S(1)} concatenate(bf16[64]{0:T(256)(128)(2,1)} %param.20, bf16[64]{0:T(256)(128)(2,1)} %param.21, bf16[64]{0:T(256)(128)(2,1)} %param.26, bf16[64]{0:T(256)(128)(2,1)} %param.27, bf16[64]{0:T(256)(128)(2,1)} %param.28, bf16[64]{0:T(256)(128)(2,1)} %param.32, bf16[384]{0:T(512)(128)(2,1)} %bitcast.85, bf16[512]{0:T(512)(128)(2,1)} %param.30, ...), dimensions={0} | concatenate | bytes 7824 | tf_op jit(solution)/shard_map/concatenate | solution.py:828
  8.3 0.7 bitcast_dynamic-update-slice_fusion.2
  9.0 0.8 constant_dynamic-update-slice_fusion
  9.9 0.8 bitcast_dynamic-update-slice_fusion.pack_ref
  10.7 2.2 constant_dynamic-slice_fusion.1
  12.9 1.7 copy.65.cot_hbm
  14.7 0.5 copy.64.img_ref.img_hbm
  15.2 54.2 %weights.1 = bf16[2,2,2,2,2,64,1664]{6,5,4,3,2,1,0:T(8,128)(2,1)} custom-call(bf16[64,1664]{1,0:T(8,128)(2,1)} %copy-done.8), custom_call_target="tpu_custom_call" | custom-call | tf_op jit(solution)/shard_map/weights/pallas_call | solution.py:170
  69.4 1.1 slice.76
  70.7 0.6 copy.79
  71.5 0.2 reshape.140
  71.7 0.1 copy.53
  71.9 1.6 fusion.1
  73.5 0.2 copy.55.tab_ref
  73.7 18.7 %attn_fwd.1 = (bf16[8,256,1536]{2,1,0:T(8,128)(2,1)}, bf16[8,4,4,64,256]{4,3,2,1,0:T(8,128)(2,1)}, bf16[8,196,512]{2,1,0:T(8,128)(2,1)S(1)}) custom-call(bf16[8,196,512]{2,1,0:T(8,128)(2,1)S(1)} %copy.64.img_ref.img_hbm, bf16[4,512,1664]{2,1,0:T(8,128)(2,1)} %bitcast.70, f32[1,1536]{1,0:T(1,128)S(1)} %bitcast.68, f32[8,512]{1,0:T(8,128)S(1)} %pad_convert_fusion.vec_ref, ...), custom_call_target="tpu_custom_call" | custom-call | tf_op jit(solution)/shard_map/attn_fwd/pallas_call | solution.py:236
  92.4 1.2 copy-done.3
  93.6 121.6 %layer.1 = (bf16[2,2,2,4,196,512]{5,4,3,2,1,0:T(8,128)(2,1)}, bf16[2,2,8,196,512]{4,3,2,1,0:T(8,128)(2,1)}, f32[64,384]{1,0:T(8,128)}, f32[64,512]{1,0:T(8,128)}...) custom-call(f32[8]{0:T(128)} %compare_convert_fusion.live_ref, bf16[8,196,512]{2,1,0:T(8,128)(2,1)} %copy-done.2, ...), custom_call_target="tpu_custom_call" | custom-call | tf_op jit(solution)/shard_map/layer/pallas_call | solution.py:721
  215.2 8.0 %copy.58 = bf16[32,196,512]{2,0,1:T(8,128)(2,1)} copy(bf16[32,196,512]{2,1,0:T(8,128)(2,1)} %bitcast.75) | data formatting | bytes 12845056
  223.2 5.1 %copy.59 = bf16[32,196,512]{2,0,1:T(8,128)(2,1)} copy(bf16[32,196,512]{2,1,0:T(8,128)(2,1)S(1)} %bitcast.74) | data formatting | bytes 12845056
  228.4 0.6 copy.73
  228.9 0.6 slice.68
  229.6 0.5 slice_bitcast_fusion.2
  230.2 0.7 copy.61
  230.9 0.1 reshape.148
  231.0 0.1 copy.57
  231.1 2.0 fusion.6
  233.1 0.6 copy_bitcast_fusion
  233.8 0.8 copy.62
  234.6 0.7 copy.86
  (58 shorter events, 0.6 us)
Async XLA Ops:
  0.6 7.6 %copy-start = (bf16[64,3,128]{2,0,1:T(8,128)(2,1)S(1)}, bf16[64,3,128]{2,0,1:T(8,128)(2,1)}, u32[]{:S(2)}) copy-start(bf16[64,3,128]{2,0,1:T(8,128)(2,1)} %param.22) | copy-start | bytes 147460
  10.7 3.9 %copy-start.8 = (bf16[64,1664]{1,0:T(8,128)(2,1)}, bf16[64,1664]{1,0:T(8,128)(2,1)S(1)}, u32[]{:S(2)}) copy-start(bf16[64,1664]{1,0:T(8,128)(2,1)S(1)} %bitcast_dynamic-update-slice_fusion.pack_ref) | copy-start | bytes 638980
  15.2 58.5 %copy-start.2 = (bf16[8,196,512]{2,1,0:T(8,128)(2,1)}, bf16[8,196,512]{2,1,0:T(8,128)(2,1)S(1)}, u32[]{:S(2)}) copy-start(bf16[8,196,512]{2,1,0:T(8,128)(2,1)S(1)} %copy.64.img_ref.img_hbm) | copy-start | bytes 4816900
  15.2 56.7 %copy-start.15 = (s32[64,64]{1,0:T(8,128)S(1)}, s32[64,64]{1,0:T(8,128)}, u32[]{:S(2)}) copy-start(s32[64,64]{1,0:T(8,128)} %constant.41) | copy-start | bytes 49156
  15.2 58.5 %copy-start.4 = (bf16[256,196]{1,0:T(8,128)(2,1)S(1)}, bf16[256,196]{1,0:T(8,128)(2,1)}, u32[]{:S(2)}) copy-start(bf16[256,196]{1,0:T(8,128)(2,1)} %constant.39.perm_ref) | copy-start | bytes 301060
  15.2 58.5 %copy-start.5 = (bf16[196,256]{1,0:T(8,128)(2,1)S(1)}, bf16[196,256]{1,0:T(8,128)(2,1)}, u32[]{:S(2)}) copy-start(bf16[196,256]{1,0:T(8,128)(2,1)} %constant.40.permt_ref) | copy-start | bytes 301060
  15.2 58.5 %copy-start.6 = (f32[4,64,256]{2,1,0:T(8,128)S(1)}, f32[4,64,256]{2,1,0:T(8,128)}, u32[]{:S(2)}) copy-start(f32[4,64,256]{2,1,0:T(8,128)} %constant.31.clone.mask_ref) | copy-start | bytes 786436
  71.5 20.9 %copy-start.7 = (f32[8,512]{1,0:T(8,128)}, f32[8,512]{1,0:T(8,128)S(1)}, u32[]{:S(2)}) copy-start(f32[8,512]{1,0:T(8,128)S(1)} %pad_convert_fusion.vec_ref) | copy-start | bytes 49156
  92.4 1.2 copy-start.3
  215.2 8.0 %slice-start = ((s8[6553600]{0:T(1024)(128)(4,1)}), s8[4194304]{0:T(1024)(128)(4,1)S(1)}, s32[]{:S(2)}) async-start(s8[6553600]{0:T(1024)(128)(4,1)} %bitcast.72), calls=%async_computation | async-start | bytes 8388608
  215.2 8.0 %slice-start.1 = ((s8[6553600]{0:T(1024)(128)(4,1)}), s8[2359296]{0:T(1024)(128)(4,1)S(1)}, s32[]{:S(2)}) async-start(s8[6553600]{0:T(1024)(128)(4,1)} %bitcast.72), calls=%async_computation.1 | async-start | bytes 4718592
  223.1 5.2 %copy-start.12 = (f32[80,256]{1,0:T(8,128)S(1)}, f32[80,256]{1,0:T(8,128)}, u32[]{:S(2)}) copy-start(f32[80,256]{1,0:T(8,128)} %get-tuple-element.30) | copy-start | bytes 245764
  223.2 7.0 %copy-start.13 = (f32[128,64]{1,0:T(8,128)S(1)}, f32[128,64]{1,0:T(8,128)}, u32[]{:S(2)}) copy-start(f32[128,64]{1,0:T(8,128)} %get-tuple-element.57) | copy-start | bytes 98308
  223.2 8.0 %copy-start.14 = (s32[64,64]{0,1:T(8,128)S(1)}, s32[64,64]{0,1:T(8,128)}, u32[]{:S(2)}) copy-start(s32[64,64]{0,1:T(8,128)} %constant.29.clone) | copy-start | bytes 49156
  223.2 10.0 %copy-start.11 = (f32[64,384]{1,0:T(8,128)S(1)}, f32[64,384]{1,0:T(8,128)}, u32[]{:S(2)}) copy-start(f32[64,384]{1,0:T(8,128)} %get-tuple-element.31) | copy-start | bytes 294916
  223.2 10.6 %copy-start.9 = (f32[512,64]{1,0:T(8,128)S(1)}, f32[512,64]{1,0:T(8,128)}, u32[]{:S(2)}) copy-start(f32[512,64]{1,0:T(8,128)} %get-tuple-element.63) | copy-start | bytes 393220
  223.2 11.4 %copy-start.10 = (f32[64,512]{1,0:T(8,128)S(1)}, f32[64,512]{1,0:T(8,128)}, u32[]{:S(2)}) copy-start(f32[64,512]{1,0:T(8,128)} %get-tuple-element.101) | copy-start | bytes 393220
  223.2 12.0 %copy-start.1 = (bf16[64,3,128]{2,0,1:T(8,128)(2,1)S(1)}, bf16[64,3,128]{2,0,1:T(8,128)(2,1)}, u32[]{:S(2)}) copy-start(bf16[64,3,128]{2,0,1:T(8,128)(2,1)} %param.22) | copy-start | bytes 147460

commit v4 on v3

--- a/solution.py
+++ b/solution.py
@@ -119,6 +119,9 @@
     return (f + t, f[:-1] + t[:-1] + f[-1:] + t[-1:])
 
 
+LAG = 1
+
+
 class Gather:
     def __init__(self, cube, full, chunks, send, recv):
         self.cube, self.full, self.chunks, self.send, self.recv = cube, full, chunks, send, recv
@@ -144,7 +147,7 @@
 
     def plan(self):
         n = self.cube.count
-        return sorted(((c, s) for c in range(len(self.chunks)) for s in range(n + 1)), key=lambda e: (e[0] + e[1], e[0]))
+        return sorted(((c, s) for c in range(len(self.chunks)) for s in range(n + 1)), key=lambda e: (LAG * e[0] + e[1], e[0]))
 
     def advance(self, c, s):
         if s > 0:
@@ -153,40 +156,98 @@
             self.start(c, s)
 
 
-def ag_kernel(pack_ref, full_ref, local, send, recv, *, fsdp, tp, chunks):
+LANES = GROUP * HD
+SMALL = 16
+W_SMALL = 3 * LANES
+W_PROJ = 5 * LANES
+W_ONE = 6 * LANES
+
+
+def digits_of(value, n):
+    return tuple((value >> (n - 1 - k)) & 1 for k in range(n))
+
+
+def front_kernel(*refs, fsdp, tp, chunks):
+    vectors, refs = refs[:6], refs[6:]
+    (bq_in, b1_in, tab_in, wq_in, wp_in, w1_in, w2_in, img_ref, rel_ref, mask_ref, perm_ref, permt_ref,
+     full_ref, qkv_ref, p_ref, mix_ref, vec_ref, b1_ref,
+     pack, wq, few, bq, tab, table, bias_scr, o_scr, local, send, recv) = refs
+    step, steps = pl.program_id(0), pl.num_programs(0)
     cube = Cube(fsdp, tp)
-    own = pltpu.make_async_copy(pack_ref, full_ref.at[cube.at(())], local)
-    own.start()
-    greet(cube, range(cube.count))
-    own.wait()
-    g = Gather(cube, full_ref, chunks, send, recv)
-    for c, s in g.plan():
-        g.advance(c, s)
-
-
-def all_gather(pack, fsdp, tp, chunks):
-    digits = len(bits_of(fsdp)) + len(bits_of(tp))
-    n = len(chunks) * digits * 2
-    return pl.pallas_call(
-        functools.partial(ag_kernel, fsdp=fsdp, tp=tp, chunks=chunks),
-        in_specs=[pl.BlockSpec(memory_space=pl.ANY)],
-        out_specs=pl.BlockSpec(memory_space=pl.ANY),
-        out_shape=jax.ShapeDtypeStruct((2,) * digits + pack.shape, pack.dtype),
-        scratch_shapes=[pltpu.SemaphoreType.DMA, pltpu.SemaphoreType.DMA((n,)), pltpu.SemaphoreType.DMA((n,))],
-        compiler_params=pltpu.CompilerParams(collective_id=1, has_side_effects=True),
-        name="weights",
-    )(pack)
-def attn_fwd_kernel(img_ref, w_ref, b_ref, vec_ref, tab_ref, mask_ref, perm_ref, permt_ref, qkv_ref, p_ref, mix_ref, bias_scr, o_scr):
-    n_win = mask_ref.shape[0]
-    n_grp = w_ref.shape[0]
-    gw = GROUP * HD
-
-    @pl.when(pl.program_id(0) == 0)
+    n, n_t, n_f = cube.count, cube.n_t, cube.count - cube.n_t
+    n_win, n_grp = mask_ref.shape[0], tp
+    gw = LANES
+    cut, ff_cut = w1_in.shape
+    heads, span = tab_in.shape
+    gather = Gather(cube, full_ref, chunks, send, recv)
+    order = gather.plan()
+    ready = order.index((0, n)) + 1
+    everything = (slice(None),) * n
+
+    @pl.when(step == 0)
     def _():
+        pack[:, W_SMALL:W_PROJ] = jnp.zeros((cut, W_PROJ - W_SMALL), BF16)
+        for i, ref in enumerate(vectors):
+            pack[i : i + 1, W_SMALL : W_SMALL + cut] = ref[...]
+        for k in range(3):
+            pack[:, k * gw : (k + 1) * gw] = wq_in[k]
+            pack[6 + k : 7 + k, W_SMALL : W_SMALL + gw] = bq_in[k : k + 1]
+        for k in range(ff_cut // gw):
+            pack[9 + k : 10 + k, W_SMALL : W_SMALL + gw] = b1_in[0:1, k * gw : (k + 1) * gw]
+        pack[0:heads, W_SMALL + gw : W_PROJ] = tab_in[:, :gw]
+        pack[heads : 2 * heads, W_SMALL + gw : W_SMALL + span] = tab_in[:, gw:]
+        pack[:, W_PROJ:W_ONE] = wp_in[...]
+        pack[:, W_ONE : W_ONE + ff_cut] = w1_in[...]
+        pack[:, W_ONE + ff_cut :] = w2_in[...]
+        own = pltpu.make_async_copy(pack, full_ref.at[cube.at(())], local.at[0])
+        own.start()
+        greet(cube, range(n))
+        own.wait()
+        for c, s in order[:ready]:
+            gather.advance(c, s)
+        loads = [
+            pltpu.make_async_copy(full_ref.at[everything + (slice(None), pl.ds(0, 3 * gw))], wq, local.at[0]),
+            pltpu.make_async_copy(
+                full_ref.at[everything + (pl.ds(0, SMALL), pl.ds(W_SMALL, W_PROJ - W_SMALL))], few, local.at[1]
+            ),
+        ]
+        for ld in loads:
+            ld.start()
+        for ld in loads:
+            ld.wait()
+        vec_ref[...] = jnp.zeros_like(vec_ref)
+        for f in range(fsdp):
+            part = few[(0,) * n_t + digits_of(f, n_f)].astype(F32)
+            vec_ref[0:6, f * cut : (f + 1) * cut] = part[0:6, :cut]
+        for t in range(tp):
+            part = few[digits_of(t, n_t) + (0,) * n_f].astype(F32)
+            for k in range(3):
+                at = (3 * t + k) * gw
+                bq[0:1, at : at + gw] = part[6 + k : 7 + k, :gw]
+            for k in range(ff_cut // gw):
+                b1_ref[k : k + 1, t * gw : (t + 1) * gw] = part[9 + k : 10 + k, :gw]
+            tab[t * heads : (t + 1) * heads, :gw] = part[0:heads, gw:]
+            tab[t * heads : (t + 1) * heads, gw:] = part[heads : 2 * heads, gw:]
+        table_rows = tab[...].astype(BF16)
+        wide = 8 * ROWS
+        for k in range(ROWS * ROWS // wide):
+            entry = lax.broadcasted_iota(jnp.int32, (2 * gw, wide), 0)
+            hot = (entry == rel_ref[0:1, k * wide : (k + 1) * wide]).astype(F32).astype(BF16)
+            value = dot(table_rows, hot)
+            for j in range(8):
+                table[:, k * 8 + j, :] = value[:, j * ROWS : (j + 1) * ROWS]
         for g in range(n_grp):
-            full = jnp.concatenate([tab_ref[g * GROUP + h] for h in range(GROUP)], axis=1)
+            full = jnp.concatenate([table[g * GROUP + h] for h in range(GROUP)], axis=1)
             for w in range(n_win):
                 bias_scr[g, w] = full + mask_ref[w]
+
+    rest = order[ready:]
+    for i, (c, s) in enumerate(rest):
+        at = 1 + 2 * (i // 2)
+
+        @pl.when(step == jnp.minimum(at, steps - 1))
+        def _(c=c, s=s):
+            gather.advance(c, s)
 
     x = img_ref[0].astype(F32)
     xhat, _ = standardize(x)
@@ -195,7 +256,8 @@
     mb, mf = head_masks(BF16), head_masks(F32)
     for g in range(n_grp):
         c0 = g * 3 * gw
-        acc = dot(xp, w_ref[g]) + b_ref[0:1, c0 : c0 + 3 * gw]
+        weight = wq[digits_of(g, n_t)].reshape(fsdp * cut, 3 * gw)
+        acc = dot(xp, weight) + bq[0:1, c0 : c0 + 3 * gw]
         qkv_ref[0, :, c0 : c0 + gw] = (acc[:, :gw] * (HD ** -0.5)).astype(BF16)
         qkv_ref[0, :, c0 + gw : c0 + 3 * gw] = acc[:, gw:].astype(BF16)
 
@@ -225,42 +287,65 @@
     mix_ref[0] = dot(permt_ref[...], o_scr[...]).astype(BF16)
 
 
-def attn_fwd(images, w_all, bqkv, vecs, table, consts):
-    mask, perm, permt = consts
-    n = images.shape[0]
-    t, c = images.shape[1:]
-    n_win, n_grp = mask.shape[0], w_all.shape[0]
-    cols = n_grp * 3 * GROUP * HD
-    rows = n_win * ROWS
-    whole = lambda a: pl.BlockSpec(a.shape, lambda i: (0,) * a.ndim)
+def front(vectors, b_qkv, b_one, table, w_qkv, w_proj, w_one, w_two, images, consts, fsdp, tp):
+    rel, mask, perm, permt = consts
+    n_img, t, c = images.shape
+    cut, ff_cut = w_one.shape
+    gw = LANES
+    n_win = mask.shape[0]
+    rows, cols = n_win * ROWS, W_ONE + 2 * ff_cut
+    heads = tp * table.shape[0]
+    n_t, n_f = len(bits_of(tp)), len(bits_of(fsdp))
+    n = n_t + n_f
+    chunks = ((0, W_PROJ), (W_PROJ, W_ONE + ff_cut), (W_ONE + ff_cut, cols))
+    n_sem = len(chunks) * n * 2
+    once = lambda a: pl.BlockSpec(a.shape, lambda i: (0,) * a.ndim, pipeline_mode=pl.Buffered(1))
+    whole = lambda s: pl.BlockSpec(s, lambda i: (0,) * len(s))
+    small = tuple(vectors) + (b_qkv, b_one, table, w_qkv, w_proj, w_one, w_two)
     return pl.pallas_call(
-        attn_fwd_kernel,
-        grid=(n,),
-        in_specs=[pl.BlockSpec((1, t, c), lambda i: (i, 0, 0)), pl.BlockSpec((n_grp, c, 3 * GROUP * HD), lambda i: (0, 0, 0))]
-        + [whole(a) for a in (bqkv, vecs, table, mask, perm, permt)],
+        functools.partial(front_kernel, fsdp=fsdp, tp=tp, chunks=chunks),
+        grid=(n_img,),
+        in_specs=[once(a) for a in small]
+        + [pl.BlockSpec((1, t, c), lambda i: (i, 0, 0))]
+        + [once(a) for a in (rel, mask, perm, permt)],
         out_specs=[
-            pl.BlockSpec((1, rows, cols), lambda i: (i, 0, 0)),
-            pl.BlockSpec((1, n_grp, n_win, ROWS, GROUP * ROWS), lambda i: (i, 0, 0, 0, 0)),
+            pl.BlockSpec(memory_space=pl.ANY),
+            pl.BlockSpec((1, rows, 3 * tp * gw), lambda i: (i, 0, 0)),
+            pl.BlockSpec((1, tp, n_win, ROWS, GROUP * ROWS), lambda i: (i, 0, 0, 0, 0)),
             pl.BlockSpec((1, t, c), lambda i: (i, 0, 0)),
+            whole((8, c)),
+            whole((ff_cut // gw, tp * gw)),
         ],
         out_shape=[
-            jax.ShapeDtypeStruct((n, rows, cols), BF16),
-            jax.ShapeDtypeStruct((n, n_grp, n_win, ROWS, GROUP * ROWS), BF16),
-            jax.ShapeDtypeStruct((n, t, c), BF16),
+            jax.ShapeDtypeStruct((2,) * n + (cut, cols), BF16),
+            jax.ShapeDtypeStruct((n_img, rows, 3 * tp * gw), BF16),
+            jax.ShapeDtypeStruct((n_img, tp, n_win, ROWS, GROUP * ROWS), BF16),
+            jax.ShapeDtypeStruct((n_img, t, c), BF16),
+            jax.ShapeDtypeStruct((8, c), F32),
+            jax.ShapeDtypeStruct((ff_cut // gw, tp * gw), F32),
         ],
         scratch_shapes=[
-            pltpu.VMEM((n_grp, n_win, ROWS, GROUP * ROWS), F32),
+            pltpu.VMEM((cut, cols), BF16),
+            pltpu.VMEM((2,) * n + (cut, 3 * gw), BF16),
+            pltpu.VMEM((2,) * n + (SMALL, W_PROJ - W_SMALL), BF16),
+            pltpu.VMEM((1, 3 * tp * gw), F32),
+            pltpu.VMEM((heads, 2 * gw), F32),
+            pltpu.VMEM((heads, ROWS, ROWS), F32),
+            pltpu.VMEM((tp, n_win, ROWS, GROUP * ROWS), F32),
             pltpu.VMEM((rows, c), BF16),
+            pltpu.SemaphoreType.DMA((2,)),
+            pltpu.SemaphoreType.DMA((n_sem,)),
+            pltpu.SemaphoreType.DMA((n_sem,)),
         ],
-        compiler_params=pltpu.CompilerParams(vmem_limit_bytes=48 << 20),
-        name="attn_fwd",
-    )(images, w_all, bqkv, vecs, table, mask, perm, permt)
+        compiler_params=pltpu.CompilerParams(
+            vmem_limit_bytes=60 << 20, collective_id=1, has_side_effects=True
+        ),
+        name="front",
+    )(*small, images, rel, mask, perm, permt)
 
 
 SQRT_HALF = float(np.sqrt(0.5))
 INV_SQRT_2PI = float(1.0 / np.sqrt(2.0 * np.pi))
-LANES = GROUP * HD
-W_PROJ = 4 * LANES
 
 
 class Spread:
@@ -343,10 +428,6 @@
     early = (t_in + f_in + t[:1], t_in + f[:-1][::-1] + f[-1:] + t[:1])
     late = (t_in + f[-1:] + t[:1] + f[:-1][::-1], t_in + t[:1] + f_in)
     return early, late, t[::-1] + f_in
-
-
-def digits_of(value, n):
-    return tuple((value >> (n - 1 - k)) & 1 for k in range(n))
 
 
 def layer_kernel(live_ref, img_hbm, cot_hbm, mix_ref, w_hbm, vec_ref, b1_ref, qkv_ref, p_ref, perm_ref, permt_ref,
@@ -390,12 +471,12 @@
     def result_of(q):
         def out(total):
             dw1_ref[:, q * gw : (q + 1) * gw] = total[:, :gw]
-            dw2_ref[q * gw : (q + 1) * gw] = total[:, gw:].T
+            dw2_ref[:, q * gw : (q + 1) * gw] = total[:, gw:]
 
         return out
 
     def result_p(total):
-        dwp_ref[...] = total.T
+        dwp_ref[...] = total
 
     def result_a(total):
         dqkv_ref[:, : 2 * gw] = total
@@ -735,14 +816,14 @@
             once(permt.shape),
         ],
         out_specs=[any_spec, any_spec]
-        + [whole(s) for s in ((cut, 3 * gw), (cut, ff_cut), (ff_cut, cut), (gw, cut), (n_small, wide))],
+        + [whole(s) for s in ((cut, 3 * gw), (cut, ff_cut), (cut, ff_cut), (cut, gw), (n_small, wide))],
         out_shape=[
             jax.ShapeDtypeStruct((2,) * n_t + (fwd_steps, per, t, c), BF16),
             jax.ShapeDtypeStruct((2,) * n_t + (n_img, t, c), BF16),
             jax.ShapeDtypeStruct((cut, 3 * gw), F32),
             jax.ShapeDtypeStruct((cut, ff_cut), F32),
-            jax.ShapeDtypeStruct((ff_cut, cut), F32),
-            jax.ShapeDtypeStruct((gw, cut), F32),
+            jax.ShapeDtypeStruct((cut, ff_cut), F32),
+            jax.ShapeDtypeStruct((cut, gw), F32),
             jax.ShapeDtypeStruct((n_small, wide), F32),
         ],
         scratch_shapes=[
@@ -810,60 +891,43 @@
 ):
     index, mask, perm = window_constants()
     span = position_table.shape[0]
-    hot = jnp.asarray(index)[None] == jnp.arange(span, dtype=jnp.int32)[:, None, None]
-    perm16 = jnp.asarray(perm).astype(BF16)
-    consts = (jnp.asarray(mask), perm16, perm16.T)
-    gw = GROUP * HD
+    gw = LANES
     cut = qkv_weight.shape[0]
     width = cut * fsdp
     ff_cut = fc1_bias.shape[0]
-    n_slots, n_tok, _ = images.shape
-    mine = n_slots // tp
+    n_qkv = qkv_bias.size
+    mine = images.shape[0] // tp
     first = lax.axis_index("tp") * mine
     img = lax.dynamic_slice_in_dim(images, first, mine, 0)
     cot = lax.dynamic_slice_in_dim(out_grad, first, mine, 0)
     live = (first + jnp.arange(mine, dtype=jnp.int32) < image_count[0]).astype(F32)
-
+    perm16 = jnp.asarray(perm).astype(BF16)
+    consts = (jnp.asarray(index).reshape(1, -1), jnp.asarray(mask), perm16, perm16.T)
     vectors = (attn_norm_gain, attn_norm_bias, proj_bias, mlp_norm_gain, mlp_norm_bias, fc2_bias)
-    flat = jnp.concatenate(vectors + (qkv_bias.reshape(-1), fc1_bias, position_table.reshape(-1)))
-    lines = -(-flat.size // gw)
-    flat = jnp.pad(flat, (0, lines * gw - flat.size)).reshape(lines, gw)
-    pack = jnp.concatenate(
-        [
-            qkv_weight.reshape(cut, 3 * gw),
-            jnp.pad(flat, ((0, cut - lines), (0, 0))),
-            proj_weight.T,
-            fc1_weight,
-            fc2_weight.T,
-        ],
-        axis=1,
+    w_all, qkv, probs, mixed, vecs, b_one = front(
+        [v.reshape(1, cut) for v in vectors],
+        qkv_bias,
+        fc1_bias.reshape(1, ff_cut),
+        position_table.T,
+        qkv_weight.transpose(1, 0, 2),
+        proj_weight.T,
+        fc1_weight,
+        fc2_weight.T,
+        img,
+        consts,
+        fsdp,
+        tp,
     )
-    first_cols, cols = 4 * gw, pack.shape[1]
-    chunks = ((0, first_cols), (first_cols, first_cols + gw + ff_cut), (first_cols + gw + ff_cut, cols))
-    w_all = all_gather(pack, fsdp, tp, chunks)
-    w_all = w_all.reshape(tp, width, cols)
-    small = w_all[:, :, 3 * gw : 4 * gw].reshape(tp, fsdp, cut, gw)[:, :, :lines].reshape(tp, fsdp, lines * gw)
-    vecs = small[0, :, : 6 * cut].reshape(fsdp, 6, cut).transpose(1, 0, 2).reshape(6, width).astype(F32)
-    vecs = jnp.pad(vecs, ((0, 2), (0, 0)))
-    rest = small[:, 0, 6 * cut :]
-    n_qkv = qkv_bias.size
-    b_qkv = rest[:, :n_qkv].reshape(1, tp * n_qkv).astype(F32)
-    b_one = rest[:, n_qkv : n_qkv + ff_cut].reshape(1, tp * ff_cut).astype(F32)
-    table = rest[:, n_qkv + ff_cut : n_qkv + ff_cut + position_table.size].reshape((tp,) + position_table.shape)
-    table = table.transpose(0, 2, 1).reshape(-1, span)
-    table = jnp.dot(table, hot.astype(BF16).reshape(span, -1), preferred_element_type=F32)
-    table = table.reshape(-1, ROWS, ROWS)
-
-    qkv, probs, mixed = attn_fwd(img, w_all, b_qkv, vecs, table, consts)
-    b_one = b_one.reshape(tp, -1, gw).transpose(1, 0, 2).reshape(-1, tp * gw)
+    w_all = w_all.reshape(tp, width, w_all.shape[-1])
     output, images_grad, d_qkv, d_one, d_two, d_proj, small = layer(
-        live, img, cot, mixed, w_all, vecs, b_one, qkv, probs, consts[1], consts[2], fsdp, tp
+        live, img, cot, mixed, w_all, vecs, b_one, qkv, probs, consts[2], consts[3], fsdp, tp
     )
     wide = GROUP * ROWS
+    hot = (jnp.asarray(index)[None] == jnp.arange(span, dtype=jnp.int32)[:, None, None]).astype(F32)
     d_tab = jnp.einsum(
         "jhi,rji->rh",
         small[:ROWS].reshape(ROWS, GROUP, ROWS),
-        hot.astype(F32),
+        hot,
         precision=lax.Precision.HIGHEST,
     )
     at = ROWS + 2
@@ -879,13 +943,13 @@
         d_qkv.reshape(qkv_weight.shape),
         dqkv_bias,
         d_tab,
-        d_proj,
+        d_proj.T,
         dvec[2],
         dvec[3],
         dvec[4],
         d_one,
         dfc1_bias,
-        d_two,
+        d_two.T,
         dvec[5],
     )
 

time: 236 us -> 211 us (0.89)
  Pallas kernels: 194 us -> 182 us
  local copies, waits for them, and re-layouts: 35 us -> 24.5 us
    pallas_call x2 -> x1, Pallas kernels: 72.9 us -> 64.6 us  [front(): pl.pallas_call(functools.partial(front_kernel, fsdp=fsdp, tp=tp, chunks=c...]
    concatenate x2 -> x0, local copies, waits for them, and re-layouts: 6.31 us -> none  [the longest x1 5.46 us: per_device(): jnp.concatenate(vectors + (qkv_bias.reshape(-1), fc1_bias, position_table...]
    pallas_call x1, Pallas kernels: 122 us -> 117 us  [layer(): pl.pallas_call(functools.partial(layer_kernel, fsdp=fsdp, tp=tp, per=per,...]
    unnamed x54 -> x24, local copies, waits for them, and re-layouts: 23 us -> 19.6 us
where the time goes in v4:
time: 211 us; the launch traced here: 210 us
  Pallas kernels  182 us (86%)
  local copies, waits for them, and re-layouts  24.5 us (12%)
    pallas_call x1, Pallas kernels, layer(): pl.pallas_call(functools.partial(layer_kernel, fsdp=fsdp, tp=tp, per=per,...  117 us
    pallas_call x1, Pallas kernels, front(): pl.pallas_call(functools.partial(front_kernel, fsdp=fsdp, tp=tp, chunks=c...  64.6 us
    unnamed x24, local copies, waits for them, and re-layouts  19.6 us

profile of v4, /device:TPU:0, one launch (start us, length us, event | category | flops | bytes accessed | tf_op | source)
XLA Modules:
  0.0 210.2 jit_solution(18433516757353053472)
XLA Ops:
  1.3 0.5 compare_convert_fusion.live_ref
  1.8 1.3 reshape.86.refs_7_
  3.1 2.1 %constant_dynamic-slice_fusion.1 = (bf16[8,196,512]{2,0,1:T(8,128)(2,1)S(1)}, bf16[8,196,512]{2,0,1:T(8,128)(2,1)S(1)}) fusion(bf16[32,196,512]{2,0,1:T(8,128)(2,1)} %param.34, s32[]{:T(128)S(6)} %select_n.7, bf16[32,196,512]{2,0,1:T(8,128)(2,1)} %param.19), kind=kLoop, calls=%fused_computation.8 | loop fusion | bytes 6422532 | tf_op jit(solution)/shard_map/dynamic_slice | solution.py:902
  5.2 1.7 copy.47.cot_hbm
  6.9 1.7 copy.46.refs_13_.img_hbm
  8.5 64.6 %front.1 = (bf16[2,2,2,2,2,64,1792]{6,5,4,3,2,1,0:T(8,128)(2,1)}, bf16[8,256,1536]{2,1,0:T(8,128)(2,1)}, bf16[8,4,4,64,256]{4,3,2,1,0:T(8,128)(2,1)}, bf16[8,196...) custom-call(bf16[1,64]{1,0:T(2,128)(2,1)} %bitcast.52, bf16[1,64]{1,0:T(2,128)(2,1)} %bitcast.53, ...), custom_call_target="tpu_custom_call" | custom-call | tf_op jit(solution)/shard_map/front/pallas_call | solution.py:305
  73.1 117.3 %layer.1 = (bf16[2,2,2,4,196,512]{5,4,3,2,1,0:T(8,128)(2,1)}, bf16[2,2,8,196,512]{4,3,2,1,0:T(8,128)(2,1)}, f32[64,384]{1,0:T(8,128)}, f32[64,512]{1,0:T(8,128)}...) custom-call(f32[8]{0:T(128)} %compare_convert_fusion.live_ref, ...), custom_call_target="tpu_custom_call" | custom-call | tf_op jit(solution)/shard_map/layer/pallas_call | solution.py:802
  190.4 0.0 copy-start
  190.4 8.0 %copy.43 = bf16[32,196,512]{2,0,1:T(8,128)(2,1)} copy(bf16[32,196,512]{2,1,0:T(8,128)(2,1)} %bitcast.43) | data formatting | bytes 12845056
  198.3 0.0 copy-done
  198.4 0.0 copy-start.4
  198.4 0.0 copy-start.5
  198.4 0.0 copy-start.2
  198.4 0.0 copy-start.1
  198.4 5.1 %copy.44 = bf16[32,196,512]{2,0,1:T(8,128)(2,1)} copy(bf16[32,196,512]{2,1,0:T(8,128)(2,1)S(1)} %bitcast.42) | data formatting | bytes 12845056
  203.5 0.0 copy-done.4
  203.5 0.6 copy.49
  204.1 0.6 slice.40
  204.7 0.1 constant_dynamic-slice_fusion
  204.8 0.5 slice_bitcast_fusion.1
  205.4 0.1 reshape.93
  205.5 0.1 copy.42
  205.6 0.0 copy-done.6
  205.6 2.0 fusion.2
  207.6 0.0 copy-done.3
  207.6 0.6 copy_bitcast_fusion
  208.3 0.0 copy-done.5
  208.3 0.6 copy.55
  208.9 0.0 copy-done.2
  208.9 0.7 copy.56
  209.5 0.0 copy-done.1
  209.5 0.7 copy.57
  (6 shorter events, 0.0 us)
Async XLA Ops:
  190.4 8.0 %copy-start = (bf16[2,2,8,196,512]{4,3,2,1,0:T(8,128)(2,1)S(1)}, bf16[2,2,8,196,512]{4,3,2,1,0:T(8,128)(2,1)}, u32[]{:S(2)}) copy-start(bf16[2,2,8,196,512]{4,3,2,1,0:T(8,128)(2,1)} %get-tuple-element.35) | copy-start | bytes 19267588
  198.4 5.2 %copy-start.4 = (f32[80,256]{1,0:T(8,128)S(1)}, f32[80,256]{1,0:T(8,128)}, u32[]{:S(2)}) copy-start(f32[80,256]{1,0:T(8,128)} %get-tuple-element.36) | copy-start | bytes 245764
  198.4 7.2 %copy-start.6 = (s32[64,64]{0,1:T(8,128)S(1)}, s32[64,64]{0,1:T(8,128)}, u32[]{:S(2)}) copy-start(s32[64,64]{0,1:T(8,128)} %constant.26.clone) | copy-start | bytes 49156
  198.4 9.3 %copy-start.3 = (f32[64,384]{1,0:T(8,128)S(1)}, f32[64,384]{1,0:T(8,128)}, u32[]{:S(2)}) copy-start(f32[64,384]{1,0:T(8,128)} %get-tuple-element.37) | copy-start | bytes 294916
  198.4 9.9 %copy-start.5 = (f32[64,128]{1,0:T(8,128)S(1)}, f32[64,128]{1,0:T(8,128)}, u32[]{:S(2)}) copy-start(f32[64,128]{1,0:T(8,128)} %get-tuple-element.38) | copy-start | bytes 98308
  198.4 10.5 %copy-start.2 = (f32[64,512]{1,0:T(8,128)S(1)}, f32[64,512]{1,0:T(8,128)}, u32[]{:S(2)}) copy-start(f32[64,512]{1,0:T(8,128)} %get-tuple-element.107) | copy-start | bytes 393220
  198.4 11.2 %copy-start.1 = (f32[64,512]{1,0:T(8,128)S(1)}, f32[64,512]{1,0:T(8,128)}, u32[]{:S(2)}) copy-start(f32[64,512]{1,0:T(8,128)} %get-tuple-element.40) | copy-start | bytes 393220

commit v5 on v4

--- a/solution.py
+++ b/solution.py
@@ -119,58 +119,55 @@
     return (f + t, f[:-1] + t[:-1] + f[-1:] + t[-1:])
 
 
-LAG = 1
-
-
 class Gather:
-    def __init__(self, cube, full, chunks, send, recv):
-        self.cube, self.full, self.chunks, self.send, self.recv = cube, full, chunks, send, recv
-        self.orders = gather_orders(cube)
+    def __init__(self, cube, chunks, send, recv):
+        self.cube, self.chunks, self.send, self.recv = cube, chunks, send, recv
+        self.lanes = [sum(len(k) for k in chunks[:c]) for c in range(len(chunks))]
 
     def copies(self, c, s):
-        lo, hi = self.chunks[c]
-        rows = self.full.shape[self.cube.count]
-        half = rows // 2
-        for h, order in enumerate(self.orders):
-            ref = self.full.at[self.cube.at(order[:s]) + (pl.ds(h * half, half), pl.ds(lo, hi - lo))]
-            i = (c * self.cube.count + s) * 2 + h
-            yield pltpu.make_async_remote_copy(ref, ref, self.send.at[i], self.recv.at[i],
-                device_id=self.cube.partner(order[s]), device_id_type=MESH)
-
-    def start(self, c, s):
-        for copy in self.copies(c, s):
-            copy.start()
-
-    def wait(self, c, s):
-        for copy in self.copies(c, s):
-            copy.wait()
+        for h, (ref, part, order) in enumerate(self.chunks[c]):
+            ref = ref.at[self.cube.at(order[:s]) + part]
+            i = (self.lanes[c] + h) * self.cube.count + s
+            yield pltpu.make_async_remote_copy(
+                ref,
+                ref,
+                self.send.at[i],
+                self.recv.at[i],
+                device_id=self.cube.partner(order[s]),
+                device_id_type=MESH,
+            )
 
     def plan(self):
         n = self.cube.count
-        return sorted(((c, s) for c in range(len(self.chunks)) for s in range(n + 1)), key=lambda e: (LAG * e[0] + e[1], e[0]))
+        events = ((c, s) for c in range(len(self.chunks)) for s in range(n + 1))
+        return sorted(events, key=lambda e: (LAGS[e[0]] + e[1], e[0]))
 
     def advance(self, c, s):
         if s > 0:
-            self.wait(c, s - 1)
+            for copy in self.copies(c, s - 1):
+                copy.wait()
         if s < self.cube.count:
-            self.start(c, s)
+            for copy in self.copies(c, s):
+                copy.start()
+
+
+LAGS = (0, 1, 2)
 
 
 LANES = GROUP * HD
 SMALL = 16
-W_SMALL = 3 * LANES
-W_PROJ = 5 * LANES
-W_ONE = 6 * LANES
+PASSES = (3, 3, 5, 5, 7)
+W_ONE = LANES
 
 
 def digits_of(value, n):
     return tuple((value >> (n - 1 - k)) & 1 for k in range(n))
 
 
-def front_kernel(*refs, fsdp, tp, chunks):
+def front_kernel(*refs, fsdp, tp):
     vectors, refs = refs[:6], refs[6:]
     (bq_in, b1_in, tab_in, wq_in, wp_in, w1_in, w2_in, img_ref, rel_ref, mask_ref, perm_ref, permt_ref,
-     full_ref, qkv_ref, p_ref, mix_ref, vec_ref, b1_ref,
+     full_ref, wq_out, qkv_ref, p_ref, mix_ref, vec_ref, b1_ref,
      pack, wq, few, bq, tab, table, bias_scr, o_scr, local, send, recv) = refs
     step, steps = pl.program_id(0), pl.num_programs(0)
     cube = Cube(fsdp, tp)
@@ -179,42 +176,42 @@
     gw = LANES
     cut, ff_cut = w1_in.shape
     heads, span = tab_in.shape
-    gather = Gather(cube, full_ref, chunks, send, recv)
+    halves = [pl.ds(h * (cut // 2), cut // 2) for h in range(2)]
+    orders = gather_orders(cube)
+    split = lambda ref, cols: [(ref, (rows, cols), order) for rows, order in zip(halves, orders)]
+    chunks = [
+        split(wq, slice(None)) + [(few, (slice(None), slice(None)), orders[0])],
+        split(full_ref, pl.ds(0, W_ONE + ff_cut)),
+        split(full_ref, pl.ds(W_ONE + ff_cut, ff_cut)),
+    ]
+    gather = Gather(cube, chunks, send, recv)
     order = gather.plan()
     ready = order.index((0, n)) + 1
-    everything = (slice(None),) * n
+    keep = pltpu.make_async_copy(wq, wq_out, local.at[1])
 
     @pl.when(step == 0)
     def _():
-        pack[:, W_SMALL:W_PROJ] = jnp.zeros((cut, W_PROJ - W_SMALL), BF16)
-        for i, ref in enumerate(vectors):
-            pack[i : i + 1, W_SMALL : W_SMALL + cut] = ref[...]
-        for k in range(3):
-            pack[:, k * gw : (k + 1) * gw] = wq_in[k]
-            pack[6 + k : 7 + k, W_SMALL : W_SMALL + gw] = bq_in[k : k + 1]
-        for k in range(ff_cut // gw):
-            pack[9 + k : 10 + k, W_SMALL : W_SMALL + gw] = b1_in[0:1, k * gw : (k + 1) * gw]
-        pack[0:heads, W_SMALL + gw : W_PROJ] = tab_in[:, :gw]
-        pack[heads : 2 * heads, W_SMALL + gw : W_SMALL + span] = tab_in[:, gw:]
-        pack[:, W_PROJ:W_ONE] = wp_in[...]
+        pack[:, :W_ONE] = wp_in[...]
         pack[:, W_ONE : W_ONE + ff_cut] = w1_in[...]
         pack[:, W_ONE + ff_cut :] = w2_in[...]
         own = pltpu.make_async_copy(pack, full_ref.at[cube.at(())], local.at[0])
         own.start()
+        here = cube.at(())
+        few[here] = jnp.zeros((SMALL, 2 * gw), BF16)
+        for i, ref in enumerate(vectors):
+            few[here + (slice(i, i + 1), slice(0, cut))] = ref[...]
+        for k in range(3):
+            wq[here + (slice(None), slice(k * gw, (k + 1) * gw))] = wq_in[k]
+            few[here + (slice(6 + k, 7 + k), slice(0, gw))] = bq_in[k : k + 1]
+        for k in range(ff_cut // gw):
+            few[here + (slice(9 + k, 10 + k), slice(0, gw))] = b1_in[0:1, k * gw : (k + 1) * gw]
+        few[here + (slice(0, heads), slice(gw, 2 * gw))] = tab_in[:, :gw]
+        few[here + (slice(heads, 2 * heads), slice(gw, span))] = tab_in[:, gw:]
         greet(cube, range(n))
         own.wait()
         for c, s in order[:ready]:
             gather.advance(c, s)
-        loads = [
-            pltpu.make_async_copy(full_ref.at[everything + (slice(None), pl.ds(0, 3 * gw))], wq, local.at[0]),
-            pltpu.make_async_copy(
-                full_ref.at[everything + (pl.ds(0, SMALL), pl.ds(W_SMALL, W_PROJ - W_SMALL))], few, local.at[1]
-            ),
-        ]
-        for ld in loads:
-            ld.start()
-        for ld in loads:
-            ld.wait()
+        keep.start()
         vec_ref[...] = jnp.zeros_like(vec_ref)
         for f in range(fsdp):
             part = few[(0,) * n_t + digits_of(f, n_f)].astype(F32)
@@ -243,11 +240,15 @@
 
     rest = order[ready:]
     for i, (c, s) in enumerate(rest):
-        at = 1 + 2 * (i // 2)
+        at = PASSES[min(i, len(PASSES) - 1)]
 
         @pl.when(step == jnp.minimum(at, steps - 1))
         def _(c=c, s=s):
             gather.advance(c, s)
+
+    @pl.when(step == steps - 1)
+    def _():
+        keep.wait()
 
     x = img_ref[0].astype(F32)
     xhat, _ = standardize(x)
@@ -297,18 +298,18 @@
     heads = tp * table.shape[0]
     n_t, n_f = len(bits_of(tp)), len(bits_of(fsdp))
     n = n_t + n_f
-    chunks = ((0, W_PROJ), (W_PROJ, W_ONE + ff_cut), (W_ONE + ff_cut, cols))
-    n_sem = len(chunks) * n * 2
+    n_sem = 7 * n
     once = lambda a: pl.BlockSpec(a.shape, lambda i: (0,) * a.ndim, pipeline_mode=pl.Buffered(1))
     whole = lambda s: pl.BlockSpec(s, lambda i: (0,) * len(s))
     small = tuple(vectors) + (b_qkv, b_one, table, w_qkv, w_proj, w_one, w_two)
     return pl.pallas_call(
-        functools.partial(front_kernel, fsdp=fsdp, tp=tp, chunks=chunks),
+        functools.partial(front_kernel, fsdp=fsdp, tp=tp),
         grid=(n_img,),
         in_specs=[once(a) for a in small]
         + [pl.BlockSpec((1, t, c), lambda i: (i, 0, 0))]
         + [once(a) for a in (rel, mask, perm, permt)],
         out_specs=[
+            pl.BlockSpec(memory_space=pl.ANY),
             pl.BlockSpec(memory_space=pl.ANY),
             pl.BlockSpec((1, rows, 3 * tp * gw), lambda i: (i, 0, 0)),
             pl.BlockSpec((1, tp, n_win, ROWS, GROUP * ROWS), lambda i: (i, 0, 0, 0, 0)),
@@ -318,6 +319,7 @@
         ],
         out_shape=[
             jax.ShapeDtypeStruct((2,) * n + (cut, cols), BF16),
+            jax.ShapeDtypeStruct((2,) * n + (cut, 3 * gw), BF16),
             jax.ShapeDtypeStruct((n_img, rows, 3 * tp * gw), BF16),
             jax.ShapeDtypeStruct((n_img, tp, n_win, ROWS, GROUP * ROWS), BF16),
             jax.ShapeDtypeStruct((n_img, t, c), BF16),
@@ -327,7 +329,7 @@
         scratch_shapes=[
             pltpu.VMEM((cut, cols), BF16),
             pltpu.VMEM((2,) * n + (cut, 3 * gw), BF16),
-            pltpu.VMEM((2,) * n + (SMALL, W_PROJ - W_SMALL), BF16),
+            pltpu.VMEM((2,) * n + (SMALL, 2 * gw), BF16),
             pltpu.VMEM((1, 3 * tp * gw), F32),
             pltpu.VMEM((heads, 2 * gw), F32),
             pltpu.VMEM((heads, ROWS, ROWS), F32),
@@ -430,7 +432,7 @@
     return early, late, t[::-1] + f_in
 
 
-def layer_kernel(live_ref, img_hbm, cot_hbm, mix_ref, w_hbm, vec_ref, b1_ref, qkv_ref, p_ref, perm_ref, permt_ref,
+def layer_kernel(live_ref, img_hbm, cot_hbm, mix_ref, w_hbm, wq_hbm, vec_ref, b1_ref, qkv_ref, p_ref, perm_ref, permt_ref,
                  out_ref, gin_ref, dqkv_ref, dw1_ref, dw2_ref, dwp_ref, small_ref,
                  img_ref, cot_ref, w1_ref, w2_ref, wq_ref, wp, act, slope, normed_two, up_scr, gres_scr,
                  db1, dvec, dqkv_scr, dw, db, dtab, res_scr, acc, acc_p, late_a, late_b, small, *rest,
@@ -451,21 +453,18 @@
     bufs, rest = rest[: 5 * n], rest[5 * n :]
     load, local, send, recv, local_in, send_in, recv_in, rs_send, rs_recv = rest
 
-    columns_at = lambda lo, width: w_hbm.at[:, :, pl.ds(lo, width)]
     wide_q = n_q * gw
     loads = [
-        pltpu.make_async_copy(columns_at(lo, ref.shape[2]), ref, load.at[k])
-        for k, (lo, ref) in enumerate(
-            ((W_PROJ + gw, w1_ref), (W_PROJ + gw + wide_q, w2_ref), (0, wq_ref))
-        )
+        pltpu.make_async_copy(w_hbm.at[:, :, pl.ds(W_ONE, wide_q)], w1_ref, load.at[0]),
+        pltpu.make_async_copy(w_hbm.at[:, :, pl.ds(W_ONE + wide_q, wide_q)], w2_ref, load.at[1]),
+        pltpu.make_async_copy(img_hbm, img_ref, load.at[2]),
+        pltpu.make_async_copy(cot_hbm, cot_ref, load.at[3]),
     ]
-    loads += [pltpu.make_async_copy(img_hbm, img_ref, load.at[3]), pltpu.make_async_copy(cot_hbm, cot_ref, load.at[4])]
     loads += [
-        pltpu.make_async_copy(
-            w_hbm.at[g, :, pl.ds(W_PROJ, gw)], wp.at[:, pl.ds(g * gw, gw)], load.at[5 + g]
-        )
+        pltpu.make_async_copy(w_hbm.at[g, :, pl.ds(0, gw)], wp.at[:, pl.ds(g * gw, gw)], load.at[5 + g])
         for g in range(n_grp)
     ]
+    load_wq = pltpu.make_async_copy(wq_hbm, wq_ref, load.at[4])
     gmix_scr = cot_ref
 
     def result_of(q):
@@ -479,10 +478,10 @@
         dwp_ref[...] = total
 
     def result_a(total):
-        dqkv_ref[:, : 2 * gw] = total
+        dqkv_ref[: cut // 2] = total
 
     def result_b(total):
-        dqkv_ref[:, 2 * gw :] = total
+        dqkv_ref[cut // 2 :] = total
 
     def result_s(total):
         small_ref[...] = total
@@ -570,7 +569,7 @@
 
     @pl.when(step == 0)
     def _():
-        for ld in loads:
+        for ld in loads + [load_wq]:
             ld.start()
         greet(cube, range(n))
         dw[...] = jnp.zeros_like(dw)
@@ -635,14 +634,16 @@
             one, two = dot(normed_two[b], dh, TN), dot(up, act[b, q], TN)
             d_one, d_two = (one, two) if b == 0 else (d_one + one, d_two + two)
         for t in range(n_grp):
-            for f in range(fsdp):
-                at = (q,) + digits_of(t, n_t) + digits_of(f, n_f)
-                r, l = slice(f * cut, (f + 1) * cut), slice(t * gw, (t + 1) * gw)
-                acc[at + (slice(None), slice(0, gw))] = d_one[r, l].astype(BF16)
-                acc[at + (slice(None), slice(gw, 2 * gw))] = d_two[r, l].astype(BF16)
+            block = (2,) * n_f + (cut, gw)
+            at = (q,) + digits_of(t, n_t) + (slice(None),) * (n_f + 1)
+            l = slice(t * gw, (t + 1) * gw)
+            acc[at + (slice(0, gw),)] = d_one[:, l].astype(BF16).reshape(block)
+            acc[at + (slice(gw, 2 * gw),)] = d_two[:, l].astype(BF16).reshape(block)
 
     @pl.when(step == att_at - 1)
     def _():
+        point(2)
+
         def back(b, d_proj):
             dn = dot(slope[b, 0], columns(w1_ref, 0), NT)
             for k in range(1, n_q):
@@ -665,9 +666,13 @@
 
         d_proj = lax.fori_loop(0, fwd_steps, back, jnp.zeros((c, c), F32))
         for t in range(n_grp):
-            for f in range(fsdp):
-                at = digits_of(t, n_t) + digits_of(f, n_f)
-                acc_p[at] = d_proj[f * cut : (f + 1) * cut, t * gw : (t + 1) * gw].astype(BF16)
+            acc_p[digits_of(t, n_t)] = (
+                d_proj[:, t * gw : (t + 1) * gw].astype(BF16).reshape((2,) * n_f + (cut, gw))
+            )
+
+    @pl.when(step == att_at)
+    def _():
+        load_wq.wait()
 
     @pl.when(step >= att_at)
     def _():
@@ -721,14 +726,10 @@
 
     @pl.when(step == last_step)
     def _():
-        def fill(index):
-            t, f = index[:n_t], index[n_t:]
-            at = lambda part: functools.reduce(lambda a, b: 2 * a + b, part)
-            rows = pl.ds(pl.multiple_of(at(f) * cut, cut), cut)
-            late_a[index] = dw[at(t), rows, : 2 * gw].astype(BF16)
-            late_b[index] = dw[at(t), rows, 2 * gw :].astype(BF16)
-
-        blocks_of(n, fill)
+        for g in range(n_grp):
+            value = dw[g].astype(BF16).reshape((2,) * n_f + (cut, 3 * gw))
+            late_a[digits_of(g, n_t)] = value[..., : cut // 2, :]
+            late_b[digits_of(g, n_t)] = value[..., cut // 2 :, :]
         for red in reduces[n_early : n_early + 2]:
             red.start()
         wide = GROUP * ROWS
@@ -751,15 +752,13 @@
                     r = r + 1
         reduces[n_early + 2].start()
         send_in_(n_img - 1)
-        for work in ends:
-            work()
         for s in range(n):
             for red in reduces[n_early:]:
                 red.advance(s)
-            if s == 0:
-                for work in tail[: len(tail) // 2]:
+            if s == TAIL_AT:
+                for work in tail:
                     work()
-        for work in tail[len(tail) // 2 :]:
+        for work in ends:
             work()
         for i in range(fwd_steps):
             spread_out.copy(n_t - 1, i).wait()
@@ -768,15 +767,16 @@
 
 
 SLOTS = (
-    ((2, 0), (3, 1), (4, 0), (5, 2), (8, 0)),
-    ((3, 0), (4, 0), (6, 0), (8, 0), (10, 0)),
-    ((4, 0), (6, 2), (8, 2), (10, 2)),
-    ((5, 2), (8, 0), (9, 3), (11, 2)),
-    ((5, 2), (8, 0), (9, 3), (11, 2)),
+    ((3, 0), (4, 2), (6, 0), (8, 0), (10, 0)),
+    ((4, 0), (6, 0), (8, 0), (10, 0)),
+    ((5, 0), (7, 0), (9, 0), (11, 0)),
+    ((6, 0), (8, 2), (10, 2), (11, 3)),
+    ((6, 0), (8, 2), (10, 2), (11, 3)),
 )
-
-
-def layer(live, images, out_grad, mixed, w_all, vecs, b1, qkv, p, perm, permt, fsdp, tp, per=4):
+TAIL_AT = 2
+
+
+def layer(live, images, out_grad, mixed, w_all, w_qkv, vecs, b1, qkv, p, perm, permt, fsdp, tp, per=4):
     n_img, t, c = mixed.shape
     rows, cols = qkv.shape[1:]
     n_grp, n_win = p.shape[1:3]
@@ -791,9 +791,17 @@
     fwd_steps = n_img // per
     att_at = fwd_steps + n_q
     bufs = []
-    for lead, width in (((n_q,), 2 * gw), ((), gw), ((), 2 * gw), ((), gw)):
-        bufs += [pltpu.VMEM(lead + (2,) * (n - 1 - s) + (cut, width), BF16) for s in range(n)]
-    bufs += [pltpu.VMEM((2,) * max(n_t - 1 - s, 0) + (n_small, wide), F32) for s in range(n)]
+    for lead, block in (
+        ((n_q,), (cut, 2 * gw)),
+        ((), (cut, gw)),
+        ((), (cut // 2, 3 * gw)),
+        ((), (cut // 2, 3 * gw)),
+    ):
+        bufs += [pltpu.VMEM(lead + (2,) * (n - 1 - s) + block, BF16) for s in range(n)]
+    both = reduce_orders(n_t, n)[2]
+    for s in range(n):
+        left = sum(k < n_t for k in both[s + 1 :])
+        bufs.append(pltpu.VMEM((2,) * left + (n_small, wide), F32))
     whole = lambda s: pl.BlockSpec(s, lambda i: (0,) * len(s))
     once = lambda s: pl.BlockSpec(s, lambda i: (0,) * len(s), pipeline_mode=pl.Buffered(1))
     image = lambda i: jnp.clip(i - att_at, 0, n_img - 1)
@@ -807,6 +815,7 @@
             any_spec,
             any_spec,
             once(mixed.shape),
+            any_spec,
             any_spec,
             once(vecs.shape),
             once(b1.shape),
@@ -847,8 +856,8 @@
             pltpu.VMEM((n_img, t, c), BF16),
             pltpu.VMEM((n_q,) + digits + (cut, 2 * gw), BF16),
             pltpu.VMEM(digits + (cut, gw), BF16),
-            pltpu.VMEM(digits + (cut, 2 * gw), BF16),
-            pltpu.VMEM(digits + (cut, gw), BF16),
+            pltpu.VMEM(digits + (cut // 2, 3 * gw), BF16),
+            pltpu.VMEM(digits + (cut // 2, 3 * gw), BF16),
             pltpu.VMEM((2,) * n_t + (n_small, wide), F32),
             *bufs,
             pltpu.SemaphoreType.DMA((5 + n_grp,)),
@@ -865,7 +874,7 @@
             vmem_limit_bytes=60 << 20, collective_id=2, has_side_effects=True
         ),
         name="layer",
-    )(live, images, out_grad, mixed, w_all, vecs, b1, qkv, p, perm, permt)
+    )(live, images, out_grad, mixed, w_all, w_qkv, vecs, b1, qkv, p, perm, permt)
 
 
 def per_device(
@@ -904,7 +913,7 @@
     perm16 = jnp.asarray(perm).astype(BF16)
     consts = (jnp.asarray(index).reshape(1, -1), jnp.asarray(mask), perm16, perm16.T)
     vectors = (attn_norm_gain, attn_norm_bias, proj_bias, mlp_norm_gain, mlp_norm_bias, fc2_bias)
-    w_all, qkv, probs, mixed, vecs, b_one = front(
+    w_all, w_qkv, qkv, probs, mixed, vecs, b_one = front(
         [v.reshape(1, cut) for v in vectors],
         qkv_bias,
         fc1_bias.reshape(1, ff_cut),
@@ -919,8 +928,9 @@
         tp,
     )
     w_all = w_all.reshape(tp, width, w_all.shape[-1])
+    w_qkv = w_qkv.reshape(tp, width, 3 * gw)
     output, images_grad, d_qkv, d_one, d_two, d_proj, small = layer(
-        live, img, cot, mixed, w_all, vecs, b_one, qkv, probs, consts[2], consts[3], fsdp, tp
+        live, img, cot, mixed, w_all, w_qkv, vecs, b_one, qkv, probs, consts[2], consts[3], fsdp, tp
     )
     wide = GROUP * ROWS
     hot = (jnp.asarray(index)[None] == jnp.arange(span, dtype=jnp.int32)[:, None, None]).astype(F32)

time: 211 us -> 197 us (0.934)
  Pallas kernels: 182 us -> 168 us
    pallas_call x1, Pallas kernels: 64.6 us -> 52.6 us  [front(): pl.pallas_call(functools.partial(front_kernel, fsdp=fsdp, tp=tp), grid=(n...]
    unnamed x24 -> x26, local copies, waits for them, and re-layouts: 19.6 us -> 19.6 us
where the time goes in v5:
time: 197 us
  Pallas kernels  168 us (85%)
  local copies, waits for them, and re-layouts  24.5 us (12%)
  matrix products  2.01 us (1%)
    pallas_call x1, Pallas kernels, layer(): pl.pallas_call(functools.partial(layer_kernel, fsdp=fsdp, tp=tp, per=per,...  116 us
    pallas_call x1, Pallas kernels, front(): pl.pallas_call(functools.partial(front_kernel, fsdp=fsdp, tp=tp), grid=(n...  52.6 us
    unnamed x26, local copies, waits for them, and re-layouts  19.6 us

profile of v5, /device:TPU:0, one launch (start us, length us, event | category | flops | bytes accessed | tf_op | source)
XLA Modules:
  0.0 196.8 jit_solution(2375927203287369663)
XLA Ops:
  1.3 0.5 compare_convert_fusion.live_ref
  1.8 1.3 reshape.89.refs_7_
  3.1 2.1 %constant_dynamic-slice_fusion.1 = (bf16[8,196,512]{2,0,1:T(8,128)(2,1)S(1)}, bf16[8,196,512]{2,0,1:T(8,128)(2,1)S(1)}) fusion(bf16[32,196,512]{2,0,1:T(8,128)(2,1)} %param.34, s32[]{:T(128)S(6)} %select_n.7, bf16[32,196,512]{2,0,1:T(8,128)(2,1)} %param.19), kind=kLoop, calls=%fused_computation.8 | loop fusion | bytes 6422532 | tf_op jit(solution)/shard_map/dynamic_slice | solution.py:911
  5.2 1.7 copy.47.cot_hbm
  6.9 1.7 copy.46.refs_13_.img_hbm
  8.5 52.6 %front.1 = (bf16[2,2,2,2,2,64,1152]{6,5,4,3,2,1,0:T(8,128)(2,1)}, bf16[2,2,2,2,2,64,384]{6,5,4,3,2,1,0:T(8,128)(2,1)}, bf16[8,256,1536]{2,1,0:T(8,128)(2,1)}, bf...) custom-call(bf16[1,64]{1,0:T(2,128)(2,1)} %bitcast.56, ...), custom_call_target="tpu_custom_call" | custom-call | tf_op jit(solution)/shard_map/front/pallas_call | solution.py:305
  61.1 115.8 %layer.1 = (bf16[2,2,2,4,196,512]{5,4,3,2,1,0:T(8,128)(2,1)}, bf16[2,2,8,196,512]{4,3,2,1,0:T(8,128)(2,1)}, f32[64,384]{1,0:T(8,128)}, f32[64,512]{1,0:T(8,128)}...) custom-call(f32[8]{0:T(128)} %compare_convert_fusion.live_ref, ...), custom_call_target="tpu_custom_call" | custom-call | tf_op jit(solution)/shard_map/layer/pallas_call | solution.py:810
  176.9 0.0 slice-start
  176.9 0.0 slice-start.1
  176.9 8.0 %copy.43 = bf16[32,196,512]{2,0,1:T(8,128)(2,1)} copy(bf16[32,196,512]{2,1,0:T(8,128)(2,1)} %bitcast.45) | data formatting | bytes 12845056
  184.9 0.0 slice-done
  184.9 0.0 slice-done.1
  184.9 0.0 copy-start.5
  184.9 0.0 copy-start.2
  184.9 0.0 copy-start.4
  184.9 0.0 copy-start.1
  184.9 0.0 copy-start
  185.0 5.1 %copy.44 = bf16[32,196,512]{2,0,1:T(8,128)(2,1)} copy(bf16[32,196,512]{2,1,0:T(8,128)(2,1)S(1)} %bitcast.44) | data formatting | bytes 12845056
  190.1 0.0 copy-done.3
  190.1 0.6 copy.49
  190.7 0.6 slice.40
  191.3 0.1 constant_dynamic-slice_fusion
  191.4 0.5 slice_bitcast_fusion.1
  191.9 0.1 reshape.97
  192.0 0.1 copy.42
  192.2 0.0 copy-done.5
  192.2 2.0 %fusion.2 = f32[169,4]{0,1:T(4,128)} fusion(f32[64,4,64]{0,1,2:T(4,128)S(1)} %copy.42, s32[64,64]{0,1:T(8,128)S(1)} %copy-done.5), kind=kOutput, calls=%fused_computation.3 | convolution fusion | flops 33918976 | bytes 84624 | tf_op jit(solution)/shard_map/jhi,rji->rh/dot_general | solution.py:937
  194.2 0.6 copy_bitcast_fusion
  194.8 0.0 copy-done.4
  194.8 0.6 copy.55
  195.5 0.7 copy.56
  196.1 0.7 copy.57
  (9 shorter events, 0.0 us)
Async XLA Ops:
  176.9 8.0 %slice-start = ((s8[6553600]{0:T(1024)(128)(4,1)}), s8[4194304]{0:T(1024)(128)(4,1)S(1)}, s32[]{:S(2)}) async-start(s8[6553600]{0:T(1024)(128)(4,1)} %bitcast.42), calls=%async_computation | async-start | bytes 8388608
  176.9 8.0 %slice-start.1 = ((s8[6553600]{0:T(1024)(128)(4,1)}), s8[2359296]{0:T(1024)(128)(4,1)S(1)}, s32[]{:S(2)}) async-start(s8[6553600]{0:T(1024)(128)(4,1)} %bitcast.42), calls=%async_computation.1 | async-start | bytes 4718592
  184.9 5.2 %copy-start.3 = (f32[80,256]{1,0:T(8,128)S(1)}, f32[80,256]{1,0:T(8,128)}, u32[]{:S(2)}) copy-start(f32[80,256]{1,0:T(8,128)} %get-tuple-element.38) | copy-start | bytes 245764
  184.9 7.3 %copy-start.5 = (s32[64,64]{0,1:T(8,128)S(1)}, s32[64,64]{0,1:T(8,128)}, u32[]{:S(2)}) copy-start(s32[64,64]{0,1:T(8,128)} %constant.26.clone) | copy-start | bytes 49156
  184.9 9.3 %copy-start.2 = (f32[64,384]{1,0:T(8,128)S(1)}, f32[64,384]{1,0:T(8,128)}, u32[]{:S(2)}) copy-start(f32[64,384]{1,0:T(8,128)} %get-tuple-element.39) | copy-start | bytes 294916
  184.9 9.9 %copy-start.4 = (f32[64,128]{1,0:T(8,128)S(1)}, f32[64,128]{1,0:T(8,128)}, u32[]{:S(2)}) copy-start(f32[64,128]{1,0:T(8,128)} %get-tuple-element.40) | copy-start | bytes 98308
  184.9 10.5 %copy-start.1 = (f32[64,512]{1,0:T(8,128)S(1)}, f32[64,512]{1,0:T(8,128)}, u32[]{:S(2)}) copy-start(f32[64,512]{1,0:T(8,128)} %get-tuple-element.109) | copy-start | bytes 393220
  184.9 11.2 %copy-start = (f32[64,512]{1,0:T(8,128)S(1)}, f32[64,512]{1,0:T(8,128)}, u32[]{:S(2)}) copy-start(f32[64,512]{1,0:T(8,128)} %get-tuple-element.42) | copy-start | bytes 393220

commit v6 on v5

--- a/solution.py
+++ b/solution.py
@@ -366,18 +366,6 @@
         )
 
 
-def blocks_of(n, body):
-    if n == 0:
-        body(())
-        return
-
-    def one(i, carry):
-        body(tuple(lax.rem(lax.div(i, 2 ** (n - 1 - k)), 2) for k in range(n)))
-        return carry
-
-    lax.fori_loop(0, 2**n, one, 0)
-
-
 class Reduce:
     def __init__(self, cube, acc, order, bufs, send, recv, n_digits, out):
         self.cube, self.acc, self.order, self.bufs = cube, acc, order, bufs
@@ -408,18 +396,11 @@
 
     def advance(self, s):
         self.copy(s).wait()
-        free = self.left(s)
-        own = self.cube.own
-
-        def add(index):
-            at = dict(zip(free, index))
-            dst = tuple(at.get(k, own[k]) for k in range(self.n_digits))
-            if s + 1 == self.stages:
-                self.out(self.acc[dst].astype(F32) + self.bufs[s][index].astype(F32))
-            else:
-                self.acc[dst] = self.acc[dst] + self.bufs[s][index]
-
-        blocks_of(len(free), add)
+        region = self.at(self.left(s))
+        if s + 1 == self.stages:
+            self.out(self.acc[region].astype(F32) + self.bufs[s][...].astype(F32))
+        else:
+            self.acc[region] = self.acc[region] + self.bufs[s][...]
         if s + 1 < self.stages:
             self.copy(s + 1).start()
 
@@ -428,7 +409,7 @@
     t, f = list(range(n_t)), list(range(n_t, n))
     t_in, f_in = t[1:][::-1], f[::-1]
     early = (t_in + f_in + t[:1], t_in + f[:-1][::-1] + f[-1:] + t[:1])
-    late = (t_in + f[-1:] + t[:1] + f[:-1][::-1], t_in + t[:1] + f_in)
+    late = (t_in + f_in + t[:1], t_in + f[1:-1][::-1] + f[-1:] + t[:1] + f[:1])
     return early, late, t[::-1] + f_in
 
 
@@ -478,10 +459,12 @@
         dwp_ref[...] = total
 
     def result_a(total):
-        dqkv_ref[: cut // 2] = total
+        for k in range(3):
+            dqkv_ref[k, : cut // 2] = total[:, k * gw : (k + 1) * gw]
 
     def result_b(total):
-        dqkv_ref[cut // 2 :] = total
+        for k in range(3):
+            dqkv_ref[k, cut // 2 :] = total[:, k * gw : (k + 1) * gw]
 
     def result_s(total):
         small_ref[...] = total
@@ -569,7 +552,7 @@
 
     @pl.when(step == 0)
     def _():
-        for ld in loads + [load_wq]:
+        for ld in loads[2:] + loads[:2] + [load_wq]:
             ld.start()
         greet(cube, range(n))
         dw[...] = jnp.zeros_like(dw)
@@ -577,7 +560,7 @@
         db[...] = jnp.zeros_like(db)
         db1[...] = jnp.zeros_like(db1)
         dtab[...] = jnp.zeros_like(dtab)
-        for ld in loads:
+        for ld in loads[2:]:
             ld.wait()
 
     def columns(ref, q):
@@ -603,6 +586,11 @@
         dvec[5:6] += jnp.sum(up, axis=0, keepdims=True)
         mixed, res, xhat, _ = middle(step)
         normed_two[step] = (xhat * vec_ref[3:4] + vec_ref[4:5]).astype(BF16)
+
+        @pl.when(step == 0)
+        def _():
+            for ld in loads[:2]:
+                ld.wait()
 
         def hidden_part(q, branch):
             hid = dot(normed_two[step], columns(w1_ref, q)) + b1_ref[pl.ds(q, 1)]
@@ -825,11 +813,11 @@
             once(permt.shape),
         ],
         out_specs=[any_spec, any_spec]
-        + [whole(s) for s in ((cut, 3 * gw), (cut, ff_cut), (cut, ff_cut), (cut, gw), (n_small, wide))],
+        + [whole(s) for s in ((3, cut, gw), (cut, ff_cut), (cut, ff_cut), (cut, gw), (n_small, wide))],
         out_shape=[
             jax.ShapeDtypeStruct((2,) * n_t + (fwd_steps, per, t, c), BF16),
             jax.ShapeDtypeStruct((2,) * n_t + (n_img, t, c), BF16),
-            jax.ShapeDtypeStruct((cut, 3 * gw), F32),
+            jax.ShapeDtypeStruct((3, cut, gw), F32),
             jax.ShapeDtypeStruct((cut, ff_cut), F32),
             jax.ShapeDtypeStruct((cut, ff_cut), F32),
             jax.ShapeDtypeStruct((cut, gw), F32),
@@ -950,7 +938,7 @@
         images_grad.reshape(images.shape),
         dvec[0],
         dvec[1],
-        d_qkv.reshape(qkv_weight.shape),
+        d_qkv.transpose(1, 0, 2),
         dqkv_bias,
         d_tab,
         d_proj.T,

time: 197 us -> 191 us (0.970)
  Pallas kernels: 168 us -> 163 us
    pallas_call x1, Pallas kernels: 116 us -> 110 us  [layer(): pl.pallas_call(functools.partial(layer_kernel, fsdp=fsdp, tp=tp, per=per,...]
where the time goes in v6:
time: 191 us
  Pallas kernels  163 us (85%)
  local copies, waits for them, and re-layouts  24.5 us (13%)
  matrix products  2.01 us (1%)
    pallas_call x1, Pallas kernels, layer(): pl.pallas_call(functools.partial(layer_kernel, fsdp=fsdp, tp=tp, per=per,...  110 us
    pallas_call x1, Pallas kernels, front(): pl.pallas_call(functools.partial(front_kernel, fsdp=fsdp, tp=tp), grid=(n...  52.6 us
    unnamed x26, local copies, waits for them, and re-layouts  19.6 us

profile of v6, /device:TPU:0, one launch (start us, length us, event | category | flops | bytes accessed | tf_op | source)
XLA Modules:
  0.0 191.0 jit_solution(14759373190968639080)
XLA Ops:
  1.3 0.5 compare_convert_fusion.live_ref
  1.8 1.3 reshape.86.refs_7_
  3.1 2.1 %constant_dynamic-slice_fusion.1 = (bf16[8,196,512]{2,0,1:T(8,128)(2,1)S(1)}, bf16[8,196,512]{2,0,1:T(8,128)(2,1)S(1)}) fusion(bf16[32,196,512]{2,0,1:T(8,128)(2,1)} %param.34, s32[]{:T(128)S(6)} %select_n.7, bf16[32,196,512]{2,0,1:T(8,128)(2,1)} %param.19), kind=kLoop, calls=%fused_computation.7 | loop fusion | bytes 6422532 | tf_op jit(solution)/shard_map/dynamic_slice | solution.py:899
  5.2 1.7 copy.40.cot_hbm
  6.9 1.7 copy.39.refs_13_.img_hbm
  8.5 52.6 %front.1 = (bf16[2,2,2,2,2,64,1152]{6,5,4,3,2,1,0:T(8,128)(2,1)}, bf16[2,2,2,2,2,64,384]{6,5,4,3,2,1,0:T(8,128)(2,1)}, bf16[8,256,1536]{2,1,0:T(8,128)(2,1)}, bf...) custom-call(bf16[1,64]{1,0:T(2,128)(2,1)} %bitcast.53, ...), custom_call_target="tpu_custom_call" | custom-call | tf_op jit(solution)/shard_map/front/pallas_call | solution.py:305
  61.1 110.1 %layer.1 = (bf16[2,2,2,4,196,512]{5,4,3,2,1,0:T(8,128)(2,1)}, bf16[2,2,8,196,512]{4,3,2,1,0:T(8,128)(2,1)}, f32[3,64,128]{2,1,0:T(8,128)}, f32[64,512]{1,0:T(8,1...) custom-call(f32[8]{0:T(128)} %compare_convert_fusion.live_ref, ...), custom_call_target="tpu_custom_call" | custom-call | tf_op jit(solution)/shard_map/layer/pallas_call | solution.py:798
  171.2 0.0 slice-start
  171.2 0.0 slice-start.1
  171.2 8.0 %copy.37 = bf16[32,196,512]{2,0,1:T(8,128)(2,1)} copy(bf16[32,196,512]{2,1,0:T(8,128)(2,1)} %bitcast.41) | data formatting | bytes 12845056
  179.2 0.0 slice-done
  179.2 0.0 slice-done.1
  179.2 0.0 copy-start.5
  179.2 0.0 copy-start.2
  179.2 0.0 copy-start.4
  179.2 0.0 copy-start.1
  179.2 0.0 copy-start
  179.2 5.1 %copy.38 = bf16[32,196,512]{2,0,1:T(8,128)(2,1)} copy(bf16[32,196,512]{2,1,0:T(8,128)(2,1)S(1)} %bitcast.40) | data formatting | bytes 12845056
  184.4 0.0 copy-done.3
  184.4 0.6 copy.41
  184.9 0.6 slice.40
  185.6 0.1 constant_dynamic-slice_fusion
  185.6 0.5 slice_bitcast_fusion.1
  186.2 0.1 reshape.93
  186.3 0.1 copy.36
  186.4 0.0 copy-done.5
  186.4 2.0 %fusion.2 = f32[169,4]{0,1:T(4,128)} fusion(f32[64,4,64]{0,1,2:T(4,128)S(1)} %copy.36, s32[64,64]{0,1:T(8,128)S(1)} %copy-done.5), kind=kOutput, calls=%fused_computation.3 | convolution fusion | flops 33918976 | bytes 84624 | tf_op jit(solution)/shard_map/jhi,rji->rh/dot_general | solution.py:925
  188.4 0.0 copy-done.2
  188.4 0.6 copy.47
  189.1 0.6 copy.48
  189.7 0.7 copy.49
  190.4 0.7 copy.50
  (9 shorter events, 0.0 us)
Async XLA Ops:
  171.2 8.0 %slice-start = ((s8[6553600]{0:T(1024)(128)(4,1)}), s8[4194304]{0:T(1024)(128)(4,1)S(1)}, s32[]{:S(2)}) async-start(s8[6553600]{0:T(1024)(128)(4,1)} %bitcast.38), calls=%async_computation | async-start | bytes 8388608
  171.2 8.0 %slice-start.1 = ((s8[6553600]{0:T(1024)(128)(4,1)}), s8[2359296]{0:T(1024)(128)(4,1)S(1)}, s32[]{:S(2)}) async-start(s8[6553600]{0:T(1024)(128)(4,1)} %bitcast.38), calls=%async_computation.1 | async-start | bytes 4718592
  179.2 5.2 %copy-start.3 = (f32[80,256]{1,0:T(8,128)S(1)}, f32[80,256]{1,0:T(8,128)}, u32[]{:S(2)}) copy-start(f32[80,256]{1,0:T(8,128)} %get-tuple-element.38) | copy-start | bytes 245764
  179.2 7.3 %copy-start.5 = (s32[64,64]{0,1:T(8,128)S(1)}, s32[64,64]{0,1:T(8,128)}, u32[]{:S(2)}) copy-start(s32[64,64]{0,1:T(8,128)} %constant.26.clone) | copy-start | bytes 49156
  179.2 9.3 %copy-start.2 = (f32[3,64,128]{2,1,0:T(8,128)S(1)}, f32[3,64,128]{2,1,0:T(8,128)}, u32[]{:S(2)}) copy-start(f32[3,64,128]{2,1,0:T(8,128)} %get-tuple-element.39) | copy-start | bytes 294916
  179.2 9.9 %copy-start.4 = (f32[64,128]{1,0:T(8,128)S(1)}, f32[64,128]{1,0:T(8,128)}, u32[]{:S(2)}) copy-start(f32[64,128]{1,0:T(8,128)} %get-tuple-element.40) | copy-start | bytes 98308
  179.2 10.5 %copy-start.1 = (f32[64,512]{1,0:T(8,128)S(1)}, f32[64,512]{1,0:T(8,128)}, u32[]{:S(2)}) copy-start(f32[64,512]{1,0:T(8,128)} %get-tuple-element.94) | copy-start | bytes 393220
  179.2 11.2 %copy-start = (f32[64,512]{1,0:T(8,128)S(1)}, f32[64,512]{1,0:T(8,128)}, u32[]{:S(2)}) copy-start(f32[64,512]{1,0:T(8,128)} %get-tuple-element.42) | copy-start | bytes 393220

commit v7 on v6

--- a/solution.py
+++ b/solution.py
@@ -741,7 +741,7 @@
         reduces[n_early + 2].start()
         send_in_(n_img - 1)
         for s in range(n):
-            for red in reduces[n_early:]:
+            for red in reduces[n_early:][::-1]:
                 red.advance(s)
             if s == TAIL_AT:
                 for work in tail:

time: 191 us -> 191 us (level)
  no operation moved by 1% of the time
where the time goes in v7:
time: 191 us
  Pallas kernels  162 us (85%)
  local copies, waits for them, and re-layouts  24.5 us (13%)
  matrix products  2.01 us (1%)
    pallas_call x1, Pallas kernels, layer(): pl.pallas_call(functools.partial(layer_kernel, fsdp=fsdp, tp=tp, per=per,...  110 us
    pallas_call x1, Pallas kernels, front(): pl.pallas_call(functools.partial(front_kernel, fsdp=fsdp, tp=tp), grid=(n...  52.6 us
    unnamed x26, local copies, waits for them, and re-layouts  19.6 us

profile of v7, /device:TPU:0, one launch (start us, length us, event | category | flops | bytes accessed | tf_op | source)
XLA Modules:
  0.0 190.7 jit_solution(5275234442671144797)
XLA Ops:
  1.3 0.5 compare_convert_fusion.live_ref
  1.8 1.3 reshape.86.refs_7_
  3.1 2.1 %constant_dynamic-slice_fusion.1 = (bf16[8,196,512]{2,0,1:T(8,128)(2,1)S(1)}, bf16[8,196,512]{2,0,1:T(8,128)(2,1)S(1)}) fusion(bf16[32,196,512]{2,0,1:T(8,128)(2,1)} %param.34, s32[]{:T(128)S(6)} %select_n.7, bf16[32,196,512]{2,0,1:T(8,128)(2,1)} %param.19), kind=kLoop, calls=%fused_computation.7 | loop fusion | bytes 6422532 | tf_op jit(solution)/shard_map/dynamic_slice | solution.py:899
  5.2 1.7 copy.40.cot_hbm
  6.9 1.7 copy.39.refs_13_.img_hbm
  8.5 52.6 %front.1 = (bf16[2,2,2,2,2,64,1152]{6,5,4,3,2,1,0:T(8,128)(2,1)}, bf16[2,2,2,2,2,64,384]{6,5,4,3,2,1,0:T(8,128)(2,1)}, bf16[8,256,1536]{2,1,0:T(8,128)(2,1)}, bf...) custom-call(bf16[1,64]{1,0:T(2,128)(2,1)} %bitcast.53, ...), custom_call_target="tpu_custom_call" | custom-call | tf_op jit(solution)/shard_map/front/pallas_call | solution.py:305
  61.1 109.8 %layer.1 = (bf16[2,2,2,4,196,512]{5,4,3,2,1,0:T(8,128)(2,1)}, bf16[2,2,8,196,512]{4,3,2,1,0:T(8,128)(2,1)}, f32[3,64,128]{2,1,0:T(8,128)}, f32[64,512]{1,0:T(8,1...) custom-call(f32[8]{0:T(128)} %compare_convert_fusion.live_ref, ...), custom_call_target="tpu_custom_call" | custom-call | tf_op jit(solution)/shard_map/layer/pallas_call | solution.py:798
  170.9 0.0 slice-start
  170.9 0.0 slice-start.1
  170.9 8.0 %copy.37 = bf16[32,196,512]{2,0,1:T(8,128)(2,1)} copy(bf16[32,196,512]{2,1,0:T(8,128)(2,1)} %bitcast.41) | data formatting | bytes 12845056
  178.9 0.0 slice-done
  178.9 0.0 slice-done.1
  178.9 0.0 copy-start.5
  178.9 0.0 copy-start.2
  178.9 0.0 copy-start.4
  178.9 0.0 copy-start.1
  178.9 0.0 copy-start
  178.9 5.1 %copy.38 = bf16[32,196,512]{2,0,1:T(8,128)(2,1)} copy(bf16[32,196,512]{2,1,0:T(8,128)(2,1)S(1)} %bitcast.40) | data formatting | bytes 12845056
  184.1 0.6 copy.41
  184.6 0.6 slice.40
  185.3 0.1 constant_dynamic-slice_fusion
  185.3 0.5 slice_bitcast_fusion.1
  185.9 0.1 reshape.93
  186.0 0.1 copy.36
  186.1 2.0 %fusion.2 = f32[169,4]{0,1:T(4,128)} fusion(f32[64,4,64]{0,1,2:T(4,128)S(1)} %copy.36, s32[64,64]{0,1:T(8,128)S(1)} %copy-done.5), kind=kOutput, calls=%fused_computation.3 | convolution fusion | flops 33918976 | bytes 84624 | tf_op jit(solution)/shard_map/jhi,rji->rh/dot_general | solution.py:925
  188.1 0.0 copy-done.2
  188.1 0.6 copy.47
  188.8 0.0 copy-done.4
  188.8 0.6 copy.48
  189.4 0.7 copy.49
  190.1 0.0 copy-done
  190.1 0.7 copy.50
  (9 shorter events, 0.0 us)
Async XLA Ops:
  170.9 8.0 %slice-start = ((s8[6553600]{0:T(1024)(128)(4,1)}), s8[4194304]{0:T(1024)(128)(4,1)S(1)}, s32[]{:S(2)}) async-start(s8[6553600]{0:T(1024)(128)(4,1)} %bitcast.38), calls=%async_computation | async-start | bytes 8388608
  170.9 8.0 %slice-start.1 = ((s8[6553600]{0:T(1024)(128)(4,1)}), s8[2359296]{0:T(1024)(128)(4,1)S(1)}, s32[]{:S(2)}) async-start(s8[6553600]{0:T(1024)(128)(4,1)} %bitcast.38), calls=%async_computation.1 | async-start | bytes 4718592
  178.9 5.2 %copy-start.3 = (f32[80,256]{1,0:T(8,128)S(1)}, f32[80,256]{1,0:T(8,128)}, u32[]{:S(2)}) copy-start(f32[80,256]{1,0:T(8,128)} %get-tuple-element.38) | copy-start | bytes 245764
  178.9 7.3 %copy-start.5 = (s32[64,64]{0,1:T(8,128)S(1)}, s32[64,64]{0,1:T(8,128)}, u32[]{:S(2)}) copy-start(s32[64,64]{0,1:T(8,128)} %constant.26.clone) | copy-start | bytes 49156
  178.9 9.3 %copy-start.2 = (f32[3,64,128]{2,1,0:T(8,128)S(1)}, f32[3,64,128]{2,1,0:T(8,128)}, u32[]{:S(2)}) copy-start(f32[3,64,128]{2,1,0:T(8,128)} %get-tuple-element.39) | copy-start | bytes 294916
  178.9 9.9 %copy-start.4 = (f32[64,128]{1,0:T(8,128)S(1)}, f32[64,128]{1,0:T(8,128)}, u32[]{:S(2)}) copy-start(f32[64,128]{1,0:T(8,128)} %get-tuple-element.40) | copy-start | bytes 98308
  178.9 10.5 %copy-start.1 = (f32[64,512]{1,0:T(8,128)S(1)}, f32[64,512]{1,0:T(8,128)}, u32[]{:S(2)}) copy-start(f32[64,512]{1,0:T(8,128)} %get-tuple-element.94) | copy-start | bytes 393220
  178.9 11.2 %copy-start = (f32[64,512]{1,0:T(8,128)S(1)}, f32[64,512]{1,0:T(8,128)}, u32[]{:S(2)}) copy-start(f32[64,512]{1,0:T(8,128)} %get-tuple-element.42) | copy-start | bytes 393220
